TPU v7x, 32 devices: a whole 2x2x4 slice. The times are simulated.
32 devices in a mesh: dp: 8 (over z, x), fsdp: 4 (over y, core).
Axes of the slice: x: 2, y: 2, z: 4, core: 2. Of those that a mesh axis runs over, the one named last changes fastest.
Arguments:
- patches: bfloat16 [25344, 768], P(('dp', 'fsdp')), may hold values from -6 to 6
- send_counts: int32 [32, 8], P(('dp', 'fsdp')), may hold values from 50 to 99, as said below
- dec_segment: int32 [64, 529], P(('dp', 'fsdp')), may hold values from 0 to 4, as said below
- source_index: int32 [64, 529], P(('dp', 'fsdp')), may hold values from -1 to 791, as said below
- cotangent: float32 [64, 529, 512], P(('dp', 'fsdp')), may hold values from -6 to 6
- enc_norms: float32 [4, 768], P('fsdp', 'dp'), may hold values from -0.9 to 1.6, as said below
- enc_qkv: float32 [768, 2304], P('fsdp', 'dp'), may hold values from -0.21875 to 0.21875
- enc_out: float32 [768, 768], P('fsdp', 'dp'), may hold values from -0.4375 to 0.4375
- enc_up: float32 [768, 3072], P('fsdp', 'dp'), may hold values from -0.21875 to 0.21875
- enc_down: float32 [3072, 768], P('fsdp', 'dp'), may hold values from -0.109375 to 0.109375
- dec_norms: float32 [8, 512], P('fsdp', 'dp'), may hold values from -1.7 to 1.7, as said below
- dec_embed: float32 [768, 512], P('fsdp', 'dp'), may hold values from -0.21875 to 0.21875
- dec_qkv: float32 [512, 1536], P('fsdp', 'dp'), may hold values from -0.25 to 0.25
- dec_out: float32 [512, 512], P('fsdp', 'dp'), may hold values from -0.5 to 0.5
- dec_up: float32 [512, 2048], P('fsdp', 'dp'), may hold values from -0.25 to 0.25
- dec_down: float32 [2048, 512], P('fsdp', 'dp'), may hold values from -0.125 to 0.125
Outputs:
- decoded: float32 [64, 529, 512], P(('dp', 'fsdp'))
- patch_grad: float32 [25344, 768], P(('dp', 'fsdp'))
- grad_enc_norms: float32 [4, 768], P('fsdp', 'dp')
- grad_enc_qkv: float32 [768, 2304], P('fsdp', 'dp')
- grad_enc_out: float32 [768, 768], P('fsdp', 'dp')
- grad_enc_up: float32 [768, 3072], P('fsdp', 'dp')
- grad_enc_down: float32 [3072, 768], P('fsdp', 'dp')
- grad_dec_norms: float32 [8, 512], P('fsdp', 'dp')
- grad_dec_embed: float32 [768, 512], P('fsdp', 'dp')
- grad_dec_qkv: float32 [512, 1536], P('fsdp', 'dp')
- grad_dec_out: float32 [512, 512], P('fsdp', 'dp')
- grad_dec_up: float32 [512, 2048], P('fsdp', 'dp')
- grad_dec_down: float32 [2048, 512], P('fsdp', 'dp')
Inputs may be any that keep to these rules, and one draw needn't show every extreme that they name: `send_counts`: entry d of device (e, f) is the number of visible patches of the one document that its slot d sends to device (d, f); they fill the slot's last rows; every entry belongs to one whole document. `dec_segment`: A strip holds 4 documents numbered in order, each whole within the strip, of 66 to 132 patches; the number 4 marks the strip's trailing padding, present in every strip. `source_index`: A visible patch names row c of the buffer that its device receives: c // 99 is the sending device along dp, c % 99 the row in that device's slot. A document of n patches has one masked span of n // 4 patches; its visible patches keep their order and come from one sender; each device receives exactly one document from every device of its dp group. Masked and padding patches have -1. `enc_norms`: even rows are gains, odd rows shifts. `dec_norms`: rows 0, 2, 4 are gains, rows 1, 3, 5, 7 shifts, row 6 the mask token.
All inputs are finite; a program needn't handle non-finite values.
Results may differ from a plain program's by a relative error of at most 0.02.
Values may be sent and summed in bfloat16 or wider, within the bound.
A program may use at most 448 MiB of HBM per device.

v0:
```python
import jax
import jax.numpy as jnp
from jax import lax
from jax.sharding import PartitionSpec as P

HEADS_E = 12
HEADS_D = 16


EPSILON = 1e-06
NEGATIVE = -1000000000.0


def in_blocks(value, dim, length):
    dims = value.shape
    pieces = value.reshape(*dims[:dim], length, dims[dim] // length, *dims[dim + 1 :])
    return jnp.moveaxis(pieces, dim, 0)


def sum_at_owner(value, axis, dim):
    length = lax.axis_size(axis)
    pieces = lax.all_to_all(in_blocks(value, dim, length), axis, 0, 0, tiled=True)
    return jnp.sum(pieces.astype(jnp.float32), axis=0)


def in_one_piece(arrays, axis, dim, along):
    widths = [a.shape[along] for a in arrays]
    both = jnp.concatenate(arrays, axis=along)
    whole = sum_at_owner(both, axis, dim)
    return tuple(jnp.split(whole, [sum(widths[:k]) for k in range(1, len(widths))], axis=along))


def layer_norm(values, scale_gain, norm_shift):
    row_mean = jnp.mean(values, axis=-1, keepdims=True)
    centred = values - row_mean
    spread = jnp.mean(centred * centred, axis=-1, keepdims=True)
    return centred * lax.rsqrt(spread + EPSILON) * scale_gain + norm_shift


def gelu_exact(values):
    return jax.nn.gelu(values, approximate=False)


def project(left_side, right_side):
    return jnp.einsum("grw,wc->grc", left_side, right_side, preferred_element_type=jnp.float32)


def project_back(gradient, right_side):
    return jnp.einsum("grc,wc->grw", gradient, right_side, preferred_element_type=jnp.float32)


def outer_sum(left_side, gradient):
    return jnp.einsum("grw,grc->wc", left_side, gradient, preferred_element_type=jnp.float32)


def split_heads(joined_qkv, head_count):
    groups, row_count, triple = joined_qkv.shape
    head_size = triple // 3 // head_count
    pieces = joined_qkv.reshape(groups, row_count, 3, head_count, head_size)
    return (pieces[:, :, 0], pieces[:, :, 1], pieces[:, :, 2], head_size)


def scores_of(queries, key_part, allowed, head_size):
    raw_scores = jnp.einsum(
        "grhd,gshd->ghrs", queries, key_part, preferred_element_type=jnp.float32
    ) * head_size ** (-0.5)
    return jnp.where(allowed[:, None], raw_scores, NEGATIVE)


def attend(joined_qkv, allowed, head_count):
    queries, key_part, values, head_size = split_heads(joined_qkv, head_count)
    scores = scores_of(queries, key_part, allowed, head_size)
    row_max = jnp.max(scores, axis=-1, keepdims=True)
    weights = jnp.exp(scores - row_max)
    row_total = jnp.sum(weights, axis=-1, keepdims=True)
    probability = weights / row_total
    log_total = row_max + jnp.log(row_total)
    mixture = jnp.einsum(
        "ghrs,gshd->grhd",
        probability.astype(jnp.bfloat16),
        values,
        preferred_element_type=jnp.float32,
    )
    return (mixture.reshape(joined_qkv.shape[0], joined_qkv.shape[1], -1), log_total)


def attend_back(joined_qkv, allowed, head_count, log_total, d_mixed):
    queries, key_part, values, head_size = split_heads(joined_qkv, head_count)
    scores = scores_of(queries, key_part, allowed, head_size)
    probability = jnp.exp(scores - log_total)
    groups, row_count = (d_mixed.shape[0], d_mixed.shape[1])
    d_heads = d_mixed.reshape(groups, row_count, head_count, head_size)
    d_probs = jnp.einsum("grhd,gshd->ghrs", d_heads, values, preferred_element_type=jnp.float32)
    d_value = jnp.einsum(
        "ghrs,grhd->gshd",
        probability.astype(jnp.bfloat16),
        d_heads,
        preferred_element_type=jnp.float32,
    )
    centre = jnp.sum(d_probs * probability, axis=-1, keepdims=True)
    d_scores = (probability * (d_probs - centre)).astype(jnp.bfloat16)
    score_scale = head_size ** (-0.5)
    d_query = (
        jnp.einsum("ghrs,gshd->grhd", d_scores, key_part, preferred_element_type=jnp.float32)
        * score_scale
    )
    d_key = (
        jnp.einsum("ghrs,grhd->gshd", d_scores, queries, preferred_element_type=jnp.float32)
        * score_scale
    )
    stacked = jnp.stack([d_query, d_key, d_value], axis=2)
    return stacked.reshape(groups, row_count, -1).astype(jnp.bfloat16)


def block_forward(inputs, params, allowed, head_count):
    norm_rows, w_qkv, w_out, w_up, w_down = params
    gain_rows = norm_rows.astype(jnp.float32)
    h_one = layer_norm(inputs, gain_rows[0], gain_rows[1]).astype(jnp.bfloat16)
    joined_qkv = project(h_one, w_qkv).astype(jnp.bfloat16)
    mixture, log_total = attend(joined_qkv, allowed, head_count)
    mixture = mixture.astype(jnp.bfloat16)
    x_one = inputs + project(mixture, w_out)
    h_two = layer_norm(x_one, gain_rows[2], gain_rows[3]).astype(jnp.bfloat16)
    up_proj = project(h_two, w_up)
    activated = gelu_exact(up_proj).astype(jnp.bfloat16)
    x_two = x_one + project(activated, w_down)
    return (x_two, (joined_qkv, log_total, mixture, x_one, up_proj))


def block_backward(inputs, params, allowed, head_count, stored, d_two):
    norm_rows, w_qkv, w_out, w_up, w_down = params
    gain_rows = norm_rows.astype(jnp.float32)
    joined_qkv, log_total, mixture, x_one, up_proj = stored
    d_branch = d_two.astype(jnp.bfloat16)
    activated, gelu_pull = jax.vjp(gelu_exact, up_proj)
    g_down = outer_sum(activated.astype(jnp.bfloat16), d_branch)
    d_up = gelu_pull(project_back(d_branch, w_down))[0].astype(jnp.bfloat16)
    h_two, norm_two_pull = jax.vjp(layer_norm, x_one, gain_rows[2], gain_rows[3])
    g_up = outer_sum(h_two.astype(jnp.bfloat16), d_up)
    d_x_two_norm, d_gain_two, d_shift_two = norm_two_pull(project_back(d_up, w_up))
    d_one = d_two + d_x_two_norm
    d_attn = d_one.astype(jnp.bfloat16)
    g_out = outer_sum(mixture, d_attn)
    d_mixed = project_back(d_attn, w_out).astype(jnp.bfloat16)
    d_qkv = attend_back(joined_qkv, allowed, head_count, log_total, d_mixed)
    h_one, norm_one_pull = jax.vjp(layer_norm, inputs, gain_rows[0], gain_rows[1])
    g_qkv = outer_sum(h_one.astype(jnp.bfloat16), d_qkv)
    d_x_one_norm, d_gain_one, d_shift_one = norm_one_pull(project_back(d_qkv, w_qkv))
    g_norms = jnp.stack([d_gain_one, d_shift_one, d_gain_two, d_shift_two])
    return (d_one + d_x_one_norm, (g_norms, g_qkv, g_out, g_up, g_down))


def per_device(
    patches,
    send_counts,
    dec_segment,
    source_index,
    cotangent,
    enc_norms,
    enc_qkv,
    enc_out,
    enc_up,
    enc_down,
    dec_norms,
    dec_embed,
    dec_qkv,
    dec_out,
    dec_up,
    dec_down,
):
    peer_count = lax.axis_size("dp")
    width_enc = patches.shape[1]
    slot_rows = patches.shape[0] // peer_count
    enc_wide = (
        lax.all_gather(enc_norms.astype(jnp.bfloat16), "dp", axis=1, tiled=True),
        lax.all_gather(enc_qkv.astype(jnp.bfloat16), "dp", axis=1, tiled=True),
        lax.all_gather(enc_out.astype(jnp.bfloat16), "dp", axis=1, tiled=True),
        lax.all_gather(enc_up.astype(jnp.bfloat16), "dp", axis=1, tiled=True),
        lax.all_gather(enc_down.astype(jnp.bfloat16), "dp", axis=1, tiled=True),
    )
    enc_full = (
        lax.all_gather(enc_wide[0], "fsdp", axis=0, tiled=True),
        lax.all_gather(enc_wide[1], "fsdp", axis=0, tiled=True),
        lax.all_gather(enc_wide[2], "fsdp", axis=0, tiled=True),
        lax.all_gather(enc_wide[3], "fsdp", axis=0, tiled=True),
        lax.all_gather(enc_wide[4], "fsdp", axis=0, tiled=True),
    )
    dec_wide = (
        lax.all_gather(dec_norms.astype(jnp.bfloat16), "dp", axis=1, tiled=True),
        lax.all_gather(dec_embed.astype(jnp.bfloat16), "dp", axis=1, tiled=True),
        lax.all_gather(dec_qkv.astype(jnp.bfloat16), "dp", axis=1, tiled=True),
        lax.all_gather(dec_out.astype(jnp.bfloat16), "dp", axis=1, tiled=True),
        lax.all_gather(dec_up.astype(jnp.bfloat16), "dp", axis=1, tiled=True),
        lax.all_gather(dec_down.astype(jnp.bfloat16), "dp", axis=1, tiled=True),
    )
    dec_full = (
        lax.all_gather(dec_wide[0], "fsdp", axis=0, tiled=True),
        lax.all_gather(dec_wide[1], "fsdp", axis=0, tiled=True),
        lax.all_gather(dec_wide[2], "fsdp", axis=0, tiled=True),
        lax.all_gather(dec_wide[3], "fsdp", axis=0, tiled=True),
        lax.all_gather(dec_wide[4], "fsdp", axis=0, tiled=True),
        lax.all_gather(dec_wide[5], "fsdp", axis=0, tiled=True),
    )
    enc_rows = patches.astype(jnp.float32).reshape(peer_count, slot_rows, width_enc)
    live_counts = send_counts.reshape(peer_count)
    live_rows = (
        jnp.arange(slot_rows, dtype=jnp.int32)[None, :] >= (slot_rows - live_counts)[:, None]
    )
    enc_allowed = jnp.broadcast_to(live_rows[:, None, :], (peer_count, slot_rows, slot_rows))
    enc_params = (enc_full[0], enc_full[1], enc_full[2], enc_full[3], enc_full[4])
    enc_result, enc_stored = block_forward(enc_rows, enc_params, enc_allowed, HEADS_E)
    enc_send = enc_result.astype(jnp.bfloat16)
    dec_gains = dec_full[0].astype(jnp.float32)
    w_embed = dec_full[1]
    arrived = lax.all_to_all(enc_send, "dp", split_axis=0, concat_axis=0, tiled=True)
    embedded = (project(arrived, w_embed) + dec_gains[7]).astype(jnp.bfloat16)
    slot_count = peer_count * slot_rows
    slot_table = embedded.reshape(slot_count, -1)
    visible = source_index >= 0
    picked = jnp.take(slot_table, jnp.where(visible, source_index, 0), axis=0)
    dec_start = jnp.where(visible[..., None], picked.astype(jnp.float32), dec_gains[6])
    dec_allowed = dec_segment[:, :, None] == dec_segment[:, None, :]
    dec_params = (dec_full[0], dec_full[2], dec_full[3], dec_full[4], dec_full[5])
    dec_two, dec_stored = block_forward(dec_start, dec_params, dec_allowed, HEADS_D)
    decoded, final_pull = jax.vjp(layer_norm, dec_two, dec_gains[4], dec_gains[5])
    enc_wide_back = (
        lax.all_gather(enc_norms.astype(jnp.bfloat16), "dp", axis=1, tiled=True),
        lax.all_gather(enc_qkv.astype(jnp.bfloat16), "dp", axis=1, tiled=True),
        lax.all_gather(enc_out.astype(jnp.bfloat16), "dp", axis=1, tiled=True),
        lax.all_gather(enc_up.astype(jnp.bfloat16), "dp", axis=1, tiled=True),
        lax.all_gather(enc_down.astype(jnp.bfloat16), "dp", axis=1, tiled=True),
    )
    enc_back = (
        lax.all_gather(enc_wide_back[0], "fsdp", axis=0, tiled=True),
        lax.all_gather(enc_wide_back[1], "fsdp", axis=0, tiled=True),
        lax.all_gather(enc_wide_back[2], "fsdp", axis=0, tiled=True),
        lax.all_gather(enc_wide_back[3], "fsdp", axis=0, tiled=True),
        lax.all_gather(enc_wide_back[4], "fsdp", axis=0, tiled=True),
    )
    dec_wide_back = (
        lax.all_gather(dec_norms.astype(jnp.bfloat16), "dp", axis=1, tiled=True),
        lax.all_gather(dec_embed.astype(jnp.bfloat16), "dp", axis=1, tiled=True),
        lax.all_gather(dec_qkv.astype(jnp.bfloat16), "dp", axis=1, tiled=True),
        lax.all_gather(dec_out.astype(jnp.bfloat16), "dp", axis=1, tiled=True),
        lax.all_gather(dec_up.astype(jnp.bfloat16), "dp", axis=1, tiled=True),
        lax.all_gather(dec_down.astype(jnp.bfloat16), "dp", axis=1, tiled=True),
    )
    dec_back = (
        lax.all_gather(dec_wide_back[0], "fsdp", axis=0, tiled=True),
        lax.all_gather(dec_wide_back[1], "fsdp", axis=0, tiled=True),
        lax.all_gather(dec_wide_back[2], "fsdp", axis=0, tiled=True),
        lax.all_gather(dec_wide_back[3], "fsdp", axis=0, tiled=True),
        lax.all_gather(dec_wide_back[4], "fsdp", axis=0, tiled=True),
        lax.all_gather(dec_wide_back[5], "fsdp", axis=0, tiled=True),
    )
    enc_params_back = (enc_back[0], enc_back[1], enc_back[2], enc_back[3], enc_back[4])
    dec_params_back = (dec_back[0], dec_back[2], dec_back[3], dec_back[4], dec_back[5])
    w_embed_back = dec_back[1]
    d_final, d_gain_final, d_shift_final = final_pull(cotangent)
    d_start, dec_grads = block_backward(
        dec_start, dec_params_back, dec_allowed, HEADS_D, dec_stored, d_final
    )
    d_token = jnp.sum(jnp.where(visible[..., None], 0.0, d_start), axis=(0, 1))
    d_picked = jnp.where(visible[..., None], d_start, 0.0).astype(jnp.bfloat16)
    d_table = jnp.zeros((slot_count, d_start.shape[-1]), jnp.bfloat16)
    d_table = d_table.at[jnp.where(visible, source_index, slot_count)].set(d_picked, mode="drop")
    d_table = d_table.reshape(peer_count, slot_rows, -1)
    g_embed_here = outer_sum(arrived, d_table)
    d_bias_here = jnp.sum(d_table.astype(jnp.float32), axis=(0, 1))
    returning = project_back(d_table, w_embed_back).astype(jnp.bfloat16)
    returned = lax.all_to_all(returning, "dp", split_axis=0, concat_axis=0, tiled=True)
    dec_norm_grad = jnp.concatenate(
        [dec_grads[0], jnp.stack([d_gain_final, d_shift_final, d_token, d_bias_here])], axis=0
    )
    dec_part = (
        lax.psum_scatter(
            dec_norm_grad.astype(jnp.bfloat16), "fsdp", scatter_dimension=0, tiled=True
        ).astype(jnp.float32),
        lax.psum_scatter(
            g_embed_here.astype(jnp.bfloat16), "fsdp", scatter_dimension=0, tiled=True
        ).astype(jnp.float32),
        lax.psum_scatter(
            dec_grads[1].astype(jnp.bfloat16), "fsdp", scatter_dimension=0, tiled=True
        ).astype(jnp.float32),
        lax.psum_scatter(
            dec_grads[2].astype(jnp.bfloat16), "fsdp", scatter_dimension=0, tiled=True
        ).astype(jnp.float32),
        lax.psum_scatter(
            dec_grads[3].astype(jnp.bfloat16), "fsdp", scatter_dimension=0, tiled=True
        ).astype(jnp.float32),
        lax.psum_scatter(
            dec_grads[4].astype(jnp.bfloat16), "fsdp", scatter_dimension=0, tiled=True
        ).astype(jnp.float32),
    )
    dec_final = (
        *in_one_piece(
            (dec_part[0].astype(jnp.bfloat16), dec_part[1].astype(jnp.bfloat16)), "dp", 1, 0
        ),
        sum_at_owner(dec_part[2].astype(jnp.bfloat16), "dp", 1),
        sum_at_owner(dec_part[3].astype(jnp.bfloat16), "dp", 1),
        sum_at_owner(dec_part[4].astype(jnp.bfloat16), "dp", 1),
        sum_at_owner(dec_part[5].astype(jnp.bfloat16), "dp", 1),
    )
    d_patches, enc_grads = block_backward(
        enc_rows, enc_params_back, enc_allowed, HEADS_E, enc_stored, returned.astype(jnp.float32)
    )
    enc_part = (
        lax.psum_scatter(
            enc_grads[0].astype(jnp.bfloat16), "fsdp", scatter_dimension=0, tiled=True
        ).astype(jnp.float32),
        lax.psum_scatter(
            enc_grads[1].astype(jnp.bfloat16), "fsdp", scatter_dimension=0, tiled=True
        ).astype(jnp.float32),
        lax.psum_scatter(
            enc_grads[2].astype(jnp.bfloat16), "fsdp", scatter_dimension=0, tiled=True
        ).astype(jnp.float32),
        lax.psum_scatter(
            enc_grads[3].astype(jnp.bfloat16), "fsdp", scatter_dimension=0, tiled=True
        ).astype(jnp.float32),
        lax.psum_scatter(
            enc_grads[4].astype(jnp.bfloat16), "fsdp", scatter_dimension=0, tiled=True
        ).astype(jnp.float32),
    )
    enc_final = (
        sum_at_owner(enc_part[0].astype(jnp.bfloat16), "dp", 1),
        sum_at_owner(enc_part[1].astype(jnp.bfloat16), "dp", 1),
        sum_at_owner(enc_part[2].astype(jnp.bfloat16), "dp", 1),
        sum_at_owner(enc_part[3].astype(jnp.bfloat16), "dp", 1),
        sum_at_owner(enc_part[4].astype(jnp.bfloat16), "dp", 1),
    )
    return (
        decoded,
        d_patches.reshape(-1, width_enc),
        enc_final[0],
        enc_final[1],
        enc_final[2],
        enc_final[3],
        enc_final[4],
        dec_final[0],
        dec_final[1],
        dec_final[2],
        dec_final[3],
        dec_final[4],
        dec_final[5],
    )


def solution(mesh):
    placed = (
        P(("dp", "fsdp"), None),
        P(("dp", "fsdp"), None),
        P(("dp", "fsdp"), None),
        P(("dp", "fsdp"), None),
        P(("dp", "fsdp"), None, None),
        P("fsdp", "dp"),
        P("fsdp", "dp"),
        P("fsdp", "dp"),
        P("fsdp", "dp"),
        P("fsdp", "dp"),
        P("fsdp", "dp"),
        P("fsdp", "dp"),
        P("fsdp", "dp"),
        P("fsdp", "dp"),
        P("fsdp", "dp"),
        P("fsdp", "dp"),
    )
    return jax.shard_map(
        per_device,
        mesh=mesh,
        in_specs=placed,
        out_specs=(
            P(("dp", "fsdp"), None, None),
            P(("dp", "fsdp"), None),
            P("fsdp", "dp"),
            P("fsdp", "dp"),
            P("fsdp", "dp"),
            P("fsdp", "dp"),
            P("fsdp", "dp"),
            P("fsdp", "dp"),
            P("fsdp", "dp"),
            P("fsdp", "dp"),
            P("fsdp", "dp"),
            P("fsdp", "dp"),
            P("fsdp", "dp"),
        ),
        check_vma=False,
    )
```

profile of v0, /device:TPU:0, one launch (start us, length us, event | category | flops | bytes accessed | tf_op | source)
XLA Modules:
  0.0 1074.0 jit_solution(9735098100267539737)
XLA Ops:
  11.7 37.4 %all_gather.90 = bf16[192,2304]{0,1:T(8,128)(2,1)S(1)} all-gather(bf16[192,288]{0,1:T(8,128)(2,1)S(1)} %copy.103), channel_id=1, replica_groups=mesh['dp'=8,'fsdp'=4] {'dp'}, dimensions={1}, use_global_device_ids=true | all-gather | bytes 995328 | tf_op jit(solution)/shard_map/all_gather | solution.py:176
  50.7 31.1 %all_gather.92 = bf16[192,768]{0,1:T(8,128)(2,1)S(1)} all-gather(bf16[192,96]{0,1:T(8,128)(2,1)S(1)} %copy.110), channel_id=1, replica_groups=mesh['dp'=8,'fsdp'=4] {'dp'}, dimensions={1}, use_global_device_ids=true | all-gather | bytes 331776 | tf_op jit(solution)/shard_map/all_gather | solution.py:177
  83.3 21.2 %all-gather.21.cloned.1.call-done = bf16[768,768]{0,1:T(8,128)(2,1)} async-done(((bf16[768,96]{0,1:T(8,128)(2,1)}), bf16[768,768]{0,1:T(8,128)(2,1)}) %all-gather.21.cloned.1.call-update) | async-done | bytes 1179664 | tf_op jit(solution)/shard_map/all_gather | solution.py:179
  106.9 31.4 %all_gather.102 = bf16[128,1536]{0,1:T(8,128)(2,1)S(1)} all-gather(bf16[128,192]{0,1:T(8,128)(2,1)S(1)} %convert_element_type.291), channel_id=1, replica_groups=mesh['dp'=8,'fsdp'=4] {'dp'}, dimensions={1}, use_global_device_ids=true | all-gather | bytes 442368 | tf_op jit(solution)/shard_map/all_gather | solution.py:191
  139.3 33.3 %all_gather.106 = bf16[128,2048]{1,0:T(8,128)(2,1)} all-gather(bf16[128,256]{1,0:T(8,128)(2,1)S(1)} %convert_element_type.299), channel_id=1, replica_groups=mesh['dp'=8,'fsdp'=4] {'dp'}, dimensions={1}, use_global_device_ids=true | all-gather | bytes 589824 | tf_op jit(solution)/shard_map/all_gather | solution.py:193
  177.4 19.2 %all-reduce = bf16[768]{0:T(1024)(128)(2,1)S(1)} all-reduce(bf16[768]{0:T(1024)(128)(2,1)S(1)} %dynamic-update-slice), channel_id=1, replica_groups=mesh['dp'=8,'fsdp'=4] {'dp'}, use_global_device_ids=true, to_apply=%add | all-reduce | flops 768 | bytes 3072
  202.6 7.3 convolution_convert_fusion
  210.0 6.7 copy.105
  232.8 9.9 fusion.36
  246.6 24.3 %multiply_convert_fusion.1 = (bf16[8,99,3072]{2,1,0:T(8,128)(2,1)}, f32[8,99,3072]{2,1,0:T(8,128)}) fusion(f32[8,99,3072]{2,1,0:T(8,128)S(1)} %get-tuple-element.104, u8[99,3072]{1,0:T(8,128)(4,1)S(1)} %get-tuple-element.53, u8[99,3072]{1,0:T(8,128)(4,1)S(1)} %get-tuple-element.52), kind=kLoop, calls=%fused_computation.22 | loop fusion | flops 170311680 | bytes 24938496 | tf_op jit(solution)/shard_map/convert_element_type | solution.py:125
  270.9 9.1 add_convert_fusion.2
  283.8 52.3 %all_gather.108 = bf16[512,512]{0,1:T(8,128)(2,1)S(1)} all-gather(bf16[512,64]{0,1:T(8,128)(2,1)S(1)} %convert_element_type.301), channel_id=1, replica_groups=mesh['dp'=8,'fsdp'=4] {'dp'}, dimensions={1}, use_global_device_ids=true | all-gather | bytes 589824 | tf_op jit(solution)/shard_map/all_gather | solution.py:194
  337.3 18.7 %all-gather.1 = bf16[8,64,2]{1,2,0:T(2,128)(2,1)S(1)} all-gather(bf16[1,64,2]{1,2,0:T(2,128)(2,1)S(1)} %convert_bitcast_fusion), channel_id=1, replica_groups=mesh['dp'=8,'fsdp'=4] {'dp'}, dimensions={0}, use_global_device_ids=true | all-gather | bytes 2304 | tf_op jit(solution)/shard_map/all_gather | solution.py:189
  362.1 30.5 %all_gather.104 = bf16[128,512]{0,1:T(8,128)(2,1)S(1)} all-gather(bf16[128,64]{0,1:T(8,128)(2,1)S(1)} %convert_element_type.297), channel_id=1, replica_groups=mesh['dp'=8,'fsdp'=4] {'dp'}, dimensions={1}, use_global_device_ids=true | all-gather | bytes 147456 | tf_op jit(solution)/shard_map/all_gather | solution.py:192
  392.7 30.8 %all_gather.98 = bf16[192,512]{0,1:T(8,128)(2,1)S(1)} all-gather(bf16[192,64]{0,1:T(8,128)(2,1)S(1)} %convert_element_type.285), channel_id=1, replica_groups=mesh['dp'=8,'fsdp'=4] {'dp'}, dimensions={1}, use_global_device_ids=true | all-gather | bytes 221184 | tf_op jit(solution)/shard_map/all_gather | solution.py:190
  423.6 7.5 all_gather.105
  431.7 8.7 all_gather.99
  461.6 19.2 %fusion.107 = (f32[2,16,529]{2,1,0:T(8,128)S(1)}, f32[2,16,529,529]{2,3,1,0:T(8,128)}) fusion(bf16[2,529,3,16,32]{1,4,3,2,0:T(8,128)(2,1)} %bitcast.268, pred[2,529,529]{1,2,0:T(8,128)(4,1)S(1)} %broadcast_compare_fusion), kind=kOutput, calls=%fused_computation.257 | convolution fusion | flops 599962112 | bytes 39068480 | tf_op jit(solution)/shard_map/grhd,gshd->ghrs/dot_general | solution.py:64
  480.9 17.2 %fusion = f32[2,16,529]{2,1,0:T(8,128)S(1)} fusion(f32[2,16,529,529]{2,3,1,0:T(8,128)} %get-tuple-element.106, f32[2,16,529]{2,1,0:T(8,128)S(1)} %get-tuple-element.105), kind=kLoop, calls=%fused_computation.8 | loop fusion | flops 17892896 | bytes 35955072 | tf_op jit(solution)/shard_map/reduce_sum | solution.py:75
  498.1 18.8 %fusion.58 = bf16[2,16,32,529]{3,2,1,0:T(8,128)(2,1)} fusion(f32[2,16,529,529]{2,3,1,0:T(8,128)} %get-tuple-element.106, f32[2,16,529]{2,1,0:T(8,128)S(1)} %fusion, f32[2,16,529]{2,1,0:T(8,128)S(1)} %get-tuple-element.105, bf16[2,529,3,16,32]{1,4,3,2,0:T(8,128)(2,1)} %bitcast.269), kind=kOutput, calls=%fused_computation.153 | convolution fusion | flops 600520832 | bytes 46438656 | tf_op jit(solution)/shard_map/ghrs,gshd->grhd/dot_general | solution.py:78
  520.2 6.6 fusion.42
  530.3 21.4 %multiply_convert_fusion.2 = (bf16[2,529,2048]{2,1,0:T(8,128)(2,1)}, f32[2,529,2048]{2,1,0:T(8,128)}) fusion(f32[2,529,2048]{2,1,0:T(8,128)S(1)} %get-tuple-element.109, u8[529,2048]{1,0:T(8,128)(4,1)S(1)} %get-tuple-element.55, u8[529,2048]{1,0:T(8,128)(4,1)S(1)} %get-tuple-element.54), kind=kLoop, calls=%fused_computation.45 | loop fusion | flops 151674880 | bytes 23834624 | tf_op jit(solution)/shard_map/convert_element_type | solution.py:125
  564.0 8.5 add_convert_fusion.1
  572.4 6.3 fusion.99
  587.7 18.2 %fusion.67 = bf16[2,529,1,16,32]{1,4,3,0,2:T(8,128)(2,1)} fusion(bf16[2,529,16,32]{1,3,2,0:T(8,128)(2,1)} %bitcast.278, f32[2,16,529,529]{2,3,1,0:T(8,128)} %get-tuple-element.106, f32[2,16,529]{2,1,0:T(8,128)S(1)} %log_add_fusion), kind=kOutput, calls=%fused_computation.165 | convolution fusion | flops 591565888 | bytes 38054144 | tf_op jit(solution)/shard_map/ghrs,grhd->gshd/dot_general | solution.py:94
  605.9 35.0 %multiply_reduce_fusion = (f32[2,16,529]{2,1,0:T(8,128)S(1)}, f32[2,16,529,529]{2,3,1,0:T(8,128)}) fusion(f32[2,16,529,529]{2,3,1,0:T(8,128)} %get-tuple-element.106, f32[2,16,529]{2,1,0:T(8,128)S(1)} %log_add_fusion, bf16[2,529,16,32]{1,3,2,0:T(8,128)(2,1)} %bitcast.279, bf16[2,529,3,16,32]{1,4,3,2,0:T(8,128)(2,1)} %bitcast.270), kind=kOutput, calls=%fused_computation.3 | convolution fusion | flops 599962112 | bytes 82485632 | tf_op jit(solution)/shard_map/grhd,gshd->ghrs/dot_general | solution.py:93
  640.9 36.0 %multiply_convert_fusion = bf16[2,16,529,529]{2,3,1,0:T(8,128)(2,1)} fusion(f32[2,16,529,529]{2,3,1,0:T(8,128)} %get-tuple-element.114, f32[2,16,529,529]{2,3,1,0:T(8,128)} %get-tuple-element.106, f32[2,16,529]{2,1,0:T(8,128)S(1)} %get-tuple-element.113, f32[2,16,529]{2,1,0:T(8,128)S(1)} %log_add_fusion), kind=kLoop, calls=%fused_computation.2 | loop fusion | flops 35819648 | bytes 89684544 | tf_op jit(solution)/shard_map/convert_element_type | solution.py:101
  676.9 11.9 %fusion.71 = bf16[2,529,1,16,32]{1,4,3,0,2:T(8,128)(2,1)} fusion(bf16[2,16,529,529]{2,3,1,0:T(8,128)(2,1)} %multiply_convert_fusion, bf16[2,529,3,16,32]{1,4,3,2,0:T(8,128)(2,1)} %bitcast.271), kind=kOutput, calls=%fused_computation.167 | convolution fusion | flops 574197760 | bytes 24348672 | tf_op jit(solution)/shard_map/ghrs,grhd->gshd/dot_general | solution.py:108
  688.8 10.7 fusion.70
  713.5 8.7 scatter_custom_fusion
  733.0 6.3 fusion.30
  739.3 21.5 %all-to-all-done.1 = bf16[8,99,768]{2,1,0:T(8,128)(2,1)S(1)} async-done(((bf16[8,99,768]{2,1,0:T(8,128)(2,1)}), bf16[8,99,768]{2,1,0:T(8,128)(2,1)S(1)}, u32[]{:S(2)}, u32[]{:S(2)}) %all-to-all-start.1) | async-done | bytes 1216544 | tf_op jit(solution)/shard_map/all_to_all | solution.py:271
  761.9 14.6 %add_convert_fusion = bf16[8,99,3072]{2,1,0:T(8,128)(2,1)S(1)} fusion(f32[8,99,3072]{2,1,0:T(8,128)} %get-tuple-element.86, f32[8,99,3072]{2,1,0:T(8,128)} %copy-done.19, bf16[8,99,768]{2,1,0:T(8,128)(2,1)} %copy-done.14, bf16[3072,768]{1,0:T(8,128)(2,1)} %all-gather.23.cloned.1.call-done), kind=kOutput, calls=%fused_computation.21 | convolution fusion | flops 3771187200 | bytes 30265344 | tf_op jit(solution)/shard_map/grc,wc->grw/dot_general | solution.py:49
  776.5 8.8 multiply_reduce_fusion.2
  791.5 7.2 bitcast_convert_fusion.3
  798.9 7.4 bitcast_convert_fusion.4
  845.2 9.6 bitcast_convert_fusion.1
  856.0 9.5 bitcast_convert_fusion
  875.0 7.3 multiply_reduce_fusion.4
  883.8 10.2 all-reduce.3
  895.4 6.0 all-to-all-start.2
  913.2 6.2 all-to-all-done.7
  925.1 6.9 all-to-all-done.8
  937.6 7.0 all-to-all-done.4
  950.9 8.2 all-to-all-done.11
  974.1 7.0 all-to-all-start.3
  983.5 24.6 %all-to-all-done.3 = bf16[8,192,288]{2,1,0:T(8,128)(2,1)} async-done(((bf16[8,192,288]{2,1,0:T(8,128)(2,1)}), bf16[8,192,288]{2,1,0:T(8,128)(2,1)}, u32[]{:S(2)}, u32[]{:S(2)}) %all-to-all-start.3) | async-done | bytes 884768 | tf_op jit(solution)/shard_map/all_to_all | solution.py:22
  1012.4 15.6 %reduce-scatter.16.cloned.1.call-done = bf16[768,768]{1,0:T(8,128)(2,1)} async-done(((bf16[3072,768]{1,0:T(8,128)(2,1)}), bf16[768,768]{1,0:T(8,128)(2,1)}) %reduce-scatter.16.cloned.1.call-update) | async-done | bytes 1179664 | tf_op jit(solution)/shard_map/reduce_scatter | solution.py:320
  (464 shorter events, 274.1 us)
Async XLA Ops:
  7.2 75.5 %all-gather.17.cloned.1.call-start = ((), (), s32[]{:S(2)}) async-start(), calls=%async_computation.23 | async-start | bytes 1327104 | tf_op jit(solution)/shard_map/all_gather | solution.py:178
  8.9 41.7 %copy-start.41 = (f32[192,96]{1,0:T(8,128)S(1)}, f32[192,96]{1,0:T(8,128)}, u32[]{:S(2)}) copy-start(f32[192,96]{1,0:T(8,128)} %param.23) | copy-start | bytes 221188
  8.9 95.5 %all-gather.21.cloned.1.call-start = ((), (), s32[]{:S(2)}) async-start(), calls=%async_computation.25 | async-start | bytes 1327104 | tf_op jit(solution)/shard_map/all_gather | solution.py:179
  10.6 192.0 %all-gather.13.cloned.1.call-start = ((), (), s32[]{:S(2)}) async-start(), calls=%async_computation.21 | async-start | bytes 4423680 | tf_op jit(solution)/shard_map/all_gather | solution.py:183
  50.5 176.7 %all-gather.15.cloned.1.call-start = ((), (), s32[]{:S(2)}) async-start(), calls=%async_computation.22 | async-start | bytes 1474560 | tf_op jit(solution)/shard_map/all_gather | solution.py:184
  82.6 150.1 %all-gather.19.cloned.1.call-start = ((), (), s32[]{:S(2)}) async-start(), calls=%async_computation.24 | async-start | bytes 5898240 | tf_op jit(solution)/shard_map/all_gather | solution.py:185
  83.2 56.1 %copy-start.39 = (f32[128,256]{1,0:T(8,128)S(1)}, f32[128,256]{1,0:T(8,128)}, u32[]{:S(2)}) copy-start(f32[128,256]{1,0:T(8,128)} %param.30) | copy-start | bytes 393220
  83.2 187.6 %all-gather.23.cloned.1.call-start = ((), (), s32[]{:S(2)}) async-start(), calls=%async_computation.26 | async-start | bytes 5898240 | tf_op jit(solution)/shard_map/all_gather | solution.py:186
  106.8 65.8 %copy-start.12 = (bf16[792,768]{1,0:T(8,128)(2,1)S(1)}, bf16[792,768]{1,0:T(8,128)(2,1)}, u32[]{:S(2)}) copy-start(bf16[792,768]{1,0:T(8,128)(2,1)} %param.16) | copy-start | bytes 3649540
  106.8 344.0 %all-gather.25.cloned.1.call-start = ((), (), s32[]{:S(2)}) async-start(), calls=%async_computation.27 | async-start | bytes 1966080 | tf_op jit(solution)/shard_map/all_gather | solution.py:199
  139.3 380.9 %all-gather.27.cloned.1.call-start = ((), (), s32[]{:S(2)}) async-start(), calls=%async_computation.28 | async-start | bytes 2621440 | tf_op jit(solution)/shard_map/all_gather | solution.py:201
  175.6 51.5 %copy-start.1 = (f32[8,99,768]{2,1,0:T(8,128)}, f32[8,99,768]{2,1,0:T(8,128)S(1)}, u32[]{:S(2)}) copy-start(f32[8,99,768]{2,1,0:T(8,128)S(1)} %reshape.326) | copy-start | bytes 7299076
  280.0 57.3 %copy-start.100 = (f32[2,64]{1,0:T(2,128)S(1)}, f32[2,64]{1,0:T(2,128)}, u32[]{:S(2)}) copy-start(f32[2,64]{1,0:T(2,128)} %param.26) | copy-start | bytes 1540
  280.0 76.1 %copy-start.77 = (s32[2,529]{1,0:T(2,128)S(1)}, s32[2,529]{1,0:T(2,128)}, u32[]{:S(2)}) copy-start(s32[2,529]{1,0:T(2,128)} %param.19) | copy-start | bytes 12700
  280.0 82.0 %copy-start.74 = (f32[128,64]{0,1:T(8,128)S(1)}, f32[128,64]{0,1:T(8,128)}, u32[]{:S(2)}) copy-start(f32[128,64]{0,1:T(8,128)} %param.29) | copy-start | bytes 98308
  280.0 82.0 %copy-start.51 = (f32[192,64]{0,1:T(8,128)S(1)}, f32[192,64]{0,1:T(8,128)}, u32[]{:S(2)}) copy-start(f32[192,64]{0,1:T(8,128)} %param.27) | copy-start | bytes 147460
  280.0 160.4 %all-to-all-start = ((bf16[8,99,768]{2,1,0:T(8,128)(2,1)}), bf16[8,99,768]{2,1,0:T(8,128)(2,1)S(1)}, u32[]{:S(2)}, u32[]{:S(2)}) async-start(bf16[8,99,768]{2,1,0:T(8,128)(2,1)} %add_convert_fusion.2), calls=%async_computation | async-start | bytes 2555904 | tf_op jit(solution)/shard_map/all_to_all | solution.py:215
  283.7 147.4 %copy-start.78 = (s32[2,529]{1,0:T(2,128)S(1)}, s32[2,529]{1,0:T(2,128)}, u32[]{:S(2)}) copy-start(s32[2,529]{1,0:T(2,128)} %param.18) | copy-start | bytes 12700
  283.8 267.9 %all-gather.29.cloned.1.call-start = ((), (), s32[]{:S(2)}) async-start(), calls=%async_computation.29 | async-start | bytes 2621440 | tf_op jit(solution)/shard_map/all_gather | solution.py:202
  337.2 532.4 %reduce-scatter.22.cloned.1.call-start = ((), (), s32[]{:S(2)}) async-start(), calls=%async_computation.36 | async-start | bytes 655360 | tf_op jit(solution)/shard_map/reduce_scatter | solution.py:285
  362.0 155.0 %copy-start.52 = (pred[2,529]{1,0:T(4,128)(4,1)}, pred[2,529]{1,0:T(4,128)(4,1)S(1)}, u32[]{:S(2)}) copy-start(pred[2,529]{1,0:T(4,128)(4,1)S(1)} %get-tuple-element.83) | copy-start | bytes 3178
  362.0 155.0 %copy-start.54 = (pred[2,529]{1,0:T(4,128)(4,1)}, pred[2,529]{1,0:T(4,128)(4,1)S(1)}, u32[]{:S(2)}) copy-start(pred[2,529]{1,0:T(4,128)(4,1)S(1)} %get-tuple-element.97) | copy-start | bytes 3178
  431.2 85.8 %copy-start.56 = (f32[1,512]{1,0:T(1,128)}, f32[1,512]{1,0:T(1,128)S(1)}, u32[]{:S(2)}) copy-start(f32[1,512]{1,0:T(1,128)S(1)} %get-tuple-element.95) | copy-start | bytes 6148
  431.2 89.0 %copy-start.94 = (f32[1,512]{1,0:T(1,128)}, f32[1,512]{1,0:T(1,128)S(1)}, u32[]{:S(2)}) copy-start(f32[1,512]{1,0:T(1,128)S(1)} %get-tuple-element.91) | copy-start | bytes 6148
  431.2 149.2 %copy-start.81 = (f32[1,512]{1,0:T(1,128)}, f32[1,512]{1,0:T(1,128)S(1)}, u32[]{:S(2)}) copy-start(f32[1,512]{1,0:T(1,128)S(1)} %get-tuple-element.92) | copy-start | bytes 6148
  449.0 68.0 %copy-start.3 = (bf16[2,529,512]{2,1,0:T(8,128)(2,1)}, bf16[2,529,512]{2,1,0:T(8,128)(2,1)S(1)}, u32[]{:S(2)}) copy-start(bf16[2,529,512]{2,1,0:T(8,128)(2,1)S(1)} %reshape.344) | copy-start | bytes 3250180
  519.7 59.0 %copy-start.10 = (f32[2,529,512]{2,1,0:T(8,128)}, f32[2,529,512]{2,1,0:T(8,128)S(1)}, u32[]{:S(2)}) copy-start(f32[2,529,512]{2,1,0:T(8,128)S(1)} %get-tuple-element.108) | copy-start | bytes 6500356
  519.7 60.7 %copy-start.43 = (f32[2,529]{1,0:T(2,128)}, f32[2,529]{1,0:T(2,128)S(1)}, u32[]{:S(2)}) copy-start(f32[2,529]{1,0:T(2,128)S(1)} %broadcast_multiply_fusion.1) | copy-start | bytes 12700
  520.2 60.3 %copy-start.58 = (f32[2,529]{1,0:T(2,128)}, f32[2,529]{1,0:T(2,128)S(1)}, u32[]{:S(2)}) copy-start(f32[2,529]{1,0:T(2,128)S(1)} %fusion.93) | copy-start | bytes 12700
  725.8 35.0 %all-to-all-start.1 = ((bf16[8,99,768]{2,1,0:T(8,128)(2,1)}), bf16[8,99,768]{2,1,0:T(8,128)(2,1)S(1)}, u32[]{:S(2)}, u32[]{:S(2)}) async-start(bf16[8,99,768]{2,1,0:T(8,128)(2,1)} %convolution_convert_fusion.3), calls=%async_computation.1 | async-start | bytes 2555904 | tf_op jit(solution)/shard_map/all_to_all | solution.py:271
  729.4 172.1 %reduce-scatter.18.cloned.1.call-start = ((), (), s32[]{:S(2)}) async-start(), calls=%async_computation.34 | async-start | bytes 983040 | tf_op jit(solution)/shard_map/reduce_scatter | solution.py:279
  732.9 178.4 %reduce-scatter.20.cloned.1.call-start = ((), (), s32[]{:S(2)}) async-start(), calls=%async_computation.35 | async-start | bytes 1966080 | tf_op jit(solution)/shard_map/reduce_scatter | solution.py:282
  739.3 183.6 %reduce-scatter.12.cloned.1.call-start = ((), (), s32[]{:S(2)}) async-start(), calls=%async_computation.31 | async-start | bytes 1474560 | tf_op jit(solution)/shard_map/reduce_scatter | solution.py:314
  791.5 144.0 %reduce-scatter.26.cloned.1.call-start = ((), (), s32[]{:S(2)}) async-start(), calls=%async_computation.38 | async-start | bytes 2621440 | tf_op jit(solution)/shard_map/reduce_scatter | solution.py:291
  798.8 150.1 %reduce-scatter.24.cloned.1.call-start = ((), (), s32[]{:S(2)}) async-start(), calls=%async_computation.37 | async-start | bytes 2621440 | tf_op jit(solution)/shard_map/reduce_scatter | solution.py:288
  806.3 157.2 %reduce-scatter.10.cloned.1.call-start = ((), (), s32[]{:S(2)}) async-start(), calls=%async_computation.30 | async-start | bytes 4423680 | tf_op jit(solution)/shard_map/reduce_scatter | solution.py:311
  844.5 136.6 %reduce-scatter.14.cloned.1.call-start = ((), (), s32[]{:S(2)}) async-start(), calls=%async_computation.32 | async-start | bytes 5898240 | tf_op jit(solution)/shard_map/reduce_scatter | solution.py:317
  854.8 173.2 %reduce-scatter.16.cloned.1.call-start = ((), (), s32[]{:S(2)}) async-start(), calls=%async_computation.33 | async-start | bytes 5898240 | tf_op jit(solution)/shard_map/reduce_scatter | solution.py:320
  871.4 24.0 %all-to-all-start.9 = ((bf16[8,128,64]{1,2,0:T(8,128)(2,1)}), bf16[8,128,64]{1,2,0:T(8,128)(2,1)S(1)}, u32[]{:S(2)}, u32[]{:S(2)}) async-start(bf16[8,128,64]{1,2,0:T(8,128)(2,1)} %bitcast.72), calls=%async_computation.16 | async-start | bytes 262144 | tf_op jit(solution)/shard_map/all_to_all | solution.py:22
  895.4 12.4 %all-to-all-start.2 = ((bf16[8,1,96]{2,1,0:T(2,128)(2,1)}), bf16[8,1,96]{2,1,0:T(2,128)(2,1)S(1)}, u32[]{:S(2)}, u32[]{:S(2)}) async-start(bf16[8,1,96]{2,1,0:T(2,128)(2,1)} %transpose_reshape.4), calls=%async_computation.2 | async-start | bytes 8192 | tf_op jit(solution)/shard_map/all_to_all | solution.py:22
  907.8 11.6 %all-to-all-start.7 = ((bf16[8,194,64]{1,2,0:T(8,128)(2,1)}), bf16[8,194,64]{1,2,0:T(8,128)(2,1)S(1)}, u32[]{:S(2)}, u32[]{:S(2)}) async-start(bf16[8,194,64]{1,2,0:T(8,128)(2,1)} %bitcast.65), calls=%async_computation.12 | async-start | bytes 524288 | tf_op jit(solution)/shard_map/all_to_all | solution.py:22
  919.4 12.6 %all-to-all-start.8 = ((bf16[8,128,192]{1,2,0:T(8,128)(2,1)}), bf16[8,128,192]{1,2,0:T(8,128)(2,1)S(1)}, u32[]{:S(2)}, u32[]{:S(2)}) async-start(bf16[8,128,192]{1,2,0:T(8,128)(2,1)} %bitcast.68), calls=%async_computation.14 | async-start | bytes 786432 | tf_op jit(solution)/shard_map/all_to_all | solution.py:22
  932.0 12.6 %all-to-all-start.4 = ((bf16[8,192,96]{2,1,0:T(8,128)(2,1)}), bf16[8,192,96]{2,1,0:T(8,128)(2,1)S(1)}, u32[]{:S(2)}, u32[]{:S(2)}) async-start(bf16[8,192,96]{2,1,0:T(8,128)(2,1)} %bitcast.264), calls=%async_computation.6 | async-start | bytes 786432 | tf_op jit(solution)/shard_map/all_to_all | solution.py:22
  945.4 13.7 %all-to-all-start.11 = ((bf16[8,512,64]{1,2,0:T(8,128)(2,1)}), bf16[8,512,64]{1,2,0:T(8,128)(2,1)S(1)}, u32[]{:S(2)}, u32[]{:S(2)}) async-start(bf16[8,512,64]{1,2,0:T(8,128)(2,1)} %bitcast.294), calls=%async_computation.20 | async-start | bytes 1048576 | tf_op jit(solution)/shard_map/all_to_all | solution.py:22
  959.1 15.0 %all-to-all-start.10 = ((bf16[8,128,256]{2,1,0:T(8,128)(2,1)}), bf16[8,128,256]{2,1,0:T(8,128)(2,1)}, u32[]{:S(2)}, u32[]{:S(2)}) async-start(bf16[8,128,256]{2,1,0:T(8,128)(2,1)} %bitcast.293), calls=%async_computation.18 | async-start | bytes 1048576 | tf_op jit(solution)/shard_map/all_to_all | solution.py:22
  974.1 34.1 %all-to-all-start.3 = ((bf16[8,192,288]{2,1,0:T(8,128)(2,1)}), bf16[8,192,288]{2,1,0:T(8,128)(2,1)}, u32[]{:S(2)}, u32[]{:S(2)}) async-start(bf16[8,192,288]{2,1,0:T(8,128)(2,1)} %bitcast.289), calls=%async_computation.4 | async-start | bytes 2359296 | tf_op jit(solution)/shard_map/all_to_all | solution.py:22
  1008.1 22.2 %all-to-all-start.5 = ((bf16[8,192,384]{2,1,0:T(8,128)(2,1)}), bf16[8,192,384]{2,1,0:T(8,128)(2,1)}, u32[]{:S(2)}, u32[]{:S(2)}) async-start(bf16[8,192,384]{2,1,0:T(8,128)(2,1)} %bitcast.290), calls=%async_computation.8 | async-start | bytes 2359296 | tf_op jit(solution)/shard_map/all_to_all | solution.py:22
  1030.3 34.2 %all-to-all-start.6 = ((bf16[8,768,96]{1,2,0:T(8,128)(2,1)}), bf16[8,768,96]{1,2,0:T(8,128)(2,1)}, u32[]{:S(2)}, u32[]{:S(2)}) async-start(bf16[8,768,96]{1,2,0:T(8,128)(2,1)} %bitcast.288), calls=%async_computation.10 | async-start | bytes 2359296 | tf_op jit(solution)/shard_map/all_to_all | solution.py:22
  (97 other events, 646.4 us)
Sparse Core Ops, SparseCore 0:
  10.6 50.5 all-gather.16
  64.0 40.3 all-gather.20
  106.6 29.5 all-gather.12
  138.1 17.4 all-gather.14
  157.1 37.4 all-gather.18
  196.5 37.4 all-gather.22
  235.6 19.6 all-gather.24
  256.8 22.5 all-gather.26
  337.3 21.7 all-gather.28
  699.6 18.2 reduce-scatter.21
  733.0 23.8 reduce-scatter.17
  759.3 28.1 reduce-scatter.19
  791.5 24.3 reduce-scatter.11
  818.3 31.4 reduce-scatter.25
  852.9 31.4 reduce-scatter.23
  886.8 40.4 reduce-scatter.9
  929.8 47.8 reduce-scatter.13
  980.1 47.8 reduce-scatter.15
where the time goes:
time: 1080 us; the launch traced here: 1070 us
  blocking collectives  321 us (30%)
  matrix products  296 us (27%)
  other arithmetic  151 us (14%)
  waiting for transfers between devices  127 us (12%)
  local copies, waits for them, and re-layouts  107 us (10%)
  starting transfers between devices  52.9 us (5%)
  between operations  18 us (2%)
    all_to_all x10, waiting for transfers between devices, sum_at_owner(): lax.all_to_all(in_blocks(value, dim, length), axis, 0, 0, tiled=True)  67.8 us
    dot_general x9, matrix products, project_back(): jnp.einsum('grc,wc->grw', gradient, right_side, preferred_element_type=jn...  57.5 us
    dot_general x9, matrix products, outer_sum(): jnp.einsum('grw,grc->wc', left_side, gradient, preferred_element_type=jnp...  53.4 us
    all_gather x1, blocking collectives, per_device(): lax.all_gather(dec_down.astype(jnp.bfloat16), 'dp', axis=1, tiled=True)  52.3 us
    dot_general x9, matrix products, project(): jnp.einsum('grw,wc->grc', left_side, right_side, preferred_element_type=j...  51.3 us
    convert_element_type x2, other arithmetic, block_forward(): activated = gelu_exact(up_proj).astype(jnp.bfloat16)  45.8 us
    all_to_all x10, starting transfers between devices, sum_at_owner(): lax.all_to_all(in_blocks(value, dim, length), axis, 0, 0, tiled=True)  44.5 us
    dot_general x2, matrix products, attend_back(): jnp.einsum('grhd,gshd->ghrs', d_heads, values, preferred_element_type=jnp...  40.2 us
  transfers between devices with their start and end apart: 30, of which 11 were waited for; matrix products, arithmetic and copies ran while one was open for 35% of the time, Pallas kernels for 0%

commit v1 on v0

v1 whole, which is shorter than its diff:
```python
import dataclasses
import functools

import jax
import jax.numpy as jnp
from jax import lax
from jax.experimental import pallas as pl
from jax.experimental.pallas import tpu as pltpu
from jax.sharding import PartitionSpec as P

HEADS_E = 12
HEADS_D = 16


EPSILON = 1e-06
NEGATIVE = -1000000000.0
MESH = pl.DeviceIdType.MESH
BF16 = jnp.bfloat16
F32 = jnp.float32


@dataclasses.dataclass(frozen=True)
class Entry:
    rows: int
    width: int
    by_core: bool

    @property
    def q(self):
        return self.width // 2 if self.by_core else self.width // 4

    @property
    def part(self):
        return self.rows // 2 if self.by_core else self.rows

    @property
    def whole(self):
        if self.by_core:
            return (4, 2, 2, self.part, self.width)
        return (4, 2, self.part, self.width)

    @property
    def cut(self):
        return -(-self.part // 32) * 16


def entry_of(rows, width):
    return Entry(rows, width, (width // 4) % 128 != 0)


def region(e, ref, zs, xs, rows, y, c):
    if e.by_core:
        return ref.at[zs, xs, c, rows, pl.ds(pl.multiple_of(y * e.q, 128), e.q)]
    return ref.at[zs, xs, rows, pl.ds(pl.multiple_of((2 * y + c) * e.q, 128), e.q)]


def region_pair(e, ref, zs, xs, rows, c):
    if e.by_core:
        return [ref.at[zs, xs, c, rows, :]]
    return [region(e, ref, zs, xs, rows, y, c) for y in range(2)]


def place():
    d, s = lax.axis_index("dp"), lax.axis_index("fsdp")
    return d // 2, lax.rem(d, 2), s // 2, lax.rem(s, 2)


def at(z, x, y, c):
    return (z * 2 + x, y * 2 + c)


def greet(z, x, y, c):
    barrier = pltpu.get_barrier_semaphore()
    peers = [at(lax.rem(z + k, 4), x, y, c) for k in (1, 2, 3)]
    peers += [at(z, 1 - x, y, c), at(z, x, 1 - y, c), at(z, x, y, 1 - c)]
    for peer in peers:
        pl.semaphore_signal(barrier, inc=1, device_id=peer, device_id_type=MESH)
    pl.semaphore_wait(barrier, len(peers))


def send(src, dst, sems, i, k, peer):
    return pltpu.make_async_remote_copy(
        src_ref=src,
        dst_ref=dst,
        send_sem=sems[0].at[i, k],
        recv_sem=sems[1].at[i, k],
        device_id=peer,
        device_id_type=MESH,
    )


ALL = slice(None)


def gather_stages(e, i, piece, out, sems, local_sem):
    z, x, y, c = place()
    top, bottom = slice(0, e.cut), slice(e.cut, e.part)

    def first():
        here = region(e, out, z, x, ALL, y, c)
        return [
            send(piece, here, sems, i, k - 1, at(lax.rem(z + k, 4), x, y, c)) for k in (1, 2, 3)
        ]

    def local():
        return pltpu.make_async_copy(piece, region(e, out, z, x, ALL, y, c), local_sem.at[i])

    def second():
        a = region(e, out, ALL, x, top, y, c)
        b = region(e, out, ALL, x, bottom, y, c)
        return [
            send(a, a, sems, i, 3, at(z, 1 - x, y, c)),
            send(b, b, sems, i, 4, at(z, x, 1 - y, c)),
        ]

    def third():
        a = region(e, out, ALL, ALL, top, y, c)
        found = [send(a, a, sems, i, 5, at(z, x, 1 - y, c))]
        for k, b in enumerate(region_pair(e, out, ALL, x, bottom, c)):
            found.append(send(b, b, sems, i, 6 + k, at(z, 1 - x, y, c)))
        return found

    def fourth():
        return [
            send(b, b, sems, i, 8 + k, at(z, x, y, 1 - c))
            for k, b in enumerate(region_pair(e, out, ALL, ALL, ALL, c))
        ]

    return local, [first, second, third, fourth]


def gather_kernel(entries, *refs):
    n = len(entries)
    pieces, outs = refs[:n], refs[n : 2 * n]
    send_sem, recv_sem, local_sem = refs[2 * n :]
    sems = (send_sem, recv_sem)
    z, x, y, c = place()
    plans = [
        gather_stages(e, i, pieces[i], outs[i], sems, local_sem) for i, e in enumerate(entries)
    ]
    locals_ = [plan[0]() for plan in plans]
    for copy in locals_:
        copy.start()
    greet(z, x, y, c)
    moving = {}
    for t in range(n + 4):
        for stage in (3, 2, 1, 0):
            i = t - stage
            if not 0 <= i < n:
                continue
            if stage > 0:
                for copy in moving[i, stage - 1]:
                    copy.wait_recv()
                if stage == 1:
                    locals_[i].wait()
            moving[i, stage] = plans[i][1][stage]()
            for copy in moving[i, stage]:
                copy.start()
    for i in range(n):
        for copy in moving[i, 3]:
            copy.wait_recv()
        for stage in range(4):
            for copy in moving[i, stage]:
                copy.wait_send()


def gather_all(entries, pieces):
    any_space = pl.BlockSpec(memory_space=pl.ANY)
    n = len(entries)
    return pl.pallas_call(
        functools.partial(gather_kernel, entries),
        out_shape=[jax.ShapeDtypeStruct(e.whole, BF16) for e in entries],
        in_specs=[any_space] * n,
        out_specs=[any_space] * n,
        scratch_shapes=[
            pltpu.SemaphoreType.DMA((n, 10)),
            pltpu.SemaphoreType.DMA((n, 10)),
            pltpu.SemaphoreType.DMA((n,)),
        ],
        compiler_params=pltpu.CompilerParams(
            collective_id=0, has_side_effects=True, vmem_limit_bytes=16 << 20
        ),
        name="gather_weights",
    )(*pieces)


def add_into(dst, src, count):
    def step(i, carry):
        dst[i] = (dst[i].astype(F32) + src[i].astype(F32)).astype(BF16)
        return carry

    lax.fori_loop(0, count, step, 0)


def reduce_stages(e, i, grad, out, buf, sems, local_sem):
    z, x, y, c = place()
    acc, r4, r3a, r3b, r2a, r2b, r1 = buf
    q, cut, part = e.q, e.cut, e.part
    top, bottom = slice(0, cut), slice(cut, part)

    def lanes(y):
        return pl.ds(pl.multiple_of(y * q, 128), q)

    def pair(ref):
        return [ref] if e.by_core else [ref.at[:, :, :, pl.ds(k * q, q)] for k in range(2)]

    def local():
        mine = zip(region_pair(e, grad, ALL, ALL, ALL, c), pair(acc))
        return [
            pltpu.make_async_copy(src, dst, local_sem.at[i, k]) for k, (src, dst) in enumerate(mine)
        ]

    def first():
        theirs = zip(region_pair(e, grad, ALL, ALL, ALL, 1 - c), pair(r4))
        return [
            send(src, dst, sems, i, k, at(z, x, y, 1 - c)) for k, (src, dst) in enumerate(theirs)
        ]

    def add_first():
        def step(k, carry):
            a, b = k // 2, lax.rem(k, 2)
            acc[a, b] = (acc[a, b].astype(F32) + r4[a, b].astype(F32)).astype(BF16)
            return carry

        lax.fori_loop(0, 8, step, 0)

    def second():
        return [
            send(acc.at[:, :, top, lanes(1 - y)], r3a, sems, i, 2, at(z, x, 1 - y, c)),
            send(acc.at[:, 1 - x, bottom, :], r3b, sems, i, 3, at(z, 1 - x, y, c)),
        ]

    def add_second():
        def step(k, carry):
            for b in range(2):
                acc[k, b, top, lanes(y)] = (
                    acc[k, b, top, lanes(y)].astype(F32) + r3a[k, b].astype(F32)
                ).astype(BF16)
            acc[k, x, bottom, :] = (
                acc[k, x, bottom, :].astype(F32) + r3b[k].astype(F32)
            ).astype(BF16)
            return carry

        lax.fori_loop(0, 4, step, 0)

    def third():
        return [
            send(acc.at[:, 1 - x, top, lanes(y)], r2a, sems, i, 4, at(z, 1 - x, y, c)),
            send(acc.at[:, x, bottom, lanes(1 - y)], r2b, sems, i, 5, at(z, x, 1 - y, c)),
        ]

    def add_third():
        def step(k, carry):
            acc[k, x, top, lanes(y)] = (
                acc[k, x, top, lanes(y)].astype(F32) + r2a[k].astype(F32)
            ).astype(BF16)
            acc[k, x, bottom, lanes(y)] = (
                acc[k, x, bottom, lanes(y)].astype(F32) + r2b[k].astype(F32)
            ).astype(BF16)
            return carry

        lax.fori_loop(0, 4, step, 0)

    def fourth():
        found = []
        for k in (1, 2, 3):
            there = lax.rem(z + k, 4)
            found.append(
                send(acc.at[there, x, :, lanes(y)], r1.at[k - 1], sems, i, 5 + k, at(there, x, y, c))
            )
        return found

    def add_fourth():
        total = acc[z, x, :, lanes(y)].astype(F32)
        for k in range(3):
            total = total + r1[k].astype(F32)
        out[...] = total

    return local, [(first, add_first), (second, add_second), (third, add_third), (fourth, add_fourth)]


def reduce_buffers(e):
    return [
        (4, 2, e.part, 2 * e.q),
        (4, 2, e.part, 2 * e.q),
        (4, 2, e.cut, e.q),
        (4, e.part - e.cut, 2 * e.q),
        (4, e.cut, e.q),
        (4, e.part - e.cut, e.q),
        (3, e.part, e.q),
    ]


def reduce_kernel(entries, *refs):
    n = len(entries)
    grads, outs = refs[:n], refs[n : 2 * n]
    bufs = [refs[2 * n + 7 * i : 2 * n + 7 * i + 7] for i in range(n)]
    send_sem, recv_sem, local_sem = refs[9 * n :]
    sems = (send_sem, recv_sem)
    z, x, y, c = place()
    plans = [
        reduce_stages(e, i, grads[i], outs[i], bufs[i], sems, local_sem)
        for i, e in enumerate(entries)
    ]
    locals_ = [plan[0]() for plan in plans]
    for copies in locals_:
        for copy in copies:
            copy.start()
    greet(z, x, y, c)
    moving = {}
    for t in range(n + 4):
        for stage in (4, 3, 2, 1, 0):
            i = t - stage
            if not 0 <= i < n:
                continue
            if stage > 0:
                for copy in moving[i, stage - 1]:
                    copy.wait_recv()
                if stage == 1:
                    for copy in locals_[i]:
                        copy.wait()
                plans[i][1][stage - 1][1]()
            if stage < 4:
                moving[i, stage] = plans[i][1][stage][0]()
                for copy in moving[i, stage]:
                    copy.start()
    for i in range(n):
        for stage in range(4):
            for copy in moving[i, stage]:
                copy.wait_send()


def reduce_all(entries, grads):
    any_space = pl.BlockSpec(memory_space=pl.ANY)
    n = len(entries)
    scratch = [pltpu.VMEM(shape, BF16) for e in entries for shape in reduce_buffers(e)]
    return pl.pallas_call(
        functools.partial(reduce_kernel, entries),
        out_shape=[jax.ShapeDtypeStruct((e.part, e.q), F32) for e in entries],
        in_specs=[any_space] * n,
        out_specs=[pl.BlockSpec(memory_space=pltpu.VMEM)] * n,
        scratch_shapes=scratch
        + [
            pltpu.SemaphoreType.DMA((n, 9)),
            pltpu.SemaphoreType.DMA((n, 9)),
            pltpu.SemaphoreType.DMA((n, 2)),
        ],
        compiler_params=pltpu.CompilerParams(
            collective_id=1, has_side_effects=True, vmem_limit_bytes=56 << 20
        ),
        name="reduce_gradients",
    )(*grads)


CORE_SWAP = [(0, 1), (1, 0), (2, 3), (3, 2)]
NORM_ROWS = 32


def halves_to_pieces(blocks):
    c = lax.rem(lax.axis_index("fsdp"), 2)
    both = jnp.concatenate([b.reshape(2, b.shape[0] // 2, b.shape[1]) for b in blocks], axis=1)
    mine = lax.dynamic_index_in_dim(both, c, 0, keepdims=False)
    other = lax.dynamic_index_in_dim(both, 1 - c, 0, keepdims=False)
    came = lax.ppermute(other, "fsdp", CORE_SWAP)
    left, right = jnp.where(c == 0, mine, came), jnp.where(c == 0, came, mine)
    return jnp.concatenate([left, right], axis=1)


def pieces_to_halves(pieces):
    c = lax.rem(lax.axis_index("fsdp"), 2)
    whole = jnp.concatenate(pieces, axis=0)
    q = whole.shape[1] // 2
    left, right = whole[:, :q], whole[:, q:]
    mine, other = jnp.where(c == 0, left, right), jnp.where(c == 0, right, left)
    came = lax.ppermute(other, "fsdp", CORE_SWAP)
    first, second = jnp.where(c == 0, mine, came), jnp.where(c == 0, came, mine)
    sizes = [p.shape[0] for p in pieces]
    ends = [sum(sizes[:k]) for k in range(1, len(sizes))]
    return [
        jnp.concatenate([a, b], axis=0)
        for a, b in zip(jnp.split(first, ends, axis=0), jnp.split(second, ends, axis=0))
    ]


def gather_masters(staged, enc_norms, dec_norms, weights):
    blocks = [w.astype(BF16).T for w in weights]
    if not staged:
        whole = []
        for b in blocks:
            tall = lax.all_gather(b, "dp", axis=0, tiled=True)
            whole.append(lax.all_gather(tall, "fsdp", axis=1, tiled=True))
        norms = []
        for rows in (enc_norms, dec_norms):
            wide = lax.all_gather(rows.astype(BF16), "dp", axis=1, tiled=True)
            norms.append(lax.all_gather(wide, "fsdp", axis=0, tiled=True))
        return norms[0], norms[1], whole
    entries = [entry_of(b.shape[0], 4 * b.shape[1]) for b in blocks]
    pieces = list(blocks)
    cores = [k for k, e in enumerate(entries) if e.by_core]
    joined = halves_to_pieces([blocks[k] for k in cores])
    start = 0
    for k in cores:
        pieces[k] = lax.slice_in_dim(joined, start, start + entries[k].part, axis=0)
        start += entries[k].part
    small = jnp.zeros((NORM_ROWS, 128), BF16)
    small = small.at[: enc_norms.shape[0], : enc_norms.shape[1]].set(enc_norms.astype(BF16))
    half = NORM_ROWS // 2
    small = small.at[half : half + dec_norms.shape[0], : dec_norms.shape[1]].set(
        dec_norms.astype(BF16)
    )
    entries = [entry_of(NORM_ROWS, 512)] + entries
    whole = gather_all(entries, [small] + pieces)
    tiles = whole[0].reshape(8, NORM_ROWS, 4, 128)
    norms = []
    for start, rows in ((0, enc_norms), (half, dec_norms)):
        n, width = rows.shape
        part = tiles[:, start : start + n, :, :width]
        norms.append(part.transpose(2, 1, 0, 3).reshape(4 * n, 8 * width))
    return norms[0], norms[1], [w.reshape(-1, e.width) for w, e in zip(whole[1:], entries[1:])]


def reduce_masters(staged, g_enc_norms, g_dec_norms, grads):
    if not staged:
        def owner(value, rows, lanes):
            part = lax.psum_scatter(value.astype(BF16), "fsdp", scatter_dimension=lanes, tiled=True)
            return sum_at_owner(part, "dp", rows)

        return (
            owner(g_enc_norms, 1, 0),
            owner(g_dec_norms, 1, 0),
            [owner(g, 0, 1).T for g in grads],
        )
    entries = [entry_of(g.shape[0] // 8, g.shape[1]) for g in grads]
    values = [g.astype(BF16).reshape(e.whole) for g, e in zip(grads, entries)]
    half = NORM_ROWS // 2
    tiles = jnp.zeros((8, NORM_ROWS, 4, 128), BF16)
    for start, rows in ((0, g_enc_norms), (half, g_dec_norms)):
        n, width = rows.shape[0] // 4, rows.shape[1] // 8
        part = rows.astype(BF16).reshape(4, n, 8, width).transpose(2, 1, 0, 3)
        tiles = tiles.at[:, start : start + n, :, :width].set(part)
    small = entry_of(NORM_ROWS, 512)
    sums = reduce_all([small] + entries, [tiles.reshape(small.whole)] + values)
    blocks = list(sums[1:])
    cores = [k for k, e in enumerate(entries) if e.by_core]
    for k, b in zip(cores, pieces_to_halves([blocks[k] for k in cores])):
        blocks[k] = b
    n_enc, w_enc = g_enc_norms.shape[0] // 4, g_enc_norms.shape[1] // 8
    n_dec, w_dec = g_dec_norms.shape[0] // 4, g_dec_norms.shape[1] // 8
    return (
        sums[0][:n_enc, :w_enc],
        sums[0][half : half + n_dec, :w_dec],
        [b.T for b in blocks],
    )


def in_blocks(value, dim, length):
    dims = value.shape
    pieces = value.reshape(*dims[:dim], length, dims[dim] // length, *dims[dim + 1 :])
    return jnp.moveaxis(pieces, dim, 0)


def sum_at_owner(value, axis, dim):
    length = lax.axis_size(axis)
    pieces = lax.all_to_all(in_blocks(value, dim, length), axis, 0, 0, tiled=True)
    return jnp.sum(pieces.astype(jnp.float32), axis=0)


def layer_norm(values, scale_gain, norm_shift):
    row_mean = jnp.mean(values, axis=-1, keepdims=True)
    centred = values - row_mean
    spread = jnp.mean(centred * centred, axis=-1, keepdims=True)
    return centred * lax.rsqrt(spread + EPSILON) * scale_gain + norm_shift


def gelu_exact(values):
    return jax.nn.gelu(values, approximate=False)


def project(left_side, right_side):
    return jnp.einsum("grw,cw->grc", left_side, right_side, preferred_element_type=jnp.float32)


def project_back(gradient, right_side):
    return jnp.einsum("grc,cw->grw", gradient, right_side, preferred_element_type=jnp.float32)


def outer_sum(left_side, gradient):
    return jnp.einsum("grc,grw->cw", gradient, left_side, preferred_element_type=jnp.float32)


def split_heads(joined_qkv, head_count):
    groups, row_count, triple = joined_qkv.shape
    head_size = triple // 3 // head_count
    pieces = joined_qkv.reshape(groups, row_count, 3, head_count, head_size)
    return (pieces[:, :, 0], pieces[:, :, 1], pieces[:, :, 2], head_size)


def scores_of(queries, key_part, allowed, head_size):
    raw_scores = jnp.einsum(
        "grhd,gshd->ghrs", queries, key_part, preferred_element_type=jnp.float32
    ) * head_size ** (-0.5)
    return jnp.where(allowed[:, None], raw_scores, NEGATIVE)


def attend(joined_qkv, allowed, head_count):
    queries, key_part, values, head_size = split_heads(joined_qkv, head_count)
    scores = scores_of(queries, key_part, allowed, head_size)
    row_max = jnp.max(scores, axis=-1, keepdims=True)
    weights = jnp.exp(scores - row_max)
    row_total = jnp.sum(weights, axis=-1, keepdims=True)
    probability = weights / row_total
    log_total = row_max + jnp.log(row_total)
    mixture = jnp.einsum(
        "ghrs,gshd->grhd",
        probability.astype(jnp.bfloat16),
        values,
        preferred_element_type=jnp.float32,
    )
    return (mixture.reshape(joined_qkv.shape[0], joined_qkv.shape[1], -1), log_total)


def attend_back(joined_qkv, allowed, head_count, log_total, d_mixed):
    queries, key_part, values, head_size = split_heads(joined_qkv, head_count)
    scores = scores_of(queries, key_part, allowed, head_size)
    probability = jnp.exp(scores - log_total)
    groups, row_count = (d_mixed.shape[0], d_mixed.shape[1])
    d_heads = d_mixed.reshape(groups, row_count, head_count, head_size)
    d_probs = jnp.einsum("grhd,gshd->ghrs", d_heads, values, preferred_element_type=jnp.float32)
    d_value = jnp.einsum(
        "ghrs,grhd->gshd",
        probability.astype(jnp.bfloat16),
        d_heads,
        preferred_element_type=jnp.float32,
    )
    centre = jnp.sum(d_probs * probability, axis=-1, keepdims=True)
    d_scores = (probability * (d_probs - centre)).astype(jnp.bfloat16)
    score_scale = head_size ** (-0.5)
    d_query = (
        jnp.einsum("ghrs,gshd->grhd", d_scores, key_part, preferred_element_type=jnp.float32)
        * score_scale
    )
    d_key = (
        jnp.einsum("ghrs,grhd->gshd", d_scores, queries, preferred_element_type=jnp.float32)
        * score_scale
    )
    stacked = jnp.stack([d_query, d_key, d_value], axis=2)
    return stacked.reshape(groups, row_count, -1).astype(jnp.bfloat16)


def block_forward(inputs, params, allowed, head_count):
    norm_rows, w_qkv, w_out, w_up, w_down = params
    gain_rows = norm_rows.astype(jnp.float32)
    h_one = layer_norm(inputs, gain_rows[0], gain_rows[1]).astype(jnp.bfloat16)
    joined_qkv = project(h_one, w_qkv).astype(jnp.bfloat16)
    mixture, log_total = attend(joined_qkv, allowed, head_count)
    mixture = mixture.astype(jnp.bfloat16)
    x_one = inputs + project(mixture, w_out)
    h_two = layer_norm(x_one, gain_rows[2], gain_rows[3]).astype(jnp.bfloat16)
    up_proj = project(h_two, w_up)
    activated = gelu_exact(up_proj).astype(jnp.bfloat16)
    x_two = x_one + project(activated, w_down)
    return (x_two, (joined_qkv, log_total, mixture, x_one, up_proj))


def block_backward(inputs, params, allowed, head_count, stored, d_two):
    norm_rows, w_qkv, w_out, w_up, w_down = params
    gain_rows = norm_rows.astype(jnp.float32)
    joined_qkv, log_total, mixture, x_one, up_proj = stored
    d_branch = d_two.astype(jnp.bfloat16)
    activated, gelu_pull = jax.vjp(gelu_exact, up_proj)
    g_down = outer_sum(activated.astype(jnp.bfloat16), d_branch)
    d_up = gelu_pull(project_back(d_branch, w_down))[0].astype(jnp.bfloat16)
    h_two, norm_two_pull = jax.vjp(layer_norm, x_one, gain_rows[2], gain_rows[3])
    g_up = outer_sum(h_two.astype(jnp.bfloat16), d_up)
    d_x_two_norm, d_gain_two, d_shift_two = norm_two_pull(project_back(d_up, w_up))
    d_one = d_two + d_x_two_norm
    d_attn = d_one.astype(jnp.bfloat16)
    g_out = outer_sum(mixture, d_attn)
    d_mixed = project_back(d_attn, w_out).astype(jnp.bfloat16)
    d_qkv = attend_back(joined_qkv, allowed, head_count, log_total, d_mixed)
    h_one, norm_one_pull = jax.vjp(layer_norm, inputs, gain_rows[0], gain_rows[1])
    g_qkv = outer_sum(h_one.astype(jnp.bfloat16), d_qkv)
    d_x_one_norm, d_gain_one, d_shift_one = norm_one_pull(project_back(d_qkv, w_qkv))
    g_norms = jnp.stack([d_gain_one, d_shift_one, d_gain_two, d_shift_two])
    return (d_one + d_x_one_norm, (g_norms, g_qkv, g_out, g_up, g_down))


def per_device(
    staged,
    patches,
    send_counts,
    dec_segment,
    source_index,
    cotangent,
    enc_norms,
    enc_qkv,
    enc_out,
    enc_up,
    enc_down,
    dec_norms,
    dec_embed,
    dec_qkv,
    dec_out,
    dec_up,
    dec_down,
):
    peer_count = lax.axis_size("dp")
    width_enc = patches.shape[1]
    slot_rows = patches.shape[0] // peer_count
    masters = (enc_qkv, enc_out, enc_up, enc_down, dec_embed, dec_qkv, dec_out, dec_up, dec_down)
    norms_e, norms_d, whole = gather_masters(staged, enc_norms, dec_norms, masters)
    enc_rows = patches.astype(jnp.float32).reshape(peer_count, slot_rows, width_enc)
    live_counts = send_counts.reshape(peer_count)
    live_rows = (
        jnp.arange(slot_rows, dtype=jnp.int32)[None, :] >= (slot_rows - live_counts)[:, None]
    )
    enc_allowed = jnp.broadcast_to(live_rows[:, None, :], (peer_count, slot_rows, slot_rows))
    enc_params = (norms_e, *whole[:4])
    enc_result, enc_stored = block_forward(enc_rows, enc_params, enc_allowed, HEADS_E)
    enc_send = enc_result.astype(jnp.bfloat16)
    dec_gains = norms_d.astype(jnp.float32)
    w_embed = whole[4]
    embedded = (project(enc_send, w_embed) + dec_gains[7]).astype(jnp.bfloat16)
    arrived = lax.all_to_all(embedded, "dp", split_axis=0, concat_axis=0, tiled=True)
    slot_count = peer_count * slot_rows
    slot_table = arrived.reshape(slot_count, -1)
    visible = source_index >= 0
    picked = jnp.take(slot_table, jnp.where(visible, source_index, 0), axis=0)
    dec_start = jnp.where(visible[..., None], picked.astype(jnp.float32), dec_gains[6])
    dec_allowed = dec_segment[:, :, None] == dec_segment[:, None, :]
    dec_params = (norms_d, *whole[5:])
    dec_two, dec_stored = block_forward(dec_start, dec_params, dec_allowed, HEADS_D)
    decoded, final_pull = jax.vjp(layer_norm, dec_two, dec_gains[4], dec_gains[5])
    d_final, d_gain_final, d_shift_final = final_pull(cotangent)
    d_start, dec_grads = block_backward(
        dec_start, dec_params, dec_allowed, HEADS_D, dec_stored, d_final
    )
    d_token = jnp.sum(jnp.where(visible[..., None], 0.0, d_start), axis=(0, 1))
    d_picked = jnp.where(visible[..., None], d_start, 0.0).astype(jnp.bfloat16)
    d_table = jnp.zeros((slot_count, d_start.shape[-1]), jnp.bfloat16)
    d_table = d_table.at[jnp.where(visible, source_index, slot_count)].set(d_picked, mode="drop")
    d_table = d_table.reshape(peer_count, slot_rows, -1)
    returned = lax.all_to_all(d_table, "dp", split_axis=0, concat_axis=0, tiled=True)
    g_embed = outer_sum(enc_send, returned)
    d_bias = jnp.sum(returned.astype(jnp.float32), axis=(0, 1))
    d_enc = project_back(returned, w_embed).astype(jnp.bfloat16)
    d_patches, enc_grads = block_backward(
        enc_rows, enc_params, enc_allowed, HEADS_E, enc_stored, d_enc.astype(jnp.float32)
    )
    g_dec_norms = jnp.concatenate(
        [dec_grads[0], jnp.stack([d_gain_final, d_shift_final, d_token, d_bias])], axis=0
    )
    s_enc_norms, s_dec_norms, sums = reduce_masters(
        staged, enc_grads[0], g_dec_norms, [*enc_grads[1:], g_embed, *dec_grads[1:]]
    )
    return (
        decoded,
        d_patches.reshape(-1, width_enc),
        s_enc_norms,
        *sums[:4],
        s_dec_norms,
        *sums[4:],
    )


def solution(mesh):
    placed = (
        P(("dp", "fsdp"), None),
        P(("dp", "fsdp"), None),
        P(("dp", "fsdp"), None),
        P(("dp", "fsdp"), None),
        P(("dp", "fsdp"), None, None),
        P("fsdp", "dp"),
        P("fsdp", "dp"),
        P("fsdp", "dp"),
        P("fsdp", "dp"),
        P("fsdp", "dp"),
        P("fsdp", "dp"),
        P("fsdp", "dp"),
        P("fsdp", "dp"),
        P("fsdp", "dp"),
        P("fsdp", "dp"),
        P("fsdp", "dp"),
    )
    staged = (mesh.shape["dp"], mesh.shape["fsdp"]) == (8, 4)
    return jax.shard_map(
        functools.partial(per_device, staged),
        mesh=mesh,
        in_specs=placed,
        out_specs=(
            P(("dp", "fsdp"), None, None),
            P(("dp", "fsdp"), None),
            P("fsdp", "dp"),
            P("fsdp", "dp"),
            P("fsdp", "dp"),
            P("fsdp", "dp"),
            P("fsdp", "dp"),
            P("fsdp", "dp"),
            P("fsdp", "dp"),
            P("fsdp", "dp"),
            P("fsdp", "dp"),
            P("fsdp", "dp"),
            P("fsdp", "dp"),
        ),
        check_vma=False,
    )
```

time: 1080 us -> 778 us (0.72)
  blocking collectives: 321 us -> 0 us
  Pallas kernels: 0 us -> 237 us
  waiting for transfers between devices: 127 us -> 21.9 us
  starting transfers between devices: 52.9 us -> 12.7 us
  matrix products: 296 us -> 257 us
  between operations: 18 us -> 2.73 us
  other arithmetic: 151 us -> 139 us
    all_gather x12 -> x0, blocking collectives: 292 us -> none  [the longest x1 52.3 us: per_device(): lax.all_gather(dec_down.astype(jnp.bfloat16), 'dp', axis=1, tiled=True)]
    pallas_call x0 -> x2, Pallas kernels: none -> 237 us  [the longest x1 119 us: gather_all(): pl.pallas_call(functools.partial(gather_kernel, entries), out_shape=[jax....]
    all_to_all x12 -> x2, waiting for transfers between devices: 89.3 us -> 21.8 us  [the longest x1 17.7 us: per_device(): lax.all_to_all(embedded, 'dp', split_axis=0, concat_axis=0, tiled=True)]
    all_to_all x12 -> x2, starting transfers between devices: 51.8 us -> 12.1 us  [the longest x1 7.69 us: per_device(): lax.all_to_all(embedded, 'dp', split_axis=0, concat_axis=0, tiled=True)]
    dot_general x27, matrix products: 162 us -> 123 us  [the longest x9 44.9 us: outer_sum(): jnp.einsum('grc,grw->cw', gradient, left_side, preferred_element_type=jnp...]
    unnamed x2 -> x0, blocking collectives: 29.5 us -> none
    all_gather x9 -> x0, waiting for transfers between devices: 21.2 us -> none  [the longest x1 21.2 us: per_device(): lax.all_gather(enc_down.astype(jnp.bfloat16), 'dp', axis=1, tiled=True)]
    reduce_scatter x9 -> x0, waiting for transfers between devices: 15.7 us -> none  [the longest x1 15.6 us: per_device(): lax.psum_scatter(enc_grads[4].astype(jnp.bfloat16), 'fsdp', scatter_dimen...]
  transfers between devices with their start and end apart: 30 -> 4, of which waited for: 11 -> 2; matrix products, arithmetic and copies ran while one was open for 35% -> 5% of each run, Pallas kernels for 0% -> 0%
where the time goes in v1:
time: 778 us; the launch traced here: 771 us
  matrix products  257 us (33%)
  Pallas kernels  237 us (30%)
  other arithmetic  139 us (18%)
  local copies, waits for them, and re-layouts  101 us (13%)
  waiting for transfers between devices  21.9 us (3%)
  starting transfers between devices  12.7 us (2%)
    pallas_call x1, Pallas kernels, gather_all(): pl.pallas_call(functools.partial(gather_kernel, entries), out_shape=[jax....  119 us
    pallas_call x1, Pallas kernels, reduce_all(): pl.pallas_call(functools.partial(reduce_kernel, entries), out_shape=[jax....  118 us
    convert_element_type x2, other arithmetic, block_forward(): activated = gelu_exact(up_proj).astype(jnp.bfloat16)  45.8 us
    dot_general x9, matrix products, outer_sum(): jnp.einsum('grc,grw->cw', gradient, left_side, preferred_element_type=jnp...  44.9 us
    dot_general x9, matrix products, project_back(): jnp.einsum('grc,cw->grw', gradient, right_side, preferred_element_type=jn...  42.2 us
    dot_general x2, matrix products, attend_back(): jnp.einsum('grhd,gshd->ghrs', d_heads, values, preferred_element_type=jnp...  39.4 us
    convert_element_type x2, other arithmetic, attend_back(): d_scores = (probability * (d_probs - centre)).astype(jnp.bfloat16)  37.1 us
    dot_general x9, matrix products, project(): jnp.einsum('grw,cw->grc', left_side, right_side, preferred_element_type=j...  36.3 us
  transfers between devices with their start and end apart: 4, of which 2 were waited for; matrix products, arithmetic and copies ran while one was open for 5% of the time, Pallas kernels for 0%

profile of v1, /device:TPU:0, one launch (start us, length us, event | category | flops | bytes accessed | tf_op | source)
XLA Modules:
  0.0 771.2 jit_solution(8181961660441327671)
XLA Ops:
  13.6 118.9 %gather_weights.1 = (bf16[4,2,32,512]{3,2,1,0:T(8,128)(2,1)S(1)}, bf16[4,2,2,144,768]{4,3,2,1,0:T(8,128)(2,1)S(1)}, bf16[4,2,2,48,768]{4,3,2,1,0:T(8,128)(2,1)S(...) custom-call(bf16[32,128]{1,0:T(8,128)(2,1)S(1)} %copy-done.13, ...), custom_call_target="tpu_custom_call" | custom-call | tf_op jit(solution)/shard_map/gather_weights/pallas_call | solution.py:170
  155.2 2.8 add_convert_fusion.4
  158.1 2.7 convert_element_type.254
  160.8 6.4 convolution_convert_fusion
  167.2 6.7 copy.66
  173.8 3.8 fusion.75
  179.9 2.6 fusion.36
  186.4 6.5 fusion.26
  192.9 24.4 %multiply_convert_fusion.1 = (bf16[8,99,3072]{2,1,0:T(8,128)(2,1)}, f32[8,99,3072]{2,1,0:T(8,128)}) fusion(f32[8,99,3072]{2,1,0:T(8,128)S(1)} %get-tuple-element.183, u8[99,3072]{1,0:T(8,128)(4,1)S(1)} %get-tuple-element.128, u8[99,3072]{1,0:T(8,128)(4,1)S(1)} %get-tuple-element.127), kind=kLoop, calls=%fused_computation.22 | loop fusion | flops 170311680 | bytes 24938496 | tf_op jit(solution)/shard_map/convert_element_type | solution.py:560
  217.4 6.8 add_convert_fusion.2
  227.1 7.7 all-to-all-start
  239.2 17.7 %all-to-all-done = bf16[8,99,512]{2,1,0:T(8,128)(2,1)} async-done(((bf16[8,99,512]{2,1,0:T(8,128)(2,1)}), bf16[8,99,512]{2,1,0:T(8,128)(2,1)}, u32[]{:S(2)}, u32[]{:S(2)}) %all-to-all-start) | async-done | bytes 811040 | tf_op jit(solution)/shard_map/all_to_all | solution.py:624
  258.3 4.6 gather_fusion
  266.4 3.7 convolution_convert_fusion.1
  270.1 5.7 copy.73
  275.7 19.2 %fusion.77 = (f32[2,16,529]{2,1,0:T(8,128)S(1)}, f32[2,16,529,529]{2,3,1,0:T(8,128)}) fusion(bf16[2,529,3,16,32]{1,4,3,2,0:T(8,128)(2,1)} %bitcast.284, pred[2,529,529]{1,2,0:T(8,128)(4,1)S(1)} %broadcast_compare_fusion), kind=kOutput, calls=%fused_computation.243 | convolution fusion | flops 599962112 | bytes 39068480 | tf_op jit(solution)/shard_map/grhd,gshd->ghrs/dot_general | solution.py:499
  295.0 17.2 %fusion = f32[2,16,529]{2,1,0:T(8,128)S(1)} fusion(f32[2,16,529,529]{2,3,1,0:T(8,128)} %get-tuple-element.185, f32[2,16,529]{2,1,0:T(8,128)S(1)} %get-tuple-element.184), kind=kLoop, calls=%fused_computation.8 | loop fusion | flops 17892896 | bytes 35955072 | tf_op jit(solution)/shard_map/reduce_sum | solution.py:510
  312.2 19.0 %fusion.41 = bf16[2,16,32,529]{3,2,1,0:T(8,128)(2,1)} fusion(f32[2,16,529,529]{2,3,1,0:T(8,128)} %get-tuple-element.185, f32[2,16,529]{2,1,0:T(8,128)S(1)} %fusion, f32[2,16,529]{2,1,0:T(8,128)S(1)} %get-tuple-element.184, bf16[2,529,3,16,32]{1,4,3,2,0:T(8,128)(2,1)} %bitcast.285), kind=kOutput, calls=%fused_computation.132 | convolution fusion | flops 600520832 | bytes 46438656 | tf_op jit(solution)/shard_map/ghrs,gshd->grhd/dot_general | solution.py:513
  331.3 2.7 fusion.78
  334.5 4.3 fusion.32
  338.8 21.4 %multiply_convert_fusion.2 = (bf16[2,529,2048]{2,1,0:T(8,128)(2,1)S(1)}, f32[2,529,2048]{2,1,0:T(8,128)}) fusion(f32[2,529,2048]{2,1,0:T(8,128)S(1)} %get-tuple-element.188, u8[529,2048]{1,0:T(8,128)(4,1)S(1)} %get-tuple-element.130, u8[529,2048]{1,0:T(8,128)(4,1)S(1)} %get-tuple-element.129), kind=kLoop, calls=%fused_computation.44 | loop fusion | flops 151674880 | bytes 23834624 | tf_op jit(solution)/shard_map/convert_element_type | solution.py:560
  367.8 4.4 bitcast_convert_fusion.3
  372.2 8.7 %add_convert_fusion.1 = bf16[2,529,2048]{2,1,0:T(8,128)(2,1)} fusion(f32[2,529,2048]{2,1,0:T(8,128)} %get-tuple-element.155, f32[2,529,2048]{2,1,0:T(8,128)S(1)} %get-tuple-element.188, bf16[512,2048,1]{1,0,2:T(8,128)(2,1)S(1)} %bitcast.277, f32[2,529,512]{2,1,0:T(8,128)S(1)} %get-tuple-element.153, f32[2,529]{1,0:T(2,128)S(1)} %negate_multiply_fusion.4), kind=kOutput, calls=%fused_computation.43 | convolution fusion | flops 2250205184 | bytes 25936008 | tf_op jit(solution)/shard_map/grc,cw->grw/dot_general | solution.py:484
  380.9 5.1 fusion.69
  392.6 18.5 %fusion.33 = bf16[2,529,1,16,32]{1,4,3,0,2:T(8,128)(2,1)} fusion(bf16[2,529,16,32]{1,3,2,0:T(8,128)(2,1)} %bitcast.298, f32[2,16,529,529]{2,3,1,0:T(8,128)} %get-tuple-element.185, f32[2,16,529]{2,1,0:T(8,128)S(1)} %log_add_fusion), kind=kOutput, calls=%fused_computation.126 | convolution fusion | flops 591024192 | bytes 38054144 | tf_op jit(solution)/shard_map/ghrs,grhd->gshd/dot_general | solution.py:529
  411.1 34.7 %multiply_reduce_fusion = (f32[2,16,529]{2,1,0:T(8,128)S(1)}, f32[2,16,529,529]{2,3,1,0:T(8,128)}) fusion(f32[2,16,529,529]{2,3,1,0:T(8,128)} %get-tuple-element.185, f32[2,16,529]{2,1,0:T(8,128)S(1)} %log_add_fusion, bf16[2,529,16,32]{1,3,2,0:T(8,128)(2,1)} %bitcast.299, bf16[2,529,3,16,32]{1,4,3,2,0:T(8,128)(2,1)} %bitcast.286), kind=kOutput, calls=%fused_computation.3 | convolution fusion | flops 599962112 | bytes 82485632 | tf_op jit(solution)/shard_map/grhd,gshd->ghrs/dot_general | solution.py:528
  445.8 36.0 %multiply_convert_fusion = bf16[2,16,529,529]{2,3,1,0:T(8,128)(2,1)} fusion(f32[2,16,529,529]{2,3,1,0:T(8,128)} %get-tuple-element.193, f32[2,16,529,529]{2,3,1,0:T(8,128)} %get-tuple-element.185, f32[2,16,529]{2,1,0:T(8,128)S(1)} %get-tuple-element.192, f32[2,16,529]{2,1,0:T(8,128)S(1)} %log_add_fusion), kind=kLoop, calls=%fused_computation.2 | loop fusion | flops 35819648 | bytes 89684544 | tf_op jit(solution)/shard_map/convert_element_type | solution.py:536
  481.8 11.1 %multiply_bitcast_fusion = bf16[2,529,1,16,32]{1,4,3,0,2:T(8,128)(2,1)S(1)} fusion(bf16[2,16,529,529]{2,3,1,0:T(8,128)(2,1)} %multiply_convert_fusion, bf16[2,529,3,16,32]{1,4,3,2,0:T(8,128)(2,1)} %bitcast.287), kind=kOutput, calls=%fused_computation.81 | convolution fusion | flops 574197760 | bytes 24348672 | tf_op jit(solution)/shard_map/ghrs,grhd->gshd/dot_general | solution.py:543
  492.9 11.5 %multiply_bitcast_fusion.1 = bf16[2,529,1,16,32]{1,4,3,0,2:T(8,128)(2,1)S(1)} fusion(bf16[2,16,529,529]{2,3,1,0:T(8,128)(2,1)} %multiply_convert_fusion, bf16[2,529,3,16,32]{1,4,3,2,0:T(8,128)(2,1)} %bitcast.288), kind=kOutput, calls=%fused_computation.82 | convolution fusion | flops 574197760 | bytes 24348672 | tf_op jit(solution)/shard_map/ghrs,gshd->grhd/dot_general | solution.py:539
  511.2 2.8 select_reduce_fusion
  516.4 9.7 %scatter_custom_fusion = bf16[792,512]{1,0:T(8,128)(2,1)} fusion(s32[1058]{0:T(1024)} %reshape.651, bf16[1058,512]{1,0:T(8,128)(2,1)} %reshape.653, bf16[]{:T(256)} %constant.241.clone.1), kind=kCustom, calls=%fused_computation.156 | custom fusion | bytes 811520 | tf_op jit(solution)/shard_map/scatter | solution.py:641
  528.4 4.4 all-to-all-start.1
  532.9 3.2 fusion.48
  536.1 3.0 copy.98
  539.2 3.6 fusion.20
  542.8 7.3 bitcast_convert_fusion.4
  550.1 4.2 all-to-all-done.1
  556.3 13.0 %add_convert_fusion = bf16[8,99,3072]{2,1,0:T(8,128)(2,1)S(1)} fusion(f32[8,99,3072]{2,1,0:T(8,128)} %get-tuple-element.159, f32[8,99,3072]{2,1,0:T(8,128)} %copy-done.42, bf16[8,99,768]{2,1,0:T(8,128)(2,1)S(1)} %convolution_convert_fusion.3, bf16[768,3072,1]{1,0,2:T(8,128)(2,1)} %bitcast.270), kind=kOutput, calls=%fused_computation.21 | convolution fusion | flops 3771187200 | bytes 30265344 | tf_op jit(solution)/shard_map/grc,cw->grw/dot_general | solution.py:484
  569.5 4.7 multiply_reduce_fusion.2
  574.2 7.6 bitcast_convert_fusion.1
  581.8 7.0 bitcast_convert_fusion
  596.8 5.6 fusion.42
  602.4 4.7 multiply_reduce_fusion.1
  616.6 5.9 bitcast_convert_fusion.2
  622.4 3.5 multiply_reduce_fusion.4
  629.0 3.5 bitcast_convert_fusion.6
  632.4 117.6 %reduce_gradients.1 = (f32[32,128]{1,0:T(8,128)}, f32[144,384]{1,0:T(8,128)}, f32[48,384]{1,0:T(8,128)}, f32[192,384]{1,0:T(8,128)}, f32[96,768]{1,0:T(8,128)}, ...) custom-call(bf16[4,2,32,512]{3,2,1,0:T(8,128)(2,1)} %reshape.630.refs, ...), custom_call_target="tpu_custom_call" | custom-call | tf_op jit(solution)/shard_map/reduce_gradients/pallas_call | solution.py:337
  759.5 3.5 reshape.629
  (410 shorter events, 118.9 us)
Async XLA Ops:
  5.0 7.5 collective-permute-start
  144.1 16.7 %copy-start = (bf16[4,2,2,144,768]{4,3,2,1,0:T(8,128)(2,1)}, bf16[4,2,2,144,768]{4,3,2,1,0:T(8,128)(2,1)S(1)}, u32[]{:S(2)}) copy-start(bf16[4,2,2,144,768]{4,3,2,1,0:T(8,128)(2,1)S(1)} %get-tuple-element.82) | copy-start | bytes 10616836
  148.7 36.5 %copy-start.92 = (f32[768]{0:T(1024)}, f32[768]{0:T(1024)S(1)}, u32[]{:S(2)}) copy-start(f32[768]{0:T(1024)S(1)} %mul.442) | copy-start | bytes 9220
  149.5 17.7 %copy-start.58 = (f32[768]{0:T(1024)}, f32[768]{0:T(1024)S(1)}, u32[]{:S(2)}) copy-start(f32[768]{0:T(1024)S(1)} %mul.435) | copy-start | bytes 9220
  155.2 111.1 %copy-start.88 = (f32[1,512]{1,0:T(1,128)}, f32[1,512]{1,0:T(1,128)S(1)}, u32[]{:S(2)}) copy-start(f32[1,512]{1,0:T(1,128)S(1)} %get-tuple-element.171) | copy-start | bytes 6148
  155.2 176.0 %copy-start.74 = (f32[1,512]{1,0:T(1,128)}, f32[1,512]{1,0:T(1,128)S(1)}, u32[]{:S(2)}) copy-start(f32[1,512]{1,0:T(1,128)S(1)} %get-tuple-element.172) | copy-start | bytes 6148
  167.2 6.7 copy-start.110
  184.1 33.2 %copy-start.31 = (f32[8,99,768]{2,1,0:T(8,128)}, f32[8,99,768]{2,1,0:T(8,128)S(1)}, u32[]{:S(2)}) copy-start(f32[8,99,768]{2,1,0:T(8,128)S(1)} %get-tuple-element.182) | copy-start | bytes 7299076
  184.2 8.7 %copy-start.80 = (f32[8,99]{1,0:T(8,128)}, f32[8,99]{1,0:T(8,128)S(1)}, u32[]{:S(2)}) copy-start(f32[8,99]{1,0:T(8,128)S(1)} %broadcast_multiply_fusion.3) | copy-start | bytes 9508
  184.2 33.1 %slice-start.4 = ((s8[4718592]{0:T(1024)(128)(4,1)}), s8[4194304]{0:T(1024)(128)(4,1)S(1)}, s32[]{:S(2)}) async-start(s8[4718592]{0:T(1024)(128)(4,1)} %bitcast.271), calls=%async_computation.6 | async-start | bytes 8388608
  184.7 8.3 %copy-start.94 = (f32[8,99]{1,0:T(8,128)}, f32[8,99]{1,0:T(8,128)S(1)}, u32[]{:S(2)}) copy-start(f32[8,99]{1,0:T(8,128)S(1)} %fusion.61) | copy-start | bytes 9508
  186.4 31.0 %slice-start.5 = ((s8[4718592]{0:T(1024)(128)(4,1)}), s8[524288]{0:T(1024)(128)(4,1)S(1)}, s32[]{:S(2)}) async-start(s8[4718592]{0:T(1024)(128)(4,1)} %bitcast.271), calls=%async_computation.7 | async-start | bytes 1048576
  192.9 24.4 %copy-start.42 = (f32[8,99,3072]{2,1,0:T(8,128)}, f32[8,99,3072]{2,1,0:T(8,128)S(1)}, u32[]{:S(2)}) copy-start(f32[8,99,3072]{2,1,0:T(8,128)S(1)} %get-tuple-element.183) | copy-start | bytes 29196292
  217.4 7.9 %copy-start.24 = (bf16[4,2,2,32,768]{4,3,2,1,0:T(8,128)(2,1)S(1)}, bf16[4,2,2,32,768]{4,3,2,1,0:T(8,128)(2,1)}, u32[]{:S(2)}) copy-start(bf16[4,2,2,32,768]{4,3,2,1,0:T(8,128)(2,1)} %copy-done.23) | copy-start | bytes 2359300
  217.4 7.8 %copy-start.106 = (f32[1,512]{1,0:T(1,128)S(1)}, f32[1,512]{1,0:T(1,128)}, u32[]{:S(2)}) copy-start(f32[1,512]{1,0:T(1,128)} %get-tuple-element.173) | copy-start | bytes 6148
  225.2 9.5 %copy-start.69 = (f32[792]{0:T(1024)S(1)}, f32[792]{0:T(1024)}, u32[]{:S(2)}) copy-start(f32[792]{0:T(1024)} %copy-done.68) | copy-start | bytes 9508
  225.2 10.2 %copy-start.39 = (f32[2,529,512]{2,0,1:T(2,128)S(1)}, f32[2,529,512]{2,0,1:T(2,128)}, u32[]{:S(2)}) copy-start(f32[2,529,512]{2,0,1:T(2,128)} %param.28) | copy-start | bytes 6500356
  227.0 9.6 %copy-start.96 = (f32[792]{0:T(1024)S(1)}, f32[792]{0:T(1024)}, u32[]{:S(2)}) copy-start(f32[792]{0:T(1024)} %get-tuple-element.177) | copy-start | bytes 9508
  227.0 10.3 %copy-start.86 = (s32[2,529]{1,0:T(2,128)S(1)}, s32[2,529]{1,0:T(2,128)}, u32[]{:S(2)}) copy-start(s32[2,529]{1,0:T(2,128)} %param.27) | copy-start | bytes 12700
  227.0 11.1 %copy-start.87 = (s32[2,529]{1,0:T(2,128)S(1)}, s32[2,529]{1,0:T(2,128)}, u32[]{:S(2)}) copy-start(s32[2,529]{1,0:T(2,128)} %param.26) | copy-start | bytes 12700
  227.1 29.9 %all-to-all-start = ((bf16[8,99,512]{2,1,0:T(8,128)(2,1)}), bf16[8,99,512]{2,1,0:T(8,128)(2,1)}, u32[]{:S(2)}, u32[]{:S(2)}) async-start(bf16[8,99,512]{2,1,0:T(8,128)(2,1)} %add_convert_fusion.8), calls=%async_computation | async-start | bytes 1703936 | tf_op jit(solution)/shard_map/all_to_all | solution.py:624
  238.0 93.2 %copy-start.70 = (pred[2,529]{1,0:T(4,128)(4,1)}, pred[2,529]{1,0:T(4,128)(4,1)S(1)}, u32[]{:S(2)}) copy-start(pred[2,529]{1,0:T(4,128)(4,1)S(1)} %get-tuple-element.156) | copy-start | bytes 3178
  238.0 93.2 %copy-start.72 = (pred[2,529]{1,0:T(4,128)(4,1)}, pred[2,529]{1,0:T(4,128)(4,1)S(1)}, u32[]{:S(2)}) copy-start(pred[2,529]{1,0:T(4,128)(4,1)S(1)} %get-tuple-element.174) | copy-start | bytes 3178
  264.5 66.7 %copy-start.29 = (bf16[2,529,512]{2,1,0:T(8,128)(2,1)}, bf16[2,529,512]{2,1,0:T(8,128)(2,1)S(1)}, u32[]{:S(2)}) copy-start(bf16[2,529,512]{2,1,0:T(8,128)(2,1)S(1)} %reshape.642) | copy-start | bytes 3250180
  312.2 19.0 %copy-start.7 = (bf16[4,2,64,512]{3,2,1,0:T(8,128)(2,1)S(1)}, bf16[4,2,64,512]{3,2,1,0:T(8,128)(2,1)}, u32[]{:S(2)}) copy-start(bf16[4,2,64,512]{3,2,1,0:T(8,128)(2,1)} %copy-done.6) | copy-start | bytes 1572868
  334.0 53.3 %copy-start.37 = (f32[2,529,512]{2,1,0:T(8,128)}, f32[2,529,512]{2,1,0:T(8,128)S(1)}, u32[]{:S(2)}) copy-start(f32[2,529,512]{2,1,0:T(8,128)S(1)} %get-tuple-element.187) | copy-start | bytes 6500356
  338.8 21.4 %copy-start.19 = (bf16[4,2,64,2048]{3,2,1,0:T(8,128)(2,1)S(1)}, bf16[4,2,64,2048]{3,2,1,0:T(8,128)(2,1)}, u32[]{:S(2)}) copy-start(bf16[4,2,64,2048]{3,2,1,0:T(8,128)(2,1)} %copy-done.18) | copy-start | bytes 6291460
  492.9 11.5 %copy-start.46 = (bf16[2,529,1,16,32]{1,4,3,0,2:T(8,128)(2,1)S(1)}, bf16[2,529,1,16,32]{1,4,3,0,2:T(8,128)(2,1)}, u32[]{:S(2)}) copy-start(bf16[2,529,1,16,32]{1,4,3,0,2:T(8,128)(2,1)} %fusion.33) | copy-start | bytes 3250180
  528.4 25.9 %all-to-all-start.1 = ((bf16[8,99,512]{2,1,0:T(8,128)(2,1)}), bf16[8,99,512]{2,1,0:T(8,128)(2,1)}, u32[]{:S(2)}, u32[]{:S(2)}) async-start(bf16[8,99,512]{2,1,0:T(8,128)(2,1)} %reshape.627), calls=%async_computation.1 | async-start | bytes 1703936 | tf_op jit(solution)/shard_map/all_to_all | solution.py:643
  542.8 11.5 %copy-start.25 = (bf16[4,2,2,32,768]{4,3,2,1,0:T(8,128)(2,1)S(1)}, bf16[4,2,2,32,768]{4,3,2,1,0:T(8,128)(2,1)}, u32[]{:S(2)}) copy-start(bf16[4,2,2,32,768]{4,3,2,1,0:T(8,128)(2,1)} %copy-done.23) | copy-start | bytes 2359300
  542.8 26.6 %slice-start.2 = ((s8[4718592]{0:T(1024)(128)(4,1)}), s8[524288]{0:T(1024)(128)(4,1)S(1)}, s32[]{:S(2)}) async-start(s8[4718592]{0:T(1024)(128)(4,1)} %bitcast.267), calls=%async_computation.4 | async-start | bytes 1048576
  556.3 33.5 %copy-start.47 = (bf16[8,99,768]{2,1,0:T(8,128)(2,1)}, bf16[8,99,768]{2,1,0:T(8,128)(2,1)S(1)}, u32[]{:S(2)}) copy-start(bf16[8,99,768]{2,1,0:T(8,128)(2,1)S(1)} %convolution_convert_fusion.3) | copy-start | bytes 3649540
  556.3 13.1 %slice-start.3 = ((s8[4718592]{0:T(1024)(128)(4,1)}), s8[4194304]{0:T(1024)(128)(4,1)S(1)}, s32[]{:S(2)}) async-start(s8[4718592]{0:T(1024)(128)(4,1)} %bitcast.267), calls=%async_computation.5 | async-start | bytes 8388608
  556.3 13.1 %copy-start.32 = (f32[8,99,768]{2,1,0:T(8,128)S(1)}, f32[8,99,768]{2,1,0:T(8,128)}, u32[]{:S(2)}) copy-start(f32[8,99,768]{2,1,0:T(8,128)} %copy-done.31) | copy-start | bytes 7299076
  556.3 13.1 %copy-start.81 = (f32[8,99]{1,0:T(8,128)S(1)}, f32[8,99]{1,0:T(8,128)}, u32[]{:S(2)}) copy-start(f32[8,99]{1,0:T(8,128)} %copy-done.80) | copy-start | bytes 9508
  556.3 13.1 %copy-start.93 = (f32[768]{0:T(1024)S(1)}, f32[768]{0:T(1024)}, u32[]{:S(2)}) copy-start(f32[768]{0:T(1024)} %copy-done.92) | copy-start | bytes 9220
  556.3 13.1 %copy-start.95 = (f32[8,99]{1,0:T(8,128)S(1)}, f32[8,99]{1,0:T(8,128)}, u32[]{:S(2)}) copy-start(f32[8,99]{1,0:T(8,128)} %copy-done.94) | copy-start | bytes 9508
  569.5 12.3 %slice-start.10 = ((s8[5111808]{0:T(1024)(128)(4,1)}), s8[4194304]{0:T(1024)(128)(4,1)S(1)}, s32[]{:S(2)}) async-start(s8[5111808]{0:T(1024)(128)(4,1)} %bitcast.302), calls=%async_computation.12 | async-start | bytes 8388608
  574.2 7.6 slice-start.11
  581.7 7.0 copy-start.83
  596.8 10.3 %slice-start.6 = ((s8[5111808]{0:T(1024)(128)(4,1)}), s8[4194304]{0:T(1024)(128)(4,1)S(1)}, s32[]{:S(2)}) async-start(s8[5111808]{0:T(1024)(128)(4,1)} %bitcast.282), calls=%async_computation.8 | async-start | bytes 8388608
  596.8 11.5 %slice-start.8 = ((s8[4718592]{0:T(1024)(128)(4,1)}), s8[4194304]{0:T(1024)(128)(4,1)S(1)}, s32[]{:S(2)}) async-start(s8[4718592]{0:T(1024)(128)(4,1)} %bitcast.294), calls=%async_computation.10 | async-start | bytes 8388608
  602.4 5.9 slice-start.9
  616.5 5.9 copy-start.1
  632.4 124.8 %copy-start.36 = (f32[8,99,768]{2,1,0:T(8,128)S(1)}, f32[8,99,768]{2,1,0:T(8,128)}, u32[]{:S(2)}) copy-start(f32[8,99,768]{2,1,0:T(8,128)} %copy-done.35) | copy-start | bytes 7299076
  632.4 124.8 %copy-start.48 = (bf16[8,99,768]{2,1,0:T(8,128)(2,1)S(1)}, bf16[8,99,768]{2,1,0:T(8,128)(2,1)}, u32[]{:S(2)}) copy-start(bf16[8,99,768]{2,1,0:T(8,128)(2,1)} %copy-done.47) | copy-start | bytes 3649540
  750.1 7.2 copy-start.34
  757.3 6.5 collective-permute-start.1
  (80 other events, 212.5 us)

commit v2 on v1

--- a/solution.py
+++ b/solution.py
@@ -14,9 +14,22 @@
 
 EPSILON = 1e-06
 NEGATIVE = -1000000000.0
+LANES = 128
 MESH = pl.DeviceIdType.MESH
 BF16 = jnp.bfloat16
 F32 = jnp.float32
+
+
+def in_blocks(value, dim, length):
+    dims = value.shape
+    pieces = value.reshape(*dims[:dim], length, dims[dim] // length, *dims[dim + 1 :])
+    return jnp.moveaxis(pieces, dim, 0)
+
+
+def sum_at_owner(value, axis, dim):
+    length = lax.axis_size(axis)
+    pieces = lax.all_to_all(in_blocks(value, dim, length), axis, 0, 0, tiled=True)
+    return jnp.sum(pieces.astype(jnp.float32), axis=0)
 
 
 @dataclasses.dataclass(frozen=True)
@@ -453,136 +466,587 @@
     )
 
 
-def in_blocks(value, dim, length):
-    dims = value.shape
-    pieces = value.reshape(*dims[:dim], length, dims[dim] // length, *dims[dim + 1 :])
-    return jnp.moveaxis(pieces, dim, 0)
-
-
-def sum_at_owner(value, axis, dim):
-    length = lax.axis_size(axis)
-    pieces = lax.all_to_all(in_blocks(value, dim, length), axis, 0, 0, tiled=True)
-    return jnp.sum(pieces.astype(jnp.float32), axis=0)
-
-
-def layer_norm(values, scale_gain, norm_shift):
-    row_mean = jnp.mean(values, axis=-1, keepdims=True)
-    centred = values - row_mean
-    spread = jnp.mean(centred * centred, axis=-1, keepdims=True)
-    return centred * lax.rsqrt(spread + EPSILON) * scale_gain + norm_shift
-
-
-def gelu_exact(values):
-    return jax.nn.gelu(values, approximate=False)
-
-
-def project(left_side, right_side):
-    return jnp.einsum("grw,cw->grc", left_side, right_side, preferred_element_type=jnp.float32)
-
-
-def project_back(gradient, right_side):
-    return jnp.einsum("grc,cw->grw", gradient, right_side, preferred_element_type=jnp.float32)
-
-
-def outer_sum(left_side, gradient):
-    return jnp.einsum("grc,grw->cw", gradient, left_side, preferred_element_type=jnp.float32)
-
-
-def split_heads(joined_qkv, head_count):
-    groups, row_count, triple = joined_qkv.shape
-    head_size = triple // 3 // head_count
-    pieces = joined_qkv.reshape(groups, row_count, 3, head_count, head_size)
-    return (pieces[:, :, 0], pieces[:, :, 1], pieces[:, :, 2], head_size)
-
-
-def scores_of(queries, key_part, allowed, head_size):
-    raw_scores = jnp.einsum(
-        "grhd,gshd->ghrs", queries, key_part, preferred_element_type=jnp.float32
-    ) * head_size ** (-0.5)
-    return jnp.where(allowed[:, None], raw_scores, NEGATIVE)
-
-
-def attend(joined_qkv, allowed, head_count):
-    queries, key_part, values, head_size = split_heads(joined_qkv, head_count)
-    scores = scores_of(queries, key_part, allowed, head_size)
-    row_max = jnp.max(scores, axis=-1, keepdims=True)
-    weights = jnp.exp(scores - row_max)
-    row_total = jnp.sum(weights, axis=-1, keepdims=True)
-    probability = weights / row_total
-    log_total = row_max + jnp.log(row_total)
-    mixture = jnp.einsum(
-        "ghrs,gshd->grhd",
-        probability.astype(jnp.bfloat16),
-        values,
-        preferred_element_type=jnp.float32,
+def nn(a, b):
+    return lax.dot_general(a, b, (((1,), (0,)), ((), ())), preferred_element_type=F32)
+
+
+def nt(a, b):
+    return lax.dot_general(a, b, (((1,), (1,)), ((), ())), preferred_element_type=F32)
+
+
+def tn(a, b):
+    return lax.dot_general(a, b, (((0,), (0,)), ((), ())), preferred_element_type=F32)
+
+
+def unit(values):
+    centred = values - jnp.mean(values, axis=-1, keepdims=True)
+    scale = lax.rsqrt(jnp.mean(centred * centred, axis=-1, keepdims=True) + EPSILON)
+    return centred * scale, scale
+
+
+def unit_back(d_hat, hat, scale):
+    along = jnp.mean(d_hat * hat, axis=-1, keepdims=True)
+    return scale * (d_hat - jnp.mean(d_hat, axis=-1, keepdims=True) - hat * along)
+
+
+def column_sum(values):
+    return jnp.sum(values, axis=0, keepdims=True)
+
+
+def gelu_pair(u):
+    phi = 0.5 + 0.5 * lax.erf(u * 0.7071067811865476)
+    return u * phi, phi + u * (0.3989422804014327 * jnp.exp(-0.5 * u * u))
+
+
+def head_lanes(shape, head_size, h):
+    return lax.broadcasted_iota(jnp.int32, shape, 1) // head_size == h
+
+
+def pick(values, head_size, h):
+    return jnp.where(head_lanes(values.shape, head_size, h), values, jnp.zeros_like(values))
+
+
+def attend_tile(q, k, v, bias, head_size):
+    v_t = v.astype(F32).T.astype(BF16)
+    mixed, totals = [], []
+    for h in range(LANES // head_size):
+        scores = nt(pick(k, head_size, h), q) * head_size**-0.5 + bias
+        top = jnp.max(scores, axis=0, keepdims=True)
+        weight = jnp.exp(scores - top)
+        total = jnp.sum(weight, axis=0, keepdims=True)
+        part = nn(v_t[h * head_size : (h + 1) * head_size], weight.astype(BF16))
+        mixed.append(part * (1.0 / total))
+        totals.append(top + jnp.log(total))
+    return jnp.concatenate(mixed, axis=0).T, totals
+
+
+def attend_tile_back(q, k, v, d_mixed, bias, totals, head_size):
+    k_t = k.astype(F32).T.astype(BF16)
+    d_q, d_k, d_v = [], 0.0, 0.0
+    for h in range(LANES // head_size):
+        scores = nt(pick(k, head_size, h), q) * head_size**-0.5 + bias
+        prob = jnp.exp(scores - totals[h])
+        d_prob = nt(pick(v, head_size, h), d_mixed)
+        centre = jnp.sum(d_prob * prob, axis=0, keepdims=True)
+        d_score = (prob * (d_prob - centre)).astype(BF16)
+        d_v = d_v + nn(prob.astype(BF16), pick(d_mixed, head_size, h))
+        d_k = d_k + nn(d_score, pick(q, head_size, h))
+        d_q.append(nn(k_t[h * head_size : (h + 1) * head_size], d_score))
+    d_q = jnp.concatenate(d_q, axis=0).T
+    return d_q * head_size**-0.5, d_k * head_size**-0.5, d_v
+
+
+def lane_tile(t):
+    return pl.ds(pl.multiple_of(t * LANES, LANES), LANES)
+
+
+def rows_of(i, n):
+    return pl.ds(pl.multiple_of(i * n, 16), n)
+
+
+def mask_bias(own, keys):
+    return jnp.where(keys == own, 0.0, NEGATIVE).astype(F32)
+
+
+def outer_loop(count, body):
+    def step(i, carry):
+        body(i)
+        return carry
+
+    lax.fori_loop(0, count, step, 0)
+
+
+def weight_sum(dst, left, right, stage, sem):
+    _, tile, width = stage.shape
+    count = left.shape[1] // tile
+
+    def off(t):
+        slot = lax.rem(t, 2)
+        rows = pl.ds(pl.multiple_of(t * tile, LANES), tile)
+        return pltpu.make_async_copy(stage.at[slot], dst.at[rows, :], sem.at[slot])
+
+    def one(t):
+        @pl.when(t >= 2)
+        def _():
+            off(t - 2).wait()
+
+        cols = pl.ds(pl.multiple_of(t * tile, LANES), tile)
+        stage[lax.rem(t, 2)] = tn(left[:, cols], right[...]).astype(BF16)
+        off(t).start()
+
+    outer_loop(count, one)
+    for t in range(max(0, count - 2), count):
+        off(t).wait()
+
+
+def decoder_kernel(
+    head_size,
+    chunk,
+    table,
+    index_col,
+    index_row,
+    seg_col,
+    seg_row,
+    cot,
+    norms,
+    w_qkv,
+    w_out,
+    w_up,
+    w_down,
+    decoded,
+    d_table,
+    g_norms,
+    g_qkv,
+    g_out,
+    g_up,
+    g_down,
+    x,
+    h_one,
+    qkv,
+    mixed,
+    totals,
+    h_two,
+    act,
+    slope,
+    d_up,
+    e_two,
+    e_one,
+    bias,
+    stage,
+    stage_wide,
+    sem,
+):
+    groups, n, width = cot.shape
+    real = decoded.shape[1]
+    rows = groups * n
+    per_group = n // chunk
+    tiles = width // LANES
+    per_tile = LANES // head_size
+    gain = [norms[k : k + 1, :].astype(F32) for k in range(8)]
+    g_norms[...] = jnp.zeros_like(g_norms)
+    d_x = cot
+
+    def start(i):
+        r = rows_of(i, chunk)
+        slots = lax.broadcasted_iota(jnp.int32, (chunk, table.shape[0]), 1)
+        named = index_col[r, :]
+        chosen = jnp.where(slots == named, 1.0, 0.0).astype(BF16)
+        picked = nn(chosen, table[...])
+        begin = jnp.where(named >= 0, picked, gain[6])
+        x[r, :] = begin
+        hat, _ = unit(begin)
+        h = (hat * gain[0] + gain[1]).astype(BF16)
+        h_one[r, :] = h
+        qkv[r, :] = nt(h, w_qkv[...]).astype(BF16)
+
+    outer_loop(rows // chunk, start)
+
+    def attend(g):
+        bias[...] = mask_bias(seg_row[g], seg_col[rows_of(g, n), :])
+        r = rows_of(g, n)
+
+        def one(t):
+            q, k, v = [qkv[r, lane_tile(t + j * tiles)] for j in range(3)]
+            out, logs = attend_tile(q, k, v, bias[...], head_size)
+            mixed[r, lane_tile(t)] = out.astype(BF16)
+            for h in range(per_tile):
+                totals[g * tiles + t, h : h + 1, :] = logs[h]
+
+        outer_loop(tiles, one)
+
+    outer_loop(groups, attend)
+
+    def middle(i):
+        g, j = i // per_group, lax.rem(i, per_group)
+        r = rows_of(i, chunk)
+        one = x[r, :] + nt(mixed[r, :], w_out[...])
+        hat_two, scale_two = unit(one)
+        h = (hat_two * gain[2] + gain[3]).astype(BF16)
+        h_two[r, :] = h
+        step = 512
+        for t in range(w_up.shape[0] // step):
+            u = nt(h, w_up[t * step : (t + 1) * step, :])
+            a, s = gelu_pair(u)
+            act[r, t * step : (t + 1) * step] = a.astype(BF16)
+            slope[:, t * step : (t + 1) * step] = s.astype(BF16)
+        two = one + nt(act[r, :], w_down[...])
+        hat, scale = unit(two)
+        result = hat * gain[4] + gain[5]
+        for b in range(groups):
+            for c in range(per_group):
+                lo = c * chunk
+                hi = min(lo + chunk, real)
+
+                @pl.when(i == b * per_group + c)
+                def _(b=b, lo=lo, hi=hi):
+                    decoded[b, lo:hi, :] = result[: hi - lo]
+
+        cr = rows_of(j, chunk)
+        d = cot[g, cr, :]
+        g_norms[4:5, :] += column_sum(d * hat)
+        g_norms[5:6, :] += column_sum(d)
+        d_two = unit_back(d * gain[4], hat, scale)
+        e = d_two.astype(BF16)
+        e_two[r, :] = e
+        for t in range(w_up.shape[0] // step):
+            cols = slice(t * step, (t + 1) * step)
+            d_act = nn(e, w_down[:, cols])
+            d_up[r, cols] = (d_act * slope[:, cols].astype(F32)).astype(BF16)
+        d_h = nn(d_up[r, :], w_up[...])
+        g_norms[2:3, :] += column_sum(d_h * hat_two)
+        g_norms[3:4, :] += column_sum(d_h)
+        d_one = d_two + unit_back(d_h * gain[2], hat_two, scale_two)
+        d_x[g, cr, :] = d_one
+        e_one[r, :] = d_one.astype(BF16)
+
+    outer_loop(rows // chunk, middle)
+
+    weight_sum(g_down, e_two, act, stage_wide, sem)
+    weight_sum(g_up, d_up, h_two, stage, sem)
+    weight_sum(g_out, e_one, mixed, stage, sem)
+
+    def mix_back(i):
+        r = rows_of(i, chunk)
+        mixed[r, :] = nn(e_one[r, :], w_out[...]).astype(BF16)
+
+    outer_loop(rows // chunk, mix_back)
+    d_qkv = act
+
+    def attend_back(g):
+        bias[...] = mask_bias(seg_row[g], seg_col[rows_of(g, n), :])
+        r = rows_of(g, n)
+
+        def one(t):
+            q, k, v = [qkv[r, lane_tile(t + j * tiles)] for j in range(3)]
+            logs = [totals[g * tiles + t, h : h + 1, :] for h in range(per_tile)]
+            found = attend_tile_back(q, k, v, mixed[r, lane_tile(t)], bias[...], logs, head_size)
+            for j in range(3):
+                d_qkv[r, lane_tile(t + j * tiles)] = found[j].astype(BF16)
+
+        outer_loop(tiles, one)
+
+    outer_loop(groups, attend_back)
+
+    weight_sum(g_qkv, d_qkv.at[:, : 3 * width], h_one, stage, sem)
+
+    def finish(i):
+        g, j = i // per_group, lax.rem(i, per_group)
+        r, cr = rows_of(i, chunk), rows_of(j, chunk)
+        d_h = nn(d_qkv[r, : 3 * width], w_qkv[...])
+        hat, scale = unit(x[r, :])
+        g_norms[0:1, :] += column_sum(d_h * hat)
+        g_norms[1:2, :] += column_sum(d_h)
+        d_start = d_x[g, cr, :] + unit_back(d_h * gain[0], hat, scale)
+        seen = index_col[r, :] >= 0
+        g_norms[6:7, :] += column_sum(jnp.where(seen, 0.0, d_start))
+        e_two[r, :] = jnp.where(seen, d_start, 0.0).astype(BF16)
+
+    outer_loop(rows // chunk, finish)
+
+    def back(s):
+        sr = rows_of(s, 128)
+        slots = lax.broadcasted_iota(jnp.int32, (128, rows), 0) + s * 128
+        chosen = jnp.where(slots == index_row[...], 1.0, 0.0).astype(BF16)
+        d_table[sr, :] = nn(chosen, e_two[...]).astype(BF16)
+
+    outer_loop(table.shape[0] // 128, back)
+
+
+def decoder(table, index, segment, cotangent, norms, weights, heads):
+    groups, real, width = cotangent.shape
+    n = -(-real // 32) * 32
+    chunk = n // 2
+    rows = groups * n
+    head_size = width // heads
+    pad = n - real
+    index = jnp.pad(index, ((0, 0), (0, pad)), constant_values=-1).reshape(rows)
+    segment = jnp.pad(segment, ((0, 0), (0, pad)), constant_values=-1)
+    cot = jnp.pad(cotangent, ((0, 0), (0, pad), (0, 0)))
+    tiles = width // LANES
+    ff = weights[2].shape[0]
+    vm = pl.BlockSpec(memory_space=pltpu.VMEM)
+    return pl.pallas_call(
+        functools.partial(decoder_kernel, head_size, chunk),
+        out_shape=[
+            jax.ShapeDtypeStruct(cotangent.shape, F32),
+            jax.ShapeDtypeStruct(table.shape, BF16),
+            jax.ShapeDtypeStruct((8, width), F32),
+        ]
+        + [jax.ShapeDtypeStruct(w.shape, BF16) for w in weights],
+        in_specs=[vm] * 11,
+        out_specs=[vm] * 3 + [pl.BlockSpec(memory_space=pl.ANY)] * 4,
+        scratch_shapes=[
+            pltpu.VMEM((rows, width), F32),
+            pltpu.VMEM((rows, width), BF16),
+            pltpu.VMEM((rows, 3 * width), BF16),
+            pltpu.VMEM((rows, width), BF16),
+            pltpu.VMEM((groups * tiles, LANES // head_size, n), F32),
+            pltpu.VMEM((rows, width), BF16),
+            pltpu.VMEM((rows, ff), BF16),
+            pltpu.VMEM((chunk, ff), BF16),
+            pltpu.VMEM((rows, ff), BF16),
+            pltpu.VMEM((rows, width), BF16),
+            pltpu.VMEM((rows, width), BF16),
+            pltpu.VMEM((n, n), F32),
+            pltpu.VMEM((2, 256, width), BF16),
+            pltpu.VMEM((2, LANES, ff), BF16),
+            pltpu.SemaphoreType.DMA((2,)),
+        ],
+        compiler_params=pltpu.CompilerParams(vmem_limit_bytes=60 << 20),
+        name="decoder",
+    )(
+        table,
+        index[:, None],
+        index[None, :],
+        segment.reshape(rows, 1),
+        segment[:, None, :],
+        cot,
+        norms,
+        *weights,
     )
-    return (mixture.reshape(joined_qkv.shape[0], joined_qkv.shape[1], -1), log_total)
-
-
-def attend_back(joined_qkv, allowed, head_count, log_total, d_mixed):
-    queries, key_part, values, head_size = split_heads(joined_qkv, head_count)
-    scores = scores_of(queries, key_part, allowed, head_size)
-    probability = jnp.exp(scores - log_total)
-    groups, row_count = (d_mixed.shape[0], d_mixed.shape[1])
-    d_heads = d_mixed.reshape(groups, row_count, head_count, head_size)
-    d_probs = jnp.einsum("grhd,gshd->ghrs", d_heads, values, preferred_element_type=jnp.float32)
-    d_value = jnp.einsum(
-        "ghrs,grhd->gshd",
-        probability.astype(jnp.bfloat16),
-        d_heads,
-        preferred_element_type=jnp.float32,
-    )
-    centre = jnp.sum(d_probs * probability, axis=-1, keepdims=True)
-    d_scores = (probability * (d_probs - centre)).astype(jnp.bfloat16)
-    score_scale = head_size ** (-0.5)
-    d_query = (
-        jnp.einsum("ghrs,gshd->grhd", d_scores, key_part, preferred_element_type=jnp.float32)
-        * score_scale
-    )
-    d_key = (
-        jnp.einsum("ghrs,grhd->gshd", d_scores, queries, preferred_element_type=jnp.float32)
-        * score_scale
-    )
-    stacked = jnp.stack([d_query, d_key, d_value], axis=2)
-    return stacked.reshape(groups, row_count, -1).astype(jnp.bfloat16)
-
-
-def block_forward(inputs, params, allowed, head_count):
-    norm_rows, w_qkv, w_out, w_up, w_down = params
-    gain_rows = norm_rows.astype(jnp.float32)
-    h_one = layer_norm(inputs, gain_rows[0], gain_rows[1]).astype(jnp.bfloat16)
-    joined_qkv = project(h_one, w_qkv).astype(jnp.bfloat16)
-    mixture, log_total = attend(joined_qkv, allowed, head_count)
-    mixture = mixture.astype(jnp.bfloat16)
-    x_one = inputs + project(mixture, w_out)
-    h_two = layer_norm(x_one, gain_rows[2], gain_rows[3]).astype(jnp.bfloat16)
-    up_proj = project(h_two, w_up)
-    activated = gelu_exact(up_proj).astype(jnp.bfloat16)
-    x_two = x_one + project(activated, w_down)
-    return (x_two, (joined_qkv, log_total, mixture, x_one, up_proj))
-
-
-def block_backward(inputs, params, allowed, head_count, stored, d_two):
-    norm_rows, w_qkv, w_out, w_up, w_down = params
-    gain_rows = norm_rows.astype(jnp.float32)
-    joined_qkv, log_total, mixture, x_one, up_proj = stored
-    d_branch = d_two.astype(jnp.bfloat16)
-    activated, gelu_pull = jax.vjp(gelu_exact, up_proj)
-    g_down = outer_sum(activated.astype(jnp.bfloat16), d_branch)
-    d_up = gelu_pull(project_back(d_branch, w_down))[0].astype(jnp.bfloat16)
-    h_two, norm_two_pull = jax.vjp(layer_norm, x_one, gain_rows[2], gain_rows[3])
-    g_up = outer_sum(h_two.astype(jnp.bfloat16), d_up)
-    d_x_two_norm, d_gain_two, d_shift_two = norm_two_pull(project_back(d_up, w_up))
-    d_one = d_two + d_x_two_norm
-    d_attn = d_one.astype(jnp.bfloat16)
-    g_out = outer_sum(mixture, d_attn)
-    d_mixed = project_back(d_attn, w_out).astype(jnp.bfloat16)
-    d_qkv = attend_back(joined_qkv, allowed, head_count, log_total, d_mixed)
-    h_one, norm_one_pull = jax.vjp(layer_norm, inputs, gain_rows[0], gain_rows[1])
-    g_qkv = outer_sum(h_one.astype(jnp.bfloat16), d_qkv)
-    d_x_one_norm, d_gain_one, d_shift_one = norm_one_pull(project_back(d_qkv, w_qkv))
-    g_norms = jnp.stack([d_gain_one, d_shift_one, d_gain_two, d_shift_two])
-    return (d_one + d_x_one_norm, (g_norms, g_qkv, g_out, g_up, g_down))
+
+
+def encoder_kernel(
+    head_size,
+    groups,
+    chunk,
+    patches,
+    key_col,
+    own_row,
+    norms,
+    shift,
+    w_qkv,
+    w_out,
+    w_up,
+    w_down,
+    w_embed,
+    embedded,
+    qkv,
+    totals,
+    mixed,
+    x_one,
+    act,
+    slope,
+    sent,
+):
+    rows, width = patches.shape
+    n = rows // groups
+    tiles = width // LANES
+    per_tile = LANES // head_size
+    gain = [norms[k : k + 1, :].astype(F32) for k in range(4)]
+    add = shift[7:8, :].astype(F32)
+
+    def start(i):
+        r = rows_of(i, chunk)
+        hat, _ = unit(patches[r, :].astype(F32))
+        qkv[r, :] = nt((hat * gain[0] + gain[1]).astype(BF16), w_qkv[...]).astype(BF16)
+
+    outer_loop(rows // chunk, start)
+
+    def attend(g):
+        r = rows_of(g, n)
+        bias = mask_bias(own_row[g], key_col[r, :])
+        for t in range(tiles):
+            q, k, v = [qkv[r, (t + j * tiles) * LANES : (t + j * tiles + 1) * LANES] for j in range(3)]
+            out, logs = attend_tile(q, k, v, bias, head_size)
+            mixed[r, t * LANES : (t + 1) * LANES] = out.astype(BF16)
+            for h in range(per_tile):
+                totals[g, t * per_tile + h : t * per_tile + h + 1, :] = logs[h]
+
+    outer_loop(groups, attend)
+
+    def middle(i):
+        r = rows_of(i, chunk)
+        one = patches[r, :].astype(F32) + nt(mixed[r, :], w_out[...])
+        x_one[r, :] = one
+        hat, _ = unit(one)
+        h = (hat * gain[2] + gain[3]).astype(BF16)
+        step = 512
+        for t in range(w_up.shape[0] // step):
+            u = nt(h, w_up[t * step : (t + 1) * step, :])
+            a, s = gelu_pair(u)
+            act[r, t * step : (t + 1) * step] = a.astype(BF16)
+            slope[r, t * step : (t + 1) * step] = s.astype(BF16)
+        two = (one + nt(act[r, :], w_down[...])).astype(BF16)
+        sent[r, :] = two
+        embedded[r, :] = (nt(two, w_embed[...]) + add).astype(BF16)
+
+    outer_loop(rows // chunk, middle)
+
+
+def encoder_back_kernel(
+    head_size,
+    groups,
+    chunk,
+    patches,
+    key_col,
+    own_row,
+    norms,
+    w_qkv,
+    w_out,
+    w_up,
+    w_down,
+    w_embed,
+    d_table,
+    qkv,
+    totals,
+    mixed,
+    x_one,
+    act,
+    slope,
+    sent,
+    d_patches,
+    g_norms,
+    g_shift,
+    g_qkv,
+    g_out,
+    g_up,
+    g_down,
+    g_embed,
+    e_two,
+    e_one,
+    stage,
+    stage_wide,
+    sem,
+):
+    rows, width = patches.shape
+    n = rows // groups
+    tiles = width // LANES
+    per_tile = LANES // head_size
+    gain = [norms[k : k + 1, :].astype(F32) for k in range(4)]
+    g_norms[...] = jnp.zeros_like(g_norms)
+    g_shift[...] = jnp.zeros_like(g_shift)
+    step = 512
+    weight_sum(g_embed, d_table, sent, stage, sem)
+    h_two = sent
+
+    def middle(i):
+        r = rows_of(i, chunk)
+        d_emb = d_table[r, :]
+        g_shift[0:1, :] += column_sum(d_emb.astype(F32))
+        e = nn(d_emb, w_embed[...]).astype(BF16)
+        e_two[r, :] = e
+        for t in range(w_up.shape[0] // step):
+            cols = slice(t * step, (t + 1) * step)
+            d_act = nn(e, w_down[:, cols])
+            slope[r, cols] = (d_act * slope[r, cols].astype(F32)).astype(BF16)
+        d_h = nn(slope[r, :], w_up[...])
+        hat, scale = unit(x_one[r, :])
+        h_two[r, :] = (hat * gain[2] + gain[3]).astype(BF16)
+        g_norms[2:3, :] += column_sum(d_h * hat)
+        g_norms[3:4, :] += column_sum(d_h)
+        d_one = e.astype(F32) + unit_back(d_h * gain[2], hat, scale)
+        d_patches[r, :] = d_one
+        e_one[r, :] = d_one.astype(BF16)
+
+    outer_loop(rows // chunk, middle)
+    weight_sum(g_down, e_two, act, stage_wide, sem)
+    weight_sum(g_up, slope, h_two, stage, sem)
+    weight_sum(g_out, e_one, mixed, stage, sem)
+
+    def mix_back(i):
+        r = rows_of(i, chunk)
+        mixed[r, :] = nn(e_one[r, :], w_out[...]).astype(BF16)
+
+    outer_loop(rows // chunk, mix_back)
+
+    def attend_back(g):
+        r = rows_of(g, n)
+        bias = mask_bias(own_row[g], key_col[r, :])
+        for t in range(tiles):
+            cols = [slice((t + j * tiles) * LANES, (t + j * tiles + 1) * LANES) for j in range(3)]
+            q, k, v = [qkv[r, col] for col in cols]
+            logs = [totals[g, t * per_tile + h : t * per_tile + h + 1, :] for h in range(per_tile)]
+            found = attend_tile_back(q, k, v, mixed[r, cols[0]], bias, logs, head_size)
+            for j in range(3):
+                act[r, cols[j]] = found[j].astype(BF16)
+
+    outer_loop(groups, attend_back)
+    h_one = h_two
+
+    def finish(i):
+        r = rows_of(i, chunk)
+        d_h = nn(act[r, : 3 * width], w_qkv[...])
+        hat, scale = unit(patches[r, :].astype(F32))
+        h_one[r, :] = (hat * gain[0] + gain[1]).astype(BF16)
+        g_norms[0:1, :] += column_sum(d_h * hat)
+        g_norms[1:2, :] += column_sum(d_h)
+        d_patches[r, :] += unit_back(d_h * gain[0], hat, scale)
+
+    outer_loop(rows // chunk, finish)
+    weight_sum(g_qkv, act.at[:, : 3 * width], h_one, stage, sem)
+
+
+def slot_plan(peers, slot_rows):
+    padded = -(-slot_rows // 16) * 16
+    joined = max(1, 128 // padded)
+    return padded, joined
+
+
+def encoder(patches, counts, norms, shift, weights, embed, heads):
+    peers = counts.shape[0]
+    width = patches.shape[1]
+    slot_rows = patches.shape[0] // peers
+    padded, joined = slot_plan(peers, slot_rows)
+    rows, groups = peers * padded, peers // joined
+    n = rows // groups
+    head_size = width // heads
+    x = jnp.pad(patches.reshape(peers, slot_rows, width), ((0, 0), (0, padded - slot_rows), (0, 0)))
+    x = x.reshape(rows, width)
+    row = jnp.arange(padded, dtype=jnp.int32)[None, :]
+    slot = jnp.arange(peers, dtype=jnp.int32)[:, None]
+    live = (row >= slot_rows - counts[:, None]) & (row < slot_rows)
+    keys = jnp.where(live, slot, -1).reshape(rows, 1)
+    own = jnp.broadcast_to(slot, (peers, padded)).reshape(groups, 1, n)
+    ff = weights[2].shape[0]
+    vm = pl.BlockSpec(memory_space=pltpu.VMEM)
+    shapes = [
+        ((rows, weights[0].shape[0]), BF16),
+        ((groups, -(-heads // 8) * 8, n), F32),
+        ((rows, width), BF16),
+        ((rows, width), F32),
+        ((rows, ff), BF16),
+        ((rows, ff), BF16),
+        ((rows, width), BF16),
+    ]
+    shapes = [jax.ShapeDtypeStruct(s, t) for s, t in shapes]
+    embedded, *stored = pl.pallas_call(
+        functools.partial(encoder_kernel, head_size, groups, 2 * n),
+        out_shape=[jax.ShapeDtypeStruct((rows, embed.shape[0]), BF16)] + shapes,
+        in_specs=[vm] * 10,
+        out_specs=[vm] * 8,
+        compiler_params=pltpu.CompilerParams(vmem_limit_bytes=60 << 20),
+        name="encoder",
+    )(x, keys, own, norms, shift, *weights, embed)
+    return embedded, (x, keys, own), stored
+
+
+def encoder_back(rows_in, norms, weights, embed, d_table, stored, heads):
+    x, keys, own = rows_in
+    rows, width = x.shape
+    groups, _, n = own.shape
+    head_size = width // heads
+    vm = pl.BlockSpec(memory_space=pltpu.VMEM)
+    return pl.pallas_call(
+        functools.partial(encoder_back_kernel, head_size, groups, 2 * n),
+        out_shape=[
+            jax.ShapeDtypeStruct((rows, width), F32),
+            jax.ShapeDtypeStruct((8, width), F32),
+            jax.ShapeDtypeStruct((8, embed.shape[0]), F32),
+        ]
+        + [jax.ShapeDtypeStruct(w.shape, BF16) for w in weights]
+        + [jax.ShapeDtypeStruct(embed.shape, BF16)],
+        in_specs=[vm] * 17,
+        out_specs=[vm] * 3 + [pl.BlockSpec(memory_space=pl.ANY)] * 5,
+        scratch_shapes=[pltpu.VMEM((rows, width), BF16)] * 2
+        + [
+            pltpu.VMEM((2, 256, width), BF16),
+            pltpu.VMEM((2, LANES, weights[2].shape[0]), BF16),
+            pltpu.SemaphoreType.DMA((2,)),
+        ],
+        compiler_params=pltpu.CompilerParams(vmem_limit_bytes=62 << 20),
+        name="encoder_back",
+    )(x, keys, own, norms, *weights, embed, d_table, *stored)
 
 
 def per_device(
@@ -604,58 +1068,37 @@
     dec_up,
     dec_down,
 ):
-    peer_count = lax.axis_size("dp")
-    width_enc = patches.shape[1]
-    slot_rows = patches.shape[0] // peer_count
+    peers = lax.axis_size("dp")
+    width = patches.shape[1]
+    slot_rows = patches.shape[0] // peers
     masters = (enc_qkv, enc_out, enc_up, enc_down, dec_embed, dec_qkv, dec_out, dec_up, dec_down)
     norms_e, norms_d, whole = gather_masters(staged, enc_norms, dec_norms, masters)
-    enc_rows = patches.astype(jnp.float32).reshape(peer_count, slot_rows, width_enc)
-    live_counts = send_counts.reshape(peer_count)
-    live_rows = (
-        jnp.arange(slot_rows, dtype=jnp.int32)[None, :] >= (slot_rows - live_counts)[:, None]
+    enc_weights, embed, dec_weights = whole[:4], whole[4], whole[5:]
+    embedded, enc_inputs, stored = encoder(
+        patches, send_counts.reshape(peers), norms_e, norms_d, enc_weights, embed, HEADS_E
     )
-    enc_allowed = jnp.broadcast_to(live_rows[:, None, :], (peer_count, slot_rows, slot_rows))
-    enc_params = (norms_e, *whole[:4])
-    enc_result, enc_stored = block_forward(enc_rows, enc_params, enc_allowed, HEADS_E)
-    enc_send = enc_result.astype(jnp.bfloat16)
-    dec_gains = norms_d.astype(jnp.float32)
-    w_embed = whole[4]
-    embedded = (project(enc_send, w_embed) + dec_gains[7]).astype(jnp.bfloat16)
-    arrived = lax.all_to_all(embedded, "dp", split_axis=0, concat_axis=0, tiled=True)
-    slot_count = peer_count * slot_rows
-    slot_table = arrived.reshape(slot_count, -1)
-    visible = source_index >= 0
-    picked = jnp.take(slot_table, jnp.where(visible, source_index, 0), axis=0)
-    dec_start = jnp.where(visible[..., None], picked.astype(jnp.float32), dec_gains[6])
-    dec_allowed = dec_segment[:, :, None] == dec_segment[:, None, :]
-    dec_params = (norms_d, *whole[5:])
-    dec_two, dec_stored = block_forward(dec_start, dec_params, dec_allowed, HEADS_D)
-    decoded, final_pull = jax.vjp(layer_norm, dec_two, dec_gains[4], dec_gains[5])
-    d_final, d_gain_final, d_shift_final = final_pull(cotangent)
-    d_start, dec_grads = block_backward(
-        dec_start, dec_params, dec_allowed, HEADS_D, dec_stored, d_final
+    padded = embedded.shape[0] // peers
+
+    def swap(table):
+        slots = table.reshape(peers, padded, table.shape[1])
+        return lax.all_to_all(slots, "dp", split_axis=0, concat_axis=0, tiled=True).reshape(table.shape)
+
+    place_of = source_index // slot_rows * padded + source_index % slot_rows
+    index = jnp.where(source_index >= 0, place_of, -1)
+    decoded, d_table, g_dec_norms, *dec_grads = decoder(
+        swap(embedded), index, dec_segment, cotangent, norms_d, dec_weights, HEADS_D
     )
-    d_token = jnp.sum(jnp.where(visible[..., None], 0.0, d_start), axis=(0, 1))
-    d_picked = jnp.where(visible[..., None], d_start, 0.0).astype(jnp.bfloat16)
-    d_table = jnp.zeros((slot_count, d_start.shape[-1]), jnp.bfloat16)
-    d_table = d_table.at[jnp.where(visible, source_index, slot_count)].set(d_picked, mode="drop")
-    d_table = d_table.reshape(peer_count, slot_rows, -1)
-    returned = lax.all_to_all(d_table, "dp", split_axis=0, concat_axis=0, tiled=True)
-    g_embed = outer_sum(enc_send, returned)
-    d_bias = jnp.sum(returned.astype(jnp.float32), axis=(0, 1))
-    d_enc = project_back(returned, w_embed).astype(jnp.bfloat16)
-    d_patches, enc_grads = block_backward(
-        enc_rows, enc_params, enc_allowed, HEADS_E, enc_stored, d_enc.astype(jnp.float32)
+    d_patches, g_enc_norms, g_shift, *enc_grads = encoder_back(
+        enc_inputs, norms_e, enc_weights, embed, swap(d_table), stored, HEADS_E
     )
-    g_dec_norms = jnp.concatenate(
-        [dec_grads[0], jnp.stack([d_gain_final, d_shift_final, d_token, d_bias])], axis=0
+    g_dec_norms = jnp.concatenate([g_dec_norms[:7], g_shift[:1]], axis=0)
+    s_enc_norms, s_dec_norms, sums = reduce_masters(
+        staged, g_enc_norms[:4], g_dec_norms, [*enc_grads, *dec_grads]
     )
-    s_enc_norms, s_dec_norms, sums = reduce_masters(
-        staged, enc_grads[0], g_dec_norms, [*enc_grads[1:], g_embed, *dec_grads[1:]]
-    )
+    d_patches = d_patches.reshape(peers, padded, width)[:, :slot_rows]
     return (
         decoded,
-        d_patches.reshape(-1, width_enc),
+        d_patches.reshape(-1, width),
         s_enc_norms,
         *sums[:4],
         s_dec_norms,

time: 778 us -> 604 us (0.78)
  matrix products: 257 us -> 0 us
  Pallas kernels: 237 us -> 479 us
  other arithmetic: 139 us -> 6.33 us
  local copies, waits for them, and re-layouts: 101 us -> 47.9 us
  waiting for transfers between devices: 21.9 us -> 40 us
  starting transfers between devices: 12.7 us -> 20.5 us
    dot_general x39 -> x0, matrix products: 257 us -> none  [the longest x9 44.9 us: outer_sum(): jnp.einsum('grc,grw->cw', gradient, left_side, preferred_element_type=jnp...]
    pallas_call x0 -> x3, Pallas kernels: none -> 243 us  [the longest x1 109 us: decoder(): pl.pallas_call(functools.partial(decoder_kernel, head_size, chunk), out_s...]
    convert_element_type x9 -> x0, other arithmetic: 89.1 us -> none  [the longest x2 45.8 us: block_forward(): activated = gelu_exact(up_proj).astype(jnp.bfloat16)]
    reduce_sum x18 -> x0, other arithmetic: 35.3 us -> none  [the longest x2 18.6 us: attend(): row_total = jnp.sum(weights, axis=-1, keepdims=True)]
    convert_element_type x8 -> x0, local copies, waits for them, and re-layouts: 22.7 us -> none  [the longest x2 12.3 us: block_forward(): joined_qkv = project(h_one, w_qkv).astype(jnp.bfloat16)]
    all_to_all x2, waiting for transfers between devices: 21.8 us -> 40 us  [swap(): lax.all_to_all(slots, 'dp', split_axis=0, concat_axis=0, tiled=True)]
    scatter x1 -> x0, local copies, waits for them, and re-layouts: 9.69 us -> none  [per_device(): d_table.at[jnp.where(visible, source_index, slot_count)]]
    all_to_all x2, starting transfers between devices: 12.1 us -> 19.9 us  [swap(): lax.all_to_all(slots, 'dp', split_axis=0, concat_axis=0, tiled=True)]
  transfers between devices with their start and end apart: 4 -> 4, of which waited for: 2 -> 2; matrix products, arithmetic and copies ran while one was open for 5% -> 3% of each run, Pallas kernels for 0% -> 0%
where the time goes in v2:
time: 604 us; the launch traced here: 595 us
  Pallas kernels  479 us (79%)
  local copies, waits for them, and re-layouts  47.9 us (8%)
  waiting for transfers between devices  40 us (7%)
  starting transfers between devices  20.5 us (3%)
  other arithmetic  6.33 us (1%)
    pallas_call x1, Pallas kernels, gather_all(): pl.pallas_call(functools.partial(gather_kernel, entries), out_shape=[jax....  119 us
    pallas_call x1, Pallas kernels, reduce_all(): pl.pallas_call(functools.partial(reduce_kernel, entries), out_shape=[jax....  117 us
    pallas_call x1, Pallas kernels, decoder(): pl.pallas_call(functools.partial(decoder_kernel, head_size, chunk), out_s...  109 us
    pallas_call x1, Pallas kernels, encoder_back(): pl.pallas_call(functools.partial(encoder_back_kernel, head_size, groups,...  83.2 us
    pallas_call x1, Pallas kernels, encoder(): pl.pallas_call(functools.partial(encoder_kernel, head_size, groups, 2 * n...  50.5 us
    all_to_all x2, waiting for transfers between devices, swap(): lax.all_to_all(slots, 'dp', split_axis=0, concat_axis=0, tiled=True)  40 us
    unnamed x78, local copies, waits for them, and re-layouts  28.3 us
    all_to_all x2, starting transfers between devices, swap(): lax.all_to_all(slots, 'dp', split_axis=0, concat_axis=0, tiled=True)  19.9 us
  transfers between devices with their start and end apart: 4, of which 2 were waited for; matrix products, arithmetic and copies ran while one was open for 3% of the time, Pallas kernels for 0%

profile of v2, /device:TPU:0, one launch (start us, length us, event | category | flops | bytes accessed | tf_op | source)
XLA Modules:
  0.0 595.1 jit_solution(17721749460520698150)
XLA Ops:
  0.7 1.0 convert_element_type.48
  1.7 1.0 copy.45
  2.7 1.1 copy.44
  3.8 1.0 convert_bitcast_fusion.1
  5.9 0.9 select_n.81.key_col
  7.2 1.2 pad.34
  8.6 1.0 bitcast_select_fusion
  10.0 118.9 %gather_weights.1 = (bf16[4,2,32,512]{3,2,1,0:T(8,128)(2,1)S(1)}, bf16[4,2,2,144,768]{4,3,2,1,0:T(8,128)(2,1)S(1)}, bf16[4,2,2,48,768]{4,3,2,1,0:T(8,128)(2,1)S(...) custom-call(bf16[32,128]{1,0:T(8,128)(2,1)S(1)} %scatter.15.refs_0_,, ...), custom_call_target="tpu_custom_call" | custom-call | tf_op jit(solution)/shard_map/gather_weights/pallas_call | solution.py:183
  128.9 2.1 copy-done
  131.0 2.1 copy-done.1
  133.1 1.9 copy-done.2
  135.0 1.0 copy-done.3
  136.0 0.9 copy-done.4
  136.9 1.3 copy-done.5
  138.3 1.3 copy-done.6
  139.6 1.1 copy-done.7
  140.7 0.8 copy-done.8
  143.6 50.5 %encoder.1 = (bf16[896,512]{1,0:T(8,128)(2,1)}, bf16[896,2304]{1,0:T(8,128)(2,1)}, f32[8,16,112]{2,1,0:T(8,128)}, bf16[896,768]{1,0:T(8,128)(2,1)}, f32[896,768]...) custom-call(bf16[896,768]{1,0:T(8,128)(2,1)} %bitcast.102, ...), custom_call_target="tpu_custom_call" | custom-call | tf_op jit(solution)/shard_map/encoder/pallas_call | solution.py:1013
  194.2 8.1 %all-to-all-start = ((bf16[8,112,512]{2,1,0:T(8,128)(2,1)}), bf16[8,112,512]{2,1,0:T(8,128)(2,1)S(1)}, u32[]{:S(2)}, u32[]{:S(2)}) async-start(bf16[8,112,512]{2,1,0:T(8,128)(2,1)} %bitcast.114), calls=%async_computation | async-start | bytes 1835008 | tf_op jit(solution)/shard_map/all_to_all | solution.py:1084
  203.0 1.2 broadcast_in_dim_reshape.9.index_col
  204.8 1.2 reshape.385.seg_col
  206.4 1.6 pad.37.cot
  208.0 17.7 %all-to-all-done = bf16[8,112,512]{2,1,0:T(8,128)(2,1)S(1)} async-done(((bf16[8,112,512]{2,1,0:T(8,128)(2,1)}), bf16[8,112,512]{2,1,0:T(8,128)(2,1)S(1)}, u32[]{:S(2)}, u32[]{:S(2)}) %all-to-all-start) | async-done | bytes 917536 | tf_op jit(solution)/shard_map/all_to_all | solution.py:1084
  225.7 1.0 copy-done.9
  226.7 109.4 %decoder.1 = (f32[2,529,512]{2,1,0:T(8,128)}, bf16[896,512]{1,0:T(8,128)(2,1)}, f32[8,512]{1,0:T(8,128)}, bf16[1536,512]{1,0:T(8,128)(2,1)}, bf16[512,512]{1,0:T...) custom-call(bf16[896,512]{1,0:T(8,128)(2,1)} %bitcast.106, ...), custom_call_target="tpu_custom_call" | custom-call | tf_op jit(solution)/shard_map/decoder/pallas_call | solution.py:768
  336.0 11.8 %all-to-all-start.1 = ((bf16[8,112,512]{2,1,0:T(8,128)(2,1)}), bf16[8,112,512]{2,1,0:T(8,128)(2,1)S(1)}, u32[]{:S(2)}, u32[]{:S(2)}) async-start(bf16[8,112,512]{2,1,0:T(8,128)(2,1)} %bitcast.115), calls=%async_computation.1 | async-start | bytes 1835008 | tf_op jit(solution)/shard_map/all_to_all | solution.py:1084
  347.9 0.7 slice.210
  348.6 22.3 %all-to-all-done.1 = bf16[8,112,512]{2,1,0:T(8,128)(2,1)S(1)} async-done(((bf16[8,112,512]{2,1,0:T(8,128)(2,1)}), bf16[8,112,512]{2,1,0:T(8,128)(2,1)S(1)}, u32[]{:S(2)}, u32[]{:S(2)}) %all-to-all-start.1) | async-done | bytes 917536 | tf_op jit(solution)/shard_map/all_to_all | solution.py:1084
  371.8 83.2 %encoder_back.1 = (f32[896,768]{1,0:T(8,128)}, f32[8,768]{1,0:T(8,128)}, f32[8,512]{1,0:T(8,128)}, bf16[2304,768]{1,0:T(8,128)(2,1)}, bf16[768,768]{1,0:T(8,128)...) custom-call(bf16[896,768]{1,0:T(8,128)(2,1)} %bitcast.103, ...), custom_call_target="tpu_custom_call" | custom-call | tf_op jit(solution)/shard_map/encoder_back/pallas_call | solution.py:1030
  455.0 0.7 slice.212
  455.7 0.7 slice.211
  457.1 0.8 reshape.375.refs_0_
  457.9 116.8 %reduce_gradients.1 = (f32[32,128]{1,0:T(8,128)}, f32[144,384]{1,0:T(8,128)}, f32[48,384]{1,0:T(8,128)}, f32[192,384]{1,0:T(8,128)}, f32[96,768]{1,0:T(8,128)}, ...) custom-call(bf16[4,2,32,512]{3,2,1,0:T(8,128)(2,1)} %reshape.375.refs, ...), custom_call_target="tpu_custom_call" | custom-call | tf_op jit(solution)/shard_map/reduce_gradients/pallas_call | solution.py:350
  574.8 1.1 constant_dynamic-update-slice_fusion.3
  575.9 0.9 constant_dynamic-update-slice_fusion.2
  576.8 1.0 constant_dynamic-update-slice_fusion.1
  577.7 0.8 constant_dynamic-update-slice_fusion
  578.5 0.9 slice_select_fusion
  579.5 3.0 copy.57
  582.5 1.2 slice.159
  583.7 1.2 slice.162
  585.1 1.7 reshape.373
  586.9 0.8 copy.61
  587.6 1.2 broadcast_select_fusion.1
  589.0 0.7 copy.59
  589.8 0.9 copy.60
  590.7 0.9 copy.58
  592.2 0.7 copy.82
  (112 shorter events, 10.2 us)
Async XLA Ops:
  0.6 4.9 copy-start.28
  0.7 4.9 copy-start.29
  0.7 4.9 copy-start.27
  0.7 4.9 copy-start.21
  0.7 4.9 copy-start.17
  0.7 5.1 copy-start.18
  0.7 5.1 copy-start.15
  0.7 6.1 %copy-start.14 = (bf16[792,768]{1,0:T(8,128)(2,1)S(1)}, bf16[792,768]{1,0:T(8,128)(2,1)}, u32[]{:S(2)}) copy-start(bf16[792,768]{1,0:T(8,128)(2,1)} %param.24) | copy-start | bytes 3649540
  5.0 3.6 collective-permute-start
  6.8 1.8 copy-start.23
  128.9 2.1 copy-start
  131.0 2.1 copy-start.1
  133.1 1.9 copy-start.2
  135.0 1.0 copy-start.3
  136.0 0.9 copy-start.4
  136.9 1.3 copy-start.5
  138.3 1.3 copy-start.6
  139.6 1.1 copy-start.7
  140.7 0.8 copy-start.8
  143.6 58.7 %copy-start.25 = (s32[2,529]{1,0:T(2,128)S(1)}, s32[2,529]{1,0:T(2,128)}, u32[]{:S(2)}) copy-start(s32[2,529]{1,0:T(2,128)} %param.27) | copy-start | bytes 12700
  194.1 10.1 %copy-start.26 = (s32[2,529]{1,0:T(2,128)S(1)}, s32[2,529]{1,0:T(2,128)}, u32[]{:S(2)}) copy-start(s32[2,529]{1,0:T(2,128)} %param.26) | copy-start | bytes 12700
  194.1 11.9 %copy-start.13 = (f32[2,529,512]{2,0,1:T(2,128)S(1)}, f32[2,529,512]{2,0,1:T(2,128)}, u32[]{:S(2)}) copy-start(f32[2,529,512]{2,0,1:T(2,128)} %param.28) | copy-start | bytes 6500356
  194.2 31.5 %all-to-all-start = ((bf16[8,112,512]{2,1,0:T(8,128)(2,1)}), bf16[8,112,512]{2,1,0:T(8,128)(2,1)S(1)}, u32[]{:S(2)}, u32[]{:S(2)}) async-start(bf16[8,112,512]{2,1,0:T(8,128)(2,1)} %bitcast.114), calls=%async_computation | async-start | bytes 1835008 | tf_op jit(solution)/shard_map/all_to_all | solution.py:1084
  225.7 1.0 copy-start.9
  336.0 34.9 %all-to-all-start.1 = ((bf16[8,112,512]{2,1,0:T(8,128)(2,1)}), bf16[8,112,512]{2,1,0:T(8,128)(2,1)S(1)}, u32[]{:S(2)}, u32[]{:S(2)}) async-start(bf16[8,112,512]{2,1,0:T(8,128)(2,1)} %bitcast.115), calls=%async_computation.1 | async-start | bytes 1835008 | tf_op jit(solution)/shard_map/all_to_all | solution.py:1084
  370.9 0.9 copy-start.10
  574.8 4.7 copy-start.12
  579.5 5.4 copy-start.11
  579.5 8.2 %collective-permute-start.1 = (f32[416,192]{1,0:T(8,128)}, f32[416,192]{1,0:T(8,128)}, u32[]{:S(2)}, u32[]{:S(2)}) collective-permute-start(f32[416,192]{1,0:T(8,128)} %slice_select_fusion), channel_id=1, source_target_pairs={{0,1},{1,0},{2,3},{3,2},{4,5},{5,4},{6,7},{7,6},{8,9},{9,8},{10,11... | collective-permute-start | bytes 958472 | tf_op jit(solution)/shard_map/ppermute | solution.py:388
  585.1 1.7 copy-start.20
  588.9 3.3 copy-start.16
  588.9 4.0 copy-start.22
  589.0 4.6 copy-start.24
  589.0 5.2 copy-start.19

commit v3 on v2

--- a/solution.py
+++ b/solution.py
@@ -140,69 +140,6 @@
         ]
 
     return local, [first, second, third, fourth]
-
-
-def gather_kernel(entries, *refs):
-    n = len(entries)
-    pieces, outs = refs[:n], refs[n : 2 * n]
-    send_sem, recv_sem, local_sem = refs[2 * n :]
-    sems = (send_sem, recv_sem)
-    z, x, y, c = place()
-    plans = [
-        gather_stages(e, i, pieces[i], outs[i], sems, local_sem) for i, e in enumerate(entries)
-    ]
-    locals_ = [plan[0]() for plan in plans]
-    for copy in locals_:
-        copy.start()
-    greet(z, x, y, c)
-    moving = {}
-    for t in range(n + 4):
-        for stage in (3, 2, 1, 0):
-            i = t - stage
-            if not 0 <= i < n:
-                continue
-            if stage > 0:
-                for copy in moving[i, stage - 1]:
-                    copy.wait_recv()
-                if stage == 1:
-                    locals_[i].wait()
-            moving[i, stage] = plans[i][1][stage]()
-            for copy in moving[i, stage]:
-                copy.start()
-    for i in range(n):
-        for copy in moving[i, 3]:
-            copy.wait_recv()
-        for stage in range(4):
-            for copy in moving[i, stage]:
-                copy.wait_send()
-
-
-def gather_all(entries, pieces):
-    any_space = pl.BlockSpec(memory_space=pl.ANY)
-    n = len(entries)
-    return pl.pallas_call(
-        functools.partial(gather_kernel, entries),
-        out_shape=[jax.ShapeDtypeStruct(e.whole, BF16) for e in entries],
-        in_specs=[any_space] * n,
-        out_specs=[any_space] * n,
-        scratch_shapes=[
-            pltpu.SemaphoreType.DMA((n, 10)),
-            pltpu.SemaphoreType.DMA((n, 10)),
-            pltpu.SemaphoreType.DMA((n,)),
-        ],
-        compiler_params=pltpu.CompilerParams(
-            collective_id=0, has_side_effects=True, vmem_limit_bytes=16 << 20
-        ),
-        name="gather_weights",
-    )(*pieces)
-
-
-def add_into(dst, src, count):
-    def step(i, carry):
-        dst[i] = (dst[i].astype(F32) + src[i].astype(F32)).astype(BF16)
-        return carry
-
-    lax.fori_loop(0, count, step, 0)
 
 
 def reduce_stages(e, i, grad, out, buf, sems, local_sem):
@@ -395,18 +332,20 @@
     ]
 
 
-def gather_masters(staged, enc_norms, dec_norms, weights):
+def gather_masters(enc_norms, dec_norms, weights):
+    whole = []
+    for w in weights:
+        tall = lax.all_gather(w.astype(BF16).T, "dp", axis=0, tiled=True)
+        whole.append(lax.all_gather(tall, "fsdp", axis=1, tiled=True))
+    norms = []
+    for rows in (enc_norms, dec_norms):
+        wide = lax.all_gather(rows.astype(BF16), "dp", axis=1, tiled=True)
+        norms.append(lax.all_gather(wide, "fsdp", axis=0, tiled=True))
+    return norms[0], norms[1], whole
+
+
+def staged_pieces(enc_norms, dec_norms, weights):
     blocks = [w.astype(BF16).T for w in weights]
-    if not staged:
-        whole = []
-        for b in blocks:
-            tall = lax.all_gather(b, "dp", axis=0, tiled=True)
-            whole.append(lax.all_gather(tall, "fsdp", axis=1, tiled=True))
-        norms = []
-        for rows in (enc_norms, dec_norms):
-            wide = lax.all_gather(rows.astype(BF16), "dp", axis=1, tiled=True)
-            norms.append(lax.all_gather(wide, "fsdp", axis=0, tiled=True))
-        return norms[0], norms[1], whole
     entries = [entry_of(b.shape[0], 4 * b.shape[1]) for b in blocks]
     pieces = list(blocks)
     cores = [k for k, e in enumerate(entries) if e.by_core]
@@ -422,14 +361,7 @@
         dec_norms.astype(BF16)
     )
     entries = [entry_of(NORM_ROWS, 512)] + entries
-    whole = gather_all(entries, [small] + pieces)
-    tiles = whole[0].reshape(8, NORM_ROWS, 4, 128)
-    norms = []
-    for start, rows in ((0, enc_norms), (half, dec_norms)):
-        n, width = rows.shape
-        part = tiles[:, start : start + n, :, :width]
-        norms.append(part.transpose(2, 1, 0, 3).reshape(4 * n, 8 * width))
-    return norms[0], norms[1], [w.reshape(-1, e.width) for w, e in zip(whole[1:], entries[1:])]
+    return entries, [small] + pieces
 
 
 def reduce_masters(staged, g_enc_norms, g_dec_norms, grads):
@@ -983,14 +915,13 @@
     return padded, joined
 
 
-def encoder(patches, counts, norms, shift, weights, embed, heads):
+def encoder_inputs(patches, counts):
     peers = counts.shape[0]
     width = patches.shape[1]
     slot_rows = patches.shape[0] // peers
     padded, joined = slot_plan(peers, slot_rows)
     rows, groups = peers * padded, peers // joined
     n = rows // groups
-    head_size = width // heads
     x = jnp.pad(patches.reshape(peers, slot_rows, width), ((0, 0), (0, padded - slot_rows), (0, 0)))
     x = x.reshape(rows, width)
     row = jnp.arange(padded, dtype=jnp.int32)[None, :]
@@ -998,6 +929,14 @@
     live = (row >= slot_rows - counts[:, None]) & (row < slot_rows)
     keys = jnp.where(live, slot, -1).reshape(rows, 1)
     own = jnp.broadcast_to(slot, (peers, padded)).reshape(groups, 1, n)
+    return x, keys, own, padded
+
+
+def encoder(patches, counts, norms, shift, weights, embed, heads):
+    x, keys, own, _ = encoder_inputs(patches, counts)
+    rows, width = x.shape
+    groups, _, n = own.shape
+    head_size = width // heads
     ff = weights[2].shape[0]
     vm = pl.BlockSpec(memory_space=pltpu.VMEM)
     shapes = [
@@ -1049,6 +988,293 @@
     )(x, keys, own, norms, *weights, embed, d_table, *stored)
 
 
+class Ticker:
+    def __init__(self, plans, locals_):
+        self.plans, self.locals_, self.moving, self.t = plans, locals_, {}, 0
+
+    def tick(self, count=1):
+        for _ in range(count):
+            for stage in (3, 2, 1, 0):
+                i = self.t - stage
+                if 0 <= i < len(self.plans):
+                    self.advance(i, stage)
+            self.t += 1
+
+    def advance(self, i, stage):
+        if stage > 0:
+            for copy in self.moving[i, stage - 1]:
+                copy.wait_recv()
+            if stage == 1:
+                self.locals_[i].wait()
+        self.moving[i, stage] = self.plans[i][stage]()
+        for copy in self.moving[i, stage]:
+            copy.start()
+
+    def arrived(self, i):
+        for copy in self.moving[i, 3]:
+            copy.wait_recv()
+
+    def drain(self):
+        for copies in self.moving.values():
+            for copy in copies:
+                copy.wait_send()
+
+
+def flat(ref):
+    value = ref[...]
+    return value.reshape(-1, value.shape[-1])
+
+
+def spread_norms(tiles, start, count, part, out):
+    width = 8 * part
+    lane = lax.broadcasted_iota(jnp.int32, (LANES, width), 1)
+    line = lax.broadcasted_iota(jnp.int32, (LANES, width), 0)
+    for f in range(4):
+        total = 0.0
+        for d in range(8):
+            put = jnp.where((lane == line + d * part) & (line < part), 1.0, 0.0).astype(BF16)
+            rows = tiles[d // 2, d % 2, start : start + 16, f * LANES : (f + 1) * LANES]
+            total = total + nn(rows, put)
+        out[f * count : (f + 1) * count, :] = total[:count]
+
+
+def front_kernel(entries, head_size, groups, chunk, sizes, *refs):
+    n_in = len(entries)
+    pieces, refs = refs[:n_in], refs[n_in:]
+    patches, key_col, own_row, *refs = refs
+    whole, refs = refs[:n_in], refs[n_in:]
+    norms_e, norms_d, table, totals, *refs = refs
+    kept_out, refs = refs[:6], refs[6:]
+    kept, refs = refs[:6], refs[6:]
+    qkv, mixed, x_one, act, slope, sent = kept
+    loaded, refs = refs[:6], refs[6:]
+    tiles_v, w_qkv, w_out, w_up, w_embed, w_down = loaded
+    embedded, send_sem, recv_sem, local_sem, load_sem, keep_sem, swap_send, swap_recv, swap_local = refs
+    rows, width = patches.shape
+    n = rows // groups
+    tiles = width // LANES
+    per_tile = LANES // head_size
+    z, x, y, c = place()
+    d = z * 2 + x
+
+    plans, locals_ = [], []
+    for i, e in enumerate(entries):
+        local, stages = gather_stages(e, i, pieces[i], whole[i], (send_sem, recv_sem), local_sem)
+        plans.append(stages)
+        locals_.append(local())
+    for copy in locals_:
+        copy.start()
+    barrier = pltpu.get_barrier_semaphore()
+    peers = [(lax.rem(d + k, 8), y * 2 + c) for k in range(1, 8)]
+    peers += [at(z, x, 1 - y, c), at(z, x, y, 1 - c)]
+    for peer in peers:
+        pl.semaphore_signal(barrier, inc=1, device_id=peer, device_id_type=MESH)
+    pl.semaphore_wait(barrier, len(peers))
+    ticker = Ticker(plans, locals_)
+
+    def load(i):
+        ticker.arrived(i)
+        copy = pltpu.make_async_copy(whole[i], loaded[i], load_sem.at[i])
+        copy.start()
+        return copy
+
+    keeping = []
+
+    def keep(k):
+        copy = pltpu.make_async_copy(kept[k], kept_out[k], keep_sem.at[k])
+        copy.start()
+        keeping.append(copy)
+
+    def some(lo, hi, body):
+        def step(i, carry):
+            body(i)
+            return carry
+
+        lax.fori_loop(lo, hi, step, 0)
+
+    ticker.tick(5)
+    copies = [load(0), load(1)]
+    for copy in copies:
+        copy.wait()
+    spread_norms(tiles_v, 0, sizes[0], sizes[1], norms_e)
+    spread_norms(tiles_v, NORM_ROWS // 2, sizes[2], sizes[3], norms_d)
+    gain = [norms_e[k : k + 1, :] for k in range(4)]
+    add = norms_d[7:8, :]
+
+    def start(i):
+        r = rows_of(i, chunk)
+        hat, _ = unit(patches[r, :].astype(F32))
+        qkv[r, :] = nt((hat * gain[0] + gain[1]).astype(BF16), flat(w_qkv)).astype(BF16)
+
+    some(0, 2, start)
+    ticker.tick()
+    some(2, 4, start)
+    keep(0)
+
+    def attend(g):
+        r = rows_of(g, n)
+        bias = mask_bias(own_row[g], key_col[r, :])
+        for t in range(tiles):
+            q, k, v = [qkv[r, (t + j * tiles) * LANES : (t + j * tiles + 1) * LANES] for j in range(3)]
+            out, logs = attend_tile(q, k, v, bias, head_size)
+            mixed[r, t * LANES : (t + 1) * LANES] = out.astype(BF16)
+            for h in range(per_tile):
+                totals[g, t * per_tile + h : t * per_tile + h + 1, :] = logs[h]
+
+    some(0, groups // 2, attend)
+    ticker.tick()
+    some(groups // 2, groups, attend)
+    keep(1)
+    copies = [load(2), load(3)]
+    ticker.tick()
+    for copy in copies:
+        copy.wait()
+    step = w_up.shape[-2] * (2 if len(w_up.shape) == 5 else 1)
+
+    def lift(i):
+        r = rows_of(i, chunk)
+        one = patches[r, :].astype(F32) + nt(mixed[r, :], flat(w_out))
+        x_one[r, :] = one
+        hat, _ = unit(one)
+        h = (hat * gain[2] + gain[3]).astype(BF16)
+        for t in range(8):
+            u = nt(h, w_up[t // 2, t % 2].reshape(step, width))
+            a, s = gelu_pair(u)
+            act[r, t * step : (t + 1) * step] = a.astype(BF16)
+            slope[r, t * step : (t + 1) * step] = s.astype(BF16)
+
+    some(0, 1, lift)
+    copies = [load(4)]
+    some(1, 2, lift)
+    ticker.tick()
+    some(2, 3, lift)
+    copies.append(load(5))
+    some(3, 4, lift)
+    for k in (2, 3, 4):
+        keep(k)
+    for copy in copies:
+        copy.wait()
+    per_chunk = chunk // embedded.shape[1]
+    for i in range(4):
+
+        def lower(i):
+            r = rows_of(i, chunk)
+            two = (x_one[r, :] + nt(act[r, :], flat(w_down))).astype(BF16)
+            sent[r, :] = two
+            out = (nt(two, flat(w_embed)) + add).astype(BF16)
+            for k in range(per_chunk):
+                embedded[i * per_chunk + k] = out[k * embedded.shape[1] : (k + 1) * embedded.shape[1]]
+
+        some(i, i + 1, lower)
+        for k in range(per_chunk):
+            s = i * per_chunk + k
+
+            @pl.when(s != d)
+            def _(s=s):
+                send_slot(embedded, table, s, d, swap_send, swap_recv, y * 2 + c).start()
+
+            @pl.when(s == d)
+            def _(s=s):
+                pltpu.make_async_copy(embedded.at[s], table.at[s], swap_local.at[0]).start()
+
+        ticker.tick()
+    keep(5)
+    while ticker.t < n_in + 3:
+        ticker.tick()
+    for i in range(6, n_in):
+        ticker.arrived(i)
+    finish_swap(embedded, table, d, swap_send, swap_recv, swap_local, y * 2 + c)
+    ticker.drain()
+    for copy in keeping:
+        copy.wait()
+
+
+def send_slot(src, dst, s, d, sends, recvs, f):
+    return pltpu.make_async_remote_copy(
+        src_ref=src.at[s],
+        dst_ref=dst.at[d],
+        send_sem=sends.at[s],
+        recv_sem=recvs.at[d],
+        device_id=(s, f),
+        device_id_type=MESH,
+    )
+
+
+def finish_swap(src, dst, d, sends, recvs, local, f):
+    for s in range(8):
+
+        @pl.when(s != d)
+        def _(s=s):
+            came = pltpu.make_async_remote_copy(
+                src_ref=src.at[s],
+                dst_ref=dst.at[s],
+                send_sem=sends.at[s],
+                recv_sem=recvs.at[s],
+                device_id=(s, f),
+                device_id_type=MESH,
+            )
+            came.wait_send()
+            came.wait_recv()
+
+    pltpu.make_async_copy(src.at[d], dst.at[d], local.at[0]).wait()
+
+
+def front(entries, pieces, patches, counts, sizes, heads):
+    peers = 8
+    width = patches.shape[1]
+    x, keys, own, padded = encoder_inputs(patches, counts)
+    rows = x.shape[0]
+    groups, _, n = own.shape
+    head_size = width // heads
+    by = {k: e for k, e in enumerate(entries)}
+    wide, ff = 3 * width, 8 * entries[3].rows
+    embed = 8 * entries[4].rows
+    kept = [
+        ((rows, wide), BF16),
+        ((rows, width), BF16),
+        ((rows, width), F32),
+        ((rows, ff), BF16),
+        ((rows, ff), BF16),
+        ((rows, width), BF16),
+    ]
+    vm, hbm = pl.BlockSpec(memory_space=pltpu.VMEM), pl.BlockSpec(memory_space=pl.ANY)
+    n_in = len(entries)
+    sem = pltpu.SemaphoreType.DMA
+    found = pl.pallas_call(
+        functools.partial(front_kernel, entries, head_size, groups, rows // 4, sizes),
+        out_shape=[jax.ShapeDtypeStruct(e.whole, BF16) for e in entries]
+        + [
+            jax.ShapeDtypeStruct((4 * sizes[0], 8 * sizes[1]), F32),
+            jax.ShapeDtypeStruct((4 * sizes[2], 8 * sizes[3]), F32),
+            jax.ShapeDtypeStruct((peers, padded, embed), BF16),
+            jax.ShapeDtypeStruct((groups, -(-heads // 8) * 8, n), F32),
+        ]
+        + [jax.ShapeDtypeStruct(s, t) for s, t in kept],
+        in_specs=[hbm] * n_in + [vm] * 3,
+        out_specs=[hbm] * n_in + [vm, vm, hbm, vm] + [hbm] * 6,
+        scratch_shapes=[pltpu.VMEM(s, t) for s, t in kept]
+        + [pltpu.VMEM(by[k].whole, BF16) for k in range(6)]
+        + [
+            pltpu.VMEM((peers, padded, embed), BF16),
+            sem((n_in, 10)),
+            sem((n_in, 10)),
+            sem((n_in,)),
+            sem((6,)),
+            sem((6,)),
+            sem((8,)),
+            sem((8,)),
+            sem((1,)),
+        ],
+        compiler_params=pltpu.CompilerParams(
+            collective_id=0, has_side_effects=True, vmem_limit_bytes=60 << 20
+        ),
+        name="front",
+    )(*pieces, x, keys, own)
+    whole, (norms_e, norms_d, table, totals) = found[:n_in], found[n_in : n_in + 4]
+    qkv, mixed, x_one, act, slope, sent = found[n_in + 4 :]
+    return whole, norms_e, norms_d, table, (x, keys, own), [qkv, totals, mixed, x_one, act, slope, sent]
+
+
 def per_device(
     staged,
     patches,
@@ -1071,22 +1297,34 @@
     peers = lax.axis_size("dp")
     width = patches.shape[1]
     slot_rows = patches.shape[0] // peers
-    masters = (enc_qkv, enc_out, enc_up, enc_down, dec_embed, dec_qkv, dec_out, dec_up, dec_down)
-    norms_e, norms_d, whole = gather_masters(staged, enc_norms, dec_norms, masters)
-    enc_weights, embed, dec_weights = whole[:4], whole[4], whole[5:]
-    embedded, enc_inputs, stored = encoder(
-        patches, send_counts.reshape(peers), norms_e, norms_d, enc_weights, embed, HEADS_E
-    )
-    padded = embedded.shape[0] // peers
+    counts = send_counts.reshape(peers)
+    masters = (enc_qkv, enc_out, enc_up, dec_embed, enc_down, dec_qkv, dec_out, dec_up, dec_down)
+    padded = slot_plan(peers, slot_rows)[0]
 
     def swap(table):
         slots = table.reshape(peers, padded, table.shape[1])
         return lax.all_to_all(slots, "dp", split_axis=0, concat_axis=0, tiled=True).reshape(table.shape)
 
+    if staged:
+        entries, pieces = staged_pieces(enc_norms, dec_norms, masters)
+        sizes = (*enc_norms.shape, *dec_norms.shape)
+        whole, norms_e, norms_d, table, enc_inputs, stored = front(
+            entries, pieces, patches, counts, sizes, HEADS_E
+        )
+        whole = [w.reshape(-1, w.shape[-1]) for w in whole[1:]]
+        table = table.reshape(-1, table.shape[-1])
+    else:
+        norms_e, norms_d, whole = gather_masters(enc_norms, dec_norms, masters)
+    enc_weights, embed, dec_weights = [*whole[:3], whole[4]], whole[3], whole[5:]
+    if not staged:
+        embedded, enc_inputs, stored = encoder(
+            patches, counts, norms_e, norms_d, enc_weights, embed, HEADS_E
+        )
+        table = swap(embedded)
     place_of = source_index // slot_rows * padded + source_index % slot_rows
     index = jnp.where(source_index >= 0, place_of, -1)
     decoded, d_table, g_dec_norms, *dec_grads = decoder(
-        swap(embedded), index, dec_segment, cotangent, norms_d, dec_weights, HEADS_D
+        table, index, dec_segment, cotangent, norms_d, dec_weights, HEADS_D
     )
     d_patches, g_enc_norms, g_shift, *enc_grads = encoder_back(
         enc_inputs, norms_e, enc_weights, embed, swap(d_table), stored, HEADS_E

time: 604 us -> 537 us (0.89)
  Pallas kernels: 479 us -> 446 us
  waiting for transfers between devices: 40 us -> 22.5 us
  local copies, waits for them, and re-layouts: 47.9 us -> 34.6 us
  starting transfers between devices: 20.5 us -> 14.2 us
    pallas_call x2 -> x1, Pallas kernels: 169 us -> 137 us  [front(): pl.pallas_call(functools.partial(front_kernel, entries, head_size, groups...]
    all_to_all x2 -> x1, waiting for transfers between devices: 40 us -> 22.5 us  [swap(): lax.all_to_all(slots, 'dp', split_axis=0, concat_axis=0, tiled=True)]
    unnamed x78 -> x58, local copies, waits for them, and re-layouts: 28.3 us -> 16.5 us
    all_to_all x2 -> x1, starting transfers between devices: 19.9 us -> 13.7 us  [swap(): lax.all_to_all(slots, 'dp', split_axis=0, concat_axis=0, tiled=True)]
  transfers between devices with their start and end apart: 4 -> 3, of which waited for: 2 -> 1; matrix products, arithmetic and copies ran while one was open for 3% -> 4% of each run, Pallas kernels for 0% -> 0%
where the time goes in v3:
time: 537 us; the launch traced here: 529 us
  Pallas kernels  446 us (83%)
  local copies, waits for them, and re-layouts  34.6 us (6%)
  waiting for transfers between devices  22.5 us (4%)
  starting transfers between devices  14.2 us (3%)
  other arithmetic  10.4 us (2%)
    pallas_call x1, Pallas kernels, front(): pl.pallas_call(functools.partial(front_kernel, entries, head_size, groups...  137 us
    pallas_call x1, Pallas kernels, reduce_all(): pl.pallas_call(functools.partial(reduce_kernel, entries), out_shape=[jax....  117 us
    pallas_call x1, Pallas kernels, decoder(): pl.pallas_call(functools.partial(decoder_kernel, head_size, chunk), out_s...  110 us
    pallas_call x1, Pallas kernels, encoder_back(): pl.pallas_call(functools.partial(encoder_back_kernel, head_size, groups,...  82.5 us
    all_to_all x1, waiting for transfers between devices, swap(): lax.all_to_all(slots, 'dp', split_axis=0, concat_axis=0, tiled=True)  22.5 us
    unnamed x58, local copies, waits for them, and re-layouts  16.5 us
    all_to_all x1, starting transfers between devices, swap(): lax.all_to_all(slots, 'dp', split_axis=0, concat_axis=0, tiled=True)  13.7 us
  transfers between devices with their start and end apart: 3, of which 1 were waited for; matrix products, arithmetic and copies ran while one was open for 4% of the time, Pallas kernels for 0%

profile of v3, /device:TPU:0, one launch (start us, length us, event | category | flops | bytes accessed | tf_op | source)
XLA Modules:
  0.0 529.5 jit_solution(10506177432536442901)
XLA Ops:
  0.7 0.9 convert_element_type.48
  1.7 1.0 copy.43
  2.7 1.1 copy.42
  3.8 1.0 convert_bitcast_fusion.1
  5.6 0.7 broadcast_in_dim_reshape.8.index_row
  6.3 1.2 broadcast_in_dim_reshape.9.index_col
  8.1 1.2 reshape.369.seg_col
  9.3 0.6 convert_bitcast_fusion.4.refs_6_
  10.0 0.7 copy.45
  10.7 0.6 convert_bitcast_fusion.2.refs_9_
  11.4 0.7 convert_bitcast_fusion.refs_5_
  12.1 1.0 select_n.81.refs_11_.key_col
  13.5 1.2 pad.34
  14.7 0.9 copy-done.3
  16.0 1.6 pad.37.cot
  18.5 0.7 pad_maximum_fusion.1.refs_4_
  19.1 0.7 fusion.2.refs_2_
  19.8 0.7 fusion.1.refs_1_
  20.6 0.8 fusion.refs_3_
  21.9 137.2 %front.1 = (bf16[4,2,32,512]{3,2,1,0:T(8,128)(2,1)}, bf16[4,2,2,144,768]{4,3,2,1,0:T(8,128)(2,1)}, bf16[4,2,2,48,768]{4,3,2,1,0:T(8,128)(2,1)}, bf16[4,2,2,192,7...) custom-call(bf16[32,128]{1,0:T(8,128)(2,1)} %copy-done.13, ...), custom_call_target="tpu_custom_call" | custom-call | tf_op jit(solution)/shard_map/front/pallas_call | solution.py:1243
  159.2 109.5 %decoder.1 = (f32[2,529,512]{2,1,0:T(8,128)}, bf16[896,512]{1,0:T(8,128)(2,1)}, f32[8,512]{1,0:T(8,128)}, bf16[1536,512]{1,0:T(8,128)(2,1)}, bf16[512,512]{1,0:T...) custom-call(bf16[896,512]{1,0:T(8,128)(2,1)} %bitcast.90, ...), custom_call_target="tpu_custom_call" | custom-call | tf_op jit(solution)/shard_map/decoder/pallas_call | solution.py:700
  268.7 13.7 %all-to-all-start = ((bf16[8,112,512]{2,1,0:T(8,128)(2,1)}), bf16[8,112,512]{2,1,0:T(8,128)(2,1)S(1)}, u32[]{:S(2)}, u32[]{:S(2)}) async-start(bf16[8,112,512]{2,1,0:T(8,128)(2,1)} %bitcast.91), calls=%async_computation | async-start | bytes 1835008 | tf_op jit(solution)/shard_map/all_to_all | solution.py:1306
  282.4 0.7 slice.200
  283.1 22.5 %all-to-all-done = bf16[8,112,512]{2,1,0:T(8,128)(2,1)S(1)} async-done(((bf16[8,112,512]{2,1,0:T(8,128)(2,1)}), bf16[8,112,512]{2,1,0:T(8,128)(2,1)S(1)}, u32[]{:S(2)}, u32[]{:S(2)}) %all-to-all-start) | async-done | bytes 917536 | tf_op jit(solution)/shard_map/all_to_all | solution.py:1306
  305.6 0.6 reshape.348.own_row
  306.6 82.5 %encoder_back.1 = (f32[896,768]{1,0:T(8,128)}, f32[8,768]{1,0:T(8,128)}, f32[8,512]{1,0:T(8,128)}, bf16[2304,768]{1,0:T(8,128)(2,1)}, bf16[768,768]{1,0:T(8,128)...) custom-call(bf16[896,768]{1,0:T(8,128)(2,1)} %bitcast.73, ...), custom_call_target="tpu_custom_call" | custom-call | tf_op jit(solution)/shard_map/encoder_back/pallas_call | solution.py:969
  389.1 0.7 slice.202
  389.8 0.7 slice.201
  391.2 0.8 reshape.359.refs_0_
  392.0 117.2 %reduce_gradients.1 = (f32[32,128]{1,0:T(8,128)}, f32[144,384]{1,0:T(8,128)}, f32[48,384]{1,0:T(8,128)}, f32[192,384]{1,0:T(8,128)}, f32[96,768]{1,0:T(8,128)}, ...) custom-call(bf16[4,2,32,512]{3,2,1,0:T(8,128)(2,1)} %reshape.359.refs, ...), custom_call_target="tpu_custom_call" | custom-call | tf_op jit(solution)/shard_map/reduce_gradients/pallas_call | solution.py:287
  509.2 1.1 constant_dynamic-update-slice_fusion.3
  510.3 0.9 constant_dynamic-update-slice_fusion.2
  511.2 1.0 constant_dynamic-update-slice_fusion.1
  512.2 0.8 constant_dynamic-update-slice_fusion
  513.0 0.9 slice_select_fusion
  513.9 3.0 copy.53
  516.9 1.2 slice.151
  518.1 1.2 slice.154
  519.6 1.7 reshape.357
  521.3 0.8 copy.57
  522.1 1.2 broadcast_select_fusion.1
  523.4 0.7 copy.55
  524.2 0.9 copy.56
  525.1 0.9 copy.54
  526.0 0.6 maximum_bitcast_fusion.3
  526.6 0.7 copy.72
  527.3 0.6 copy.73
  528.6 0.7 copy.75
  (84 shorter events, 5.7 us)
Async XLA Ops:
  0.6 4.9 copy-start.16
  0.7 6.8 %copy-start.17 = (s32[2,529]{1,0:T(2,128)S(1)}, s32[2,529]{1,0:T(2,128)}, u32[]{:S(2)}) copy-start(s32[2,529]{1,0:T(2,128)} %param.26) | copy-start | bytes 12700
  0.7 8.6 %copy-start.19 = (s32[1,8]{1,0:T(1,128)S(1)}, s32[1,8]{1,0:T(1,128)}, u32[]{:S(2)}) copy-start(s32[1,8]{1,0:T(1,128)} %param.25) | copy-start | bytes 100
  0.7 8.6 %copy-start.20 = (f32[1,96]{1,0:T(1,128)S(1)}, f32[1,96]{1,0:T(1,128)}, u32[]{:S(2)}) copy-start(f32[1,96]{1,0:T(1,128)} %param.29) | copy-start | bytes 1156
  0.7 8.6 %copy-start.18 = (f32[2,64]{1,0:T(2,128)S(1)}, f32[2,64]{1,0:T(2,128)}, u32[]{:S(2)}) copy-start(f32[2,64]{1,0:T(2,128)} %param.34) | copy-start | bytes 1540
  0.7 8.6 %copy-start.11 = (f32[128,192]{0,1:T(8,128)S(1)}, f32[128,192]{0,1:T(8,128)}, u32[]{:S(2)}) copy-start(f32[128,192]{0,1:T(8,128)} %param.36) | copy-start | bytes 294916
  0.7 9.3 %copy-start.7 = (f32[128,256]{1,0:T(8,128)S(1)}, f32[128,256]{1,0:T(8,128)}, u32[]{:S(2)}) copy-start(f32[128,256]{1,0:T(8,128)} %param.38) | copy-start | bytes 393220
  0.7 10.0 %copy-start.8 = (f32[512,64]{0,1:T(8,128)S(1)}, f32[512,64]{0,1:T(8,128)}, u32[]{:S(2)}) copy-start(f32[512,64]{0,1:T(8,128)} %param.39) | copy-start | bytes 393220
  1.7 9.7 %copy-start.5 = (f32[768,96]{0,1:T(8,128)S(1)}, f32[768,96]{0,1:T(8,128)}, u32[]{:S(2)}) copy-start(f32[768,96]{0,1:T(8,128)} %param.33) | copy-start | bytes 884740
  4.8 8.3 %copy-start.4 = (bf16[792,768]{1,0:T(8,128)(2,1)S(1)}, bf16[792,768]{1,0:T(8,128)(2,1)}, u32[]{:S(2)}) copy-start(bf16[792,768]{1,0:T(8,128)(2,1)} %param.24) | copy-start | bytes 3649540
  5.0 13.4 %collective-permute-start = (bf16[416,192]{1,0:T(8,128)(2,1)S(1)}, bf16[416,192]{1,0:T(8,128)(2,1)S(1)}, u32[]{:S(2)}, u32[]{:S(2)}) collective-permute-start(bf16[416,192]{1,0:T(8,128)(2,1)S(1)} %dynamic-slice_bitcast_fusion), channel_id=1, source_target_pairs={{0,1},{1,0},{2,3},{3,2},{4,5},{5,4},{6,7},{7,6},{8,9},{9,8},{10,11... | collective-permute-start | bytes 479240 | tf_op jit(solution)/shard_map/ppermute | solution.py:314
  13.4 2.1 copy-start.3
  16.0 1.8 copy-start.14
  17.8 4.1 copy-start.13
  268.7 36.9 %all-to-all-start = ((bf16[8,112,512]{2,1,0:T(8,128)(2,1)}), bf16[8,112,512]{2,1,0:T(8,128)(2,1)S(1)}, u32[]{:S(2)}, u32[]{:S(2)}) async-start(bf16[8,112,512]{2,1,0:T(8,128)(2,1)} %bitcast.91), calls=%async_computation | async-start | bytes 1835008 | tf_op jit(solution)/shard_map/all_to_all | solution.py:1306
  305.6 1.0 copy-start
  509.2 4.7 copy-start.2
  513.9 5.4 %copy-start.1 = (f32[896,768]{1,0:T(8,128)S(1)}, f32[896,768]{1,0:T(8,128)}, u32[]{:S(2)}) copy-start(f32[896,768]{1,0:T(8,128)} %get-tuple-element.126) | copy-start | bytes 8257540
  513.9 8.1 %collective-permute-start.1 = (f32[416,192]{1,0:T(8,128)}, f32[416,192]{1,0:T(8,128)}, u32[]{:S(2)}, u32[]{:S(2)}) collective-permute-start(f32[416,192]{1,0:T(8,128)} %slice_select_fusion), channel_id=1, source_target_pairs={{0,1},{1,0},{2,3},{3,2},{4,5},{5,4},{6,7},{7,6},{8,9},{9,8},{10,11... | collective-permute-start | bytes 958472 | tf_op jit(solution)/shard_map/ppermute | solution.py:325
  519.5 1.7 copy-start.10
  523.3 3.3 copy-start.6
  523.3 4.0 copy-start.12
  523.4 4.6 copy-start.15
  523.4 5.2 copy-start.9

commit v4 on v3

--- a/solution.py
+++ b/solution.py
@@ -80,15 +80,6 @@
 
 def at(z, x, y, c):
     return (z * 2 + x, y * 2 + c)
-
-
-def greet(z, x, y, c):
-    barrier = pltpu.get_barrier_semaphore()
-    peers = [at(lax.rem(z + k, 4), x, y, c) for k in (1, 2, 3)]
-    peers += [at(z, 1 - x, y, c), at(z, x, 1 - y, c), at(z, x, y, 1 - c)]
-    for peer in peers:
-        pl.semaphore_signal(barrier, inc=1, device_id=peer, device_id_type=MESH)
-    pl.semaphore_wait(barrier, len(peers))
 
 
 def send(src, dst, sems, i, k, peer):
@@ -151,20 +142,29 @@
     def lanes(y):
         return pl.ds(pl.multiple_of(y * q, 128), q)
 
-    def pair(ref):
-        return [ref] if e.by_core else [ref.at[:, :, :, pl.ds(k * q, q)] for k in range(2)]
+    def share(core, ref):
+        if len(grad.shape) > 2:
+            into = [ref] if e.by_core else [ref.at[:, :, :, pl.ds(k * q, q)] for k in range(2)]
+            return list(zip(region_pair(e, grad, ALL, ALL, ALL, core), into))
+        found = []
+        for b in range(8):
+            to = ref.at[b // 2, b % 2]
+            if e.by_core:
+                found.append((grad.at[pl.ds(pl.multiple_of((2 * b + core) * part, 16), part), :], to))
+                continue
+            for k in range(2):
+                cols = pl.ds(pl.multiple_of((2 * k + core) * q, 128), q)
+                found.append((grad.at[pl.ds(b * part, part), cols], to.at[:, pl.ds(k * q, q)]))
+        return found
 
     def local():
-        mine = zip(region_pair(e, grad, ALL, ALL, ALL, c), pair(acc))
-        return [
-            pltpu.make_async_copy(src, dst, local_sem.at[i, k]) for k, (src, dst) in enumerate(mine)
-        ]
+        copies = [pltpu.make_async_copy(src, dst, local_sem.at[i]) for src, dst in share(c, acc)]
+        return copies, [pltpu.make_async_copy(acc, acc, local_sem.at[i])]
 
     def first():
-        theirs = zip(region_pair(e, grad, ALL, ALL, ALL, 1 - c), pair(r4))
-        return [
-            send(src, dst, sems, i, k, at(z, x, y, 1 - c)) for k, (src, dst) in enumerate(theirs)
-        ]
+        peer = at(z, x, y, 1 - c)
+        copies = [send(src, dst, sems, i, 0, peer) for src, dst in share(1 - c, r4)]
+        return copies, [send(r4, r4, sems, i, 0, peer)]
 
     def add_first():
         def step(k, carry):
@@ -175,10 +175,11 @@
         lax.fori_loop(0, 8, step, 0)
 
     def second():
-        return [
+        found = [
             send(acc.at[:, :, top, lanes(1 - y)], r3a, sems, i, 2, at(z, x, 1 - y, c)),
             send(acc.at[:, 1 - x, bottom, :], r3b, sems, i, 3, at(z, 1 - x, y, c)),
         ]
+        return found, found
 
     def add_second():
         def step(k, carry):
@@ -194,10 +195,11 @@
         lax.fori_loop(0, 4, step, 0)
 
     def third():
-        return [
+        found = [
             send(acc.at[:, 1 - x, top, lanes(y)], r2a, sems, i, 4, at(z, 1 - x, y, c)),
             send(acc.at[:, x, bottom, lanes(1 - y)], r2b, sems, i, 5, at(z, x, 1 - y, c)),
         ]
+        return found, found
 
     def add_third():
         def step(k, carry):
@@ -218,7 +220,7 @@
             found.append(
                 send(acc.at[there, x, :, lanes(y)], r1.at[k - 1], sems, i, 5 + k, at(there, x, y, c))
             )
-        return found
+        return found, found
 
     def add_fourth():
         total = acc[z, x, :, lanes(y)].astype(F32)
@@ -239,67 +241,6 @@
         (4, e.part - e.cut, e.q),
         (3, e.part, e.q),
     ]
-
-
-def reduce_kernel(entries, *refs):
-    n = len(entries)
-    grads, outs = refs[:n], refs[n : 2 * n]
-    bufs = [refs[2 * n + 7 * i : 2 * n + 7 * i + 7] for i in range(n)]
-    send_sem, recv_sem, local_sem = refs[9 * n :]
-    sems = (send_sem, recv_sem)
-    z, x, y, c = place()
-    plans = [
-        reduce_stages(e, i, grads[i], outs[i], bufs[i], sems, local_sem)
-        for i, e in enumerate(entries)
-    ]
-    locals_ = [plan[0]() for plan in plans]
-    for copies in locals_:
-        for copy in copies:
-            copy.start()
-    greet(z, x, y, c)
-    moving = {}
-    for t in range(n + 4):
-        for stage in (4, 3, 2, 1, 0):
-            i = t - stage
-            if not 0 <= i < n:
-                continue
-            if stage > 0:
-                for copy in moving[i, stage - 1]:
-                    copy.wait_recv()
-                if stage == 1:
-                    for copy in locals_[i]:
-                        copy.wait()
-                plans[i][1][stage - 1][1]()
-            if stage < 4:
-                moving[i, stage] = plans[i][1][stage][0]()
-                for copy in moving[i, stage]:
-                    copy.start()
-    for i in range(n):
-        for stage in range(4):
-            for copy in moving[i, stage]:
-                copy.wait_send()
-
-
-def reduce_all(entries, grads):
-    any_space = pl.BlockSpec(memory_space=pl.ANY)
-    n = len(entries)
-    scratch = [pltpu.VMEM(shape, BF16) for e in entries for shape in reduce_buffers(e)]
-    return pl.pallas_call(
-        functools.partial(reduce_kernel, entries),
-        out_shape=[jax.ShapeDtypeStruct((e.part, e.q), F32) for e in entries],
-        in_specs=[any_space] * n,
-        out_specs=[pl.BlockSpec(memory_space=pltpu.VMEM)] * n,
-        scratch_shapes=scratch
-        + [
-            pltpu.SemaphoreType.DMA((n, 9)),
-            pltpu.SemaphoreType.DMA((n, 9)),
-            pltpu.SemaphoreType.DMA((n, 2)),
-        ],
-        compiler_params=pltpu.CompilerParams(
-            collective_id=1, has_side_effects=True, vmem_limit_bytes=56 << 20
-        ),
-        name="reduce_gradients",
-    )(*grads)
 
 
 CORE_SWAP = [(0, 1), (1, 0), (2, 3), (3, 2)]
@@ -364,38 +305,24 @@
     return entries, [small] + pieces
 
 
-def reduce_masters(staged, g_enc_norms, g_dec_norms, grads):
-    if not staged:
-        def owner(value, rows, lanes):
-            part = lax.psum_scatter(value.astype(BF16), "fsdp", scatter_dimension=lanes, tiled=True)
-            return sum_at_owner(part, "dp", rows)
-
-        return (
-            owner(g_enc_norms, 1, 0),
-            owner(g_dec_norms, 1, 0),
-            [owner(g, 0, 1).T for g in grads],
-        )
-    entries = [entry_of(g.shape[0] // 8, g.shape[1]) for g in grads]
-    values = [g.astype(BF16).reshape(e.whole) for g, e in zip(grads, entries)]
-    half = NORM_ROWS // 2
-    tiles = jnp.zeros((8, NORM_ROWS, 4, 128), BF16)
-    for start, rows in ((0, g_enc_norms), (half, g_dec_norms)):
-        n, width = rows.shape[0] // 4, rows.shape[1] // 8
-        part = rows.astype(BF16).reshape(4, n, 8, width).transpose(2, 1, 0, 3)
-        tiles = tiles.at[:, start : start + n, :, :width].set(part)
-    small = entry_of(NORM_ROWS, 512)
-    sums = reduce_all([small] + entries, [tiles.reshape(small.whole)] + values)
-    blocks = list(sums[1:])
-    cores = [k for k, e in enumerate(entries) if e.by_core]
+def reduce_masters(g_enc_norms, g_dec_norms, grads):
+    def owner(value, rows, lanes):
+        part = lax.psum_scatter(value.astype(BF16), "fsdp", scatter_dimension=lanes, tiled=True)
+        return sum_at_owner(part, "dp", rows)
+
+    return (
+        owner(g_enc_norms, 1, 0),
+        owner(g_dec_norms, 1, 0),
+        [owner(g, 0, 1).T for g in grads],
+    )
+
+
+def own_blocks(sums, like):
+    blocks = list(sums)
+    cores = [k for k, b in enumerate(blocks) if b.shape[0] != like[k].shape[1]]
     for k, b in zip(cores, pieces_to_halves([blocks[k] for k in cores])):
         blocks[k] = b
-    n_enc, w_enc = g_enc_norms.shape[0] // 4, g_enc_norms.shape[1] // 8
-    n_dec, w_dec = g_dec_norms.shape[0] // 4, g_dec_norms.shape[1] // 8
-    return (
-        sums[0][:n_enc, :w_enc],
-        sums[0][half : half + n_dec, :w_dec],
-        [b.T for b in blocks],
-    )
+    return [b.T for b in blocks]
 
 
 def nn(a, b):
@@ -511,7 +438,8 @@
         off(t).wait()
 
 
-def decoder_kernel(
+def decoder_body(
+    hooks,
     head_size,
     chunk,
     table,
@@ -544,6 +472,7 @@
     e_two,
     e_one,
     bias,
+    d_x,
     stage,
     stage_wide,
     sem,
@@ -556,7 +485,6 @@
     per_tile = LANES // head_size
     gain = [norms[k : k + 1, :].astype(F32) for k in range(8)]
     g_norms[...] = jnp.zeros_like(g_norms)
-    d_x = cot
 
     def start(i):
         r = rows_of(i, chunk)
@@ -634,8 +562,11 @@
     outer_loop(rows // chunk, middle)
 
     weight_sum(g_down, e_two, act, stage_wide, sem)
+    hooks.summed(0)
     weight_sum(g_up, d_up, h_two, stage, sem)
+    hooks.summed(1)
     weight_sum(g_out, e_one, mixed, stage, sem)
+    hooks.summed(2)
 
     def mix_back(i):
         r = rows_of(i, chunk)
@@ -644,22 +575,20 @@
     outer_loop(rows // chunk, mix_back)
     d_qkv = act
 
-    def attend_back(g):
+    for g in range(groups):
         bias[...] = mask_bias(seg_row[g], seg_col[rows_of(g, n), :])
         r = rows_of(g, n)
 
-        def one(t):
+        def one(t, g=g, r=r):
             q, k, v = [qkv[r, lane_tile(t + j * tiles)] for j in range(3)]
             logs = [totals[g * tiles + t, h : h + 1, :] for h in range(per_tile)]
             found = attend_tile_back(q, k, v, mixed[r, lane_tile(t)], bias[...], logs, head_size)
             for j in range(3):
                 d_qkv[r, lane_tile(t + j * tiles)] = found[j].astype(BF16)
 
-        outer_loop(tiles, one)
-
-    outer_loop(groups, attend_back)
-
-    weight_sum(g_qkv, d_qkv.at[:, : 3 * width], h_one, stage, sem)
+        for half in range(2):
+            some(half * tiles // 2, (half + 1) * tiles // 2, one)
+            hooks.pause(2 * g + half)
 
     def finish(i):
         g, j = i // per_group, lax.rem(i, per_group)
@@ -675,16 +604,107 @@
 
     outer_loop(rows // chunk, finish)
 
+    slots, slot_rows, _ = d_table.shape
+
     def back(s):
-        sr = rows_of(s, 128)
-        slots = lax.broadcasted_iota(jnp.int32, (128, rows), 0) + s * 128
-        chosen = jnp.where(slots == index_row[...], 1.0, 0.0).astype(BF16)
-        d_table[sr, :] = nn(chosen, e_two[...]).astype(BF16)
-
-    outer_loop(table.shape[0] // 128, back)
-
-
-def decoder(table, index, segment, cotangent, norms, weights, heads):
+        line = lax.broadcasted_iota(jnp.int32, (slot_rows, rows), 0) + s * slot_rows
+        chosen = jnp.where(line == index_row[...], 1.0, 0.0).astype(BF16)
+        d_table[s] = nn(chosen, e_two[...]).astype(BF16)
+
+    hooks.slots(back, slots)
+    weight_sum(g_qkv, d_qkv.at[:, : 3 * width], h_one, stage, sem)
+    hooks.end()
+
+
+def some(lo, hi, body):
+    def step(i, carry):
+        body(i)
+        return carry
+
+    lax.fori_loop(lo, hi, step, 0)
+
+
+class NoHooks:
+    def summed(self, k):
+        pass
+
+    def pause(self, k):
+        pass
+
+    def slots(self, body, count):
+        outer_loop(count, body)
+
+    def end(self):
+        pass
+
+
+class MiddleHooks:
+    def __init__(self, reducer, d_table, returned, swap_send, swap_recv, swap_local):
+        self.reducer = reducer
+        self.d_table, self.returned = d_table, returned
+        self.swap = (swap_send, swap_recv, swap_local)
+
+    def summed(self, k):
+        self.reducer.begin(k)
+        for i in range(k):
+            self.reducer.step(i)
+
+    def pause(self, k):
+        for i in range(3):
+            self.reducer.step(i)
+
+    def slots(self, body, count):
+        z, x, y, c = place()
+        d, f = z * 2 + x, y * 2 + c
+        send_sem, recv_sem, local_sem = self.swap
+        for s in range(count):
+            some(s, s + 1, body)
+
+            @pl.when(s != d)
+            def _(s=s):
+                send_slot(self.d_table, self.returned, s, d, send_sem, recv_sem, f).start()
+
+            @pl.when(s == d)
+            def _(s=s):
+                pltpu.make_async_copy(
+                    self.d_table.at[s], self.returned.at[s], local_sem.at[0]
+                ).start()
+
+    def end(self):
+        z, x, y, c = place()
+        for i in range(3):
+            self.reducer.finish(i)
+        finish_swap(self.d_table, self.returned, z * 2 + x, *self.swap, y * 2 + c)
+        self.reducer.drain()
+
+
+def decoder_kernel(head_size, chunk, *refs):
+    decoder_body(NoHooks(), head_size, chunk, *refs)
+
+
+def middle_kernel(entries, head_size, chunk, *refs):
+    ins, refs = refs[:11], refs[11:]
+    decoded, returned, g_norms, *refs = refs
+    grads, refs = refs[:4], refs[4:]
+    outs, refs = refs[:3], refs[3:]
+    scratch, refs = refs[:16], refs[16:]
+    d_table, *refs = refs
+    bufs, refs = refs[:21], refs[21:]
+    send_sem, recv_sem, local_sem, swap_send, swap_recv, swap_local = refs
+    z, x, y, c = place()
+    meet(z, x, y, c)
+    by_entry = [grads[3], grads[2], grads[1]]
+    reducer = Reducer(
+        [
+            reduce_stages(e, i, by_entry[i], outs[i], bufs[7 * i : 7 * i + 7], (send_sem, recv_sem), local_sem)
+            for i, e in enumerate(entries)
+        ]
+    )
+    hooks = MiddleHooks(reducer, d_table, returned, swap_send, swap_recv, swap_local)
+    decoder_body(hooks, head_size, chunk, *ins, decoded, d_table, g_norms, *grads, *scratch)
+
+
+def decoder(staged, table, index, segment, cotangent, norms, weights, heads):
     groups, real, width = cotangent.shape
     n = -(-real // 32) * 32
     chunk = n // 2
@@ -697,36 +717,26 @@
     tiles = width // LANES
     ff = weights[2].shape[0]
     vm = pl.BlockSpec(memory_space=pltpu.VMEM)
-    return pl.pallas_call(
-        functools.partial(decoder_kernel, head_size, chunk),
-        out_shape=[
-            jax.ShapeDtypeStruct(cotangent.shape, F32),
-            jax.ShapeDtypeStruct(table.shape, BF16),
-            jax.ShapeDtypeStruct((8, width), F32),
-        ]
-        + [jax.ShapeDtypeStruct(w.shape, BF16) for w in weights],
-        in_specs=[vm] * 11,
-        out_specs=[vm] * 3 + [pl.BlockSpec(memory_space=pl.ANY)] * 4,
-        scratch_shapes=[
-            pltpu.VMEM((rows, width), F32),
-            pltpu.VMEM((rows, width), BF16),
-            pltpu.VMEM((rows, 3 * width), BF16),
-            pltpu.VMEM((rows, width), BF16),
-            pltpu.VMEM((groups * tiles, LANES // head_size, n), F32),
-            pltpu.VMEM((rows, width), BF16),
-            pltpu.VMEM((rows, ff), BF16),
-            pltpu.VMEM((chunk, ff), BF16),
-            pltpu.VMEM((rows, ff), BF16),
-            pltpu.VMEM((rows, width), BF16),
-            pltpu.VMEM((rows, width), BF16),
-            pltpu.VMEM((n, n), F32),
-            pltpu.VMEM((2, 256, width), BF16),
-            pltpu.VMEM((2, LANES, ff), BF16),
-            pltpu.SemaphoreType.DMA((2,)),
-        ],
-        compiler_params=pltpu.CompilerParams(vmem_limit_bytes=60 << 20),
-        name="decoder",
-    )(
+    hbm = pl.BlockSpec(memory_space=pl.ANY)
+    scratch = [
+        pltpu.VMEM((rows, width), F32),
+        pltpu.VMEM((rows, width), BF16),
+        pltpu.VMEM((rows, 3 * width), BF16),
+        pltpu.VMEM((rows, width), BF16),
+        pltpu.VMEM((groups * tiles, LANES // head_size, n), F32),
+        pltpu.VMEM((rows, width), BF16),
+        pltpu.VMEM((rows, ff), BF16),
+        pltpu.VMEM((chunk, ff), BF16),
+        pltpu.VMEM((rows, ff), BF16),
+        pltpu.VMEM((rows, width), BF16),
+        pltpu.VMEM((rows, width), BF16),
+        pltpu.VMEM((n, n), F32),
+        pltpu.VMEM(cot.shape, F32),
+        pltpu.VMEM((2, 256, width), BF16),
+        pltpu.VMEM((2, LANES, ff), BF16),
+        pltpu.SemaphoreType.DMA((2,)),
+    ]
+    args = (
         table,
         index[:, None],
         index[None, :],
@@ -736,6 +746,38 @@
         norms,
         *weights,
     )
+    slots = (8, table.shape[0] // 8, width)
+    shapes = [
+        jax.ShapeDtypeStruct(cotangent.shape, F32),
+        jax.ShapeDtypeStruct(slots, BF16),
+        jax.ShapeDtypeStruct((8, width), F32),
+    ] + [jax.ShapeDtypeStruct(w.shape, BF16) for w in weights]
+    if not staged:
+        return pl.pallas_call(
+            functools.partial(decoder_kernel, head_size, chunk),
+            out_shape=shapes,
+            in_specs=[vm] * 11,
+            out_specs=[vm] * 3 + [hbm] * 4,
+            scratch_shapes=scratch,
+            compiler_params=pltpu.CompilerParams(vmem_limit_bytes=60 << 20),
+            name="decoder",
+        )(*args)
+    entries = [entry_of(w.shape[0] // 8, w.shape[1]) for w in (weights[3], weights[2], weights[1])]
+    sem = pltpu.SemaphoreType.DMA
+    return pl.pallas_call(
+        functools.partial(middle_kernel, entries, head_size, chunk),
+        out_shape=shapes + [jax.ShapeDtypeStruct((e.part, e.q), F32) for e in entries],
+        in_specs=[vm] * 11,
+        out_specs=[vm, hbm, vm] + [hbm] * 4 + [vm] * 3,
+        scratch_shapes=scratch
+        + [pltpu.VMEM(slots, BF16)]
+        + [pltpu.VMEM(shape, BF16) for e in entries for shape in reduce_buffers(e)]
+        + [sem((3, 9)), sem((3, 9)), sem((3,)), sem((8,)), sem((8,)), sem((1,))],
+        compiler_params=pltpu.CompilerParams(
+            collective_id=1, has_side_effects=True, vmem_limit_bytes=62 << 20
+        ),
+        name="middle",
+    )(*args)
 
 
 def encoder_kernel(
@@ -1064,12 +1106,7 @@
         locals_.append(local())
     for copy in locals_:
         copy.start()
-    barrier = pltpu.get_barrier_semaphore()
-    peers = [(lax.rem(d + k, 8), y * 2 + c) for k in range(1, 8)]
-    peers += [at(z, x, 1 - y, c), at(z, x, y, 1 - c)]
-    for peer in peers:
-        pl.semaphore_signal(barrier, inc=1, device_id=peer, device_id_type=MESH)
-    pl.semaphore_wait(barrier, len(peers))
+    meet(z, x, y, c)
     ticker = Ticker(plans, locals_)
 
     def load(i):
@@ -1084,13 +1121,6 @@
         copy = pltpu.make_async_copy(kept[k], kept_out[k], keep_sem.at[k])
         copy.start()
         keeping.append(copy)
-
-    def some(lo, hi, body):
-        def step(i, carry):
-            body(i)
-            return carry
-
-        lax.fori_loop(lo, hi, step, 0)
 
     ticker.tick(5)
     copies = [load(0), load(1)]
@@ -1275,6 +1305,288 @@
     return whole, norms_e, norms_d, table, (x, keys, own), [qkv, totals, mixed, x_one, act, slope, sent]
 
 
+class Reducer:
+    def __init__(self, plans):
+        self.plans, self.stage, self.moving, self.waits = plans, {}, [], {}
+
+    def start(self, i, copies, waits):
+        for copy in copies:
+            copy.start()
+        self.waits[i] = waits
+        self.moving += waits
+
+    def begin(self, i):
+        local, stages = self.plans[i]
+        copies, self.local_waits = local()
+        for copy in copies:
+            copy.start()
+        self.waits[i, 0] = self.local_waits
+        self.start(i, *stages[0][0]())
+        self.stage[i] = 0
+
+    def step(self, i):
+        k = self.stage[i]
+        if k == 4:
+            return
+        _, stages = self.plans[i]
+        for copy in self.waits[i]:
+            copy.wait_recv()
+        if k == 0:
+            for copy in self.waits[i, 0]:
+                copy.wait()
+        stages[k][1]()
+        if k < 3:
+            self.start(i, *stages[k + 1][0]())
+        self.stage[i] = k + 1
+
+    def finish(self, i):
+        while self.stage[i] < 4:
+            self.step(i)
+
+    def drain(self):
+        for copy in self.moving:
+            copy.wait_send()
+
+
+def meet(z, x, y, c):
+    d = z * 2 + x
+    barrier = pltpu.get_barrier_semaphore()
+    peers = [(lax.rem(d + k, 8), y * 2 + c) for k in range(1, 8)]
+    peers += [at(z, x, 1 - y, c), at(z, x, y, 1 - c)]
+    for peer in peers:
+        pl.semaphore_signal(barrier, inc=1, device_id=peer, device_id_type=MESH)
+    pl.semaphore_wait(barrier, len(peers))
+
+
+def gather_norms(g, start, count, part, tiles):
+    width = 8 * part
+    lane = lax.broadcasted_iota(jnp.int32, (width, LANES), 1)
+    line = lax.broadcasted_iota(jnp.int32, (width, LANES), 0)
+    rows = g.astype(BF16)
+    for d in range(8):
+        put = jnp.where((line == lane + d * part) & (lane < part), 1.0, 0.0).astype(BF16)
+        cut = nn(rows, put).astype(BF16)
+        for f in range(4):
+            tiles[d // 2, d % 2, start : start + count, f * LANES : (f + 1) * LANES] = cut[
+                f * count : (f + 1) * count
+            ]
+
+
+def rear_kernel(entries, head_size, groups, chunk, sizes, *refs):
+    patches, key_col, own_row, norms, g_dec, g_dec_qkv, *refs = refs
+    weights, refs = refs[:5], refs[5:]
+    d_table, *refs = refs
+    stored, refs = refs[:7], refs[7:]
+    d_patches, *refs = refs
+    g_embed, g_down, g_up, g_out, g_qkv, *refs = refs
+    n_in = len(entries)
+    outs, refs = refs[:n_in], refs[n_in:]
+    up_v, down_v, embed_v, act, slope, mixed, sent, e_two, e_one, d_emb, totals, small, *refs = refs
+    stage, stage_wide, sem, g_norms, g_shift, *refs = refs
+    bufs, refs = refs[: 7 * n_in], refs[7 * n_in :]
+    send_sem, recv_sem, local_sem, load_sem = refs
+    w_qkv, w_out, w_up, w_down, w_embed = weights
+    s_qkv, s_totals, s_mixed, s_one, s_act, s_slope, s_sent = stored
+    rows, width = patches.shape
+    n = rows // groups
+    tiles = width // LANES
+    per_tile = LANES // head_size
+    wide = 3 * width
+    z, x, y, c = place()
+    loads = {}
+
+    def load(k, src, dst):
+        loads[k] = pltpu.make_async_copy(src, dst, load_sem.at[k])
+        loads[k].start()
+
+    load(0, w_embed, embed_v)
+    load(1, d_table, d_emb)
+    load(2, s_act, act)
+    load(3, s_sent, sent)
+    load(4, w_down, down_v)
+    load(5, s_slope, slope)
+    load(6, w_up, up_v)
+    load(7, s_one, d_patches)
+    load(8, s_mixed, mixed)
+    load(9, s_totals, totals)
+    small[...] = jnp.zeros_like(small)
+    g_norms[...] = jnp.zeros_like(g_norms)
+    g_shift[...] = jnp.zeros_like(g_shift)
+    meet(z, x, y, c)
+    grads = [g_dec_qkv, g_down, g_embed, g_up, g_out, g_qkv, small]
+    reducer = Reducer(
+        [
+            reduce_stages(e, i, grads[i], outs[i], bufs[7 * i : 7 * i + 7], (send_sem, recv_sem), local_sem)
+            for i, e in enumerate(entries)
+        ]
+    )
+    reducer.begin(0)
+    gain = [norms[k : k + 1, :] for k in range(4)]
+
+    def enter(i):
+        r = rows_of(i, chunk)
+        g_shift[0:1, :] += column_sum(d_emb[r, :].astype(F32))
+        e_two[r, :] = nn(d_emb[r, :], embed_v[...]).astype(BF16)
+
+    loads[0].wait()
+    loads[1].wait()
+    outer_loop(rows // chunk, enter)
+    loads[2].wait()
+    weight_sum(g_down, e_two, act, stage_wide, sem)
+    reducer.begin(1)
+    reducer.step(0)
+    loads[3].wait()
+    weight_sum(g_embed, d_emb, sent, stage, sem)
+    reducer.begin(2)
+    reducer.step(1)
+    reducer.step(0)
+    h_two = sent
+    step = 512
+
+    def middle(i):
+        r = rows_of(i, chunk)
+        e = e_two[r, :]
+        for t in range(slope.shape[1] // step):
+            cols = slice(t * step, (t + 1) * step)
+            d_act = nn(e, down_v[:, cols])
+            slope[r, cols] = (d_act * slope[r, cols].astype(F32)).astype(BF16)
+        d_h = nn(slope[r, :], up_v[...])
+        hat, scale = unit(d_patches[r, :])
+        h_two[r, :] = (hat * gain[2] + gain[3]).astype(BF16)
+        g_norms[2:3, :] += column_sum(d_h * hat)
+        g_norms[3:4, :] += column_sum(d_h)
+        d_one = e.astype(F32) + unit_back(d_h * gain[2], hat, scale)
+        d_patches[r, :] = d_one
+        e_one[r, :] = d_one.astype(BF16)
+
+    for k in range(4, 8):
+        loads[k].wait()
+    for i, then in enumerate(((2, 0), (0, 2), (1, 2), (2,))):
+        some(i, i + 1, middle)
+        for k in then:
+            reducer.step(k)
+    load(10, w_qkv, up_v.at[:wide, :])
+    load(11, w_out, up_v.at[wide:, :])
+    weight_sum(g_up, slope, h_two, stage, sem)
+    reducer.begin(3)
+    reducer.step(1)
+    qkv = slope.at[:, :wide]
+    load(12, s_qkv, qkv)
+    loads[8].wait()
+    loads[9].wait()
+    weight_sum(g_out, e_one, mixed, stage, sem)
+    reducer.begin(4)
+
+    def mix_back(i):
+        r = rows_of(i, chunk)
+        mixed[r, :] = nn(e_one[r, :], up_v[wide:, :]).astype(BF16)
+        hat, _ = unit(patches[r, :].astype(F32))
+        e_two[r, :] = (hat * gain[0] + gain[1]).astype(BF16)
+
+    loads[11].wait()
+    outer_loop(rows // chunk, mix_back)
+    h_one = e_two
+    reducer.step(3)
+    reducer.step(4)
+    loads[12].wait()
+
+    def attend_back(g):
+        r = rows_of(g, n)
+        bias = mask_bias(own_row[g], key_col[r, :])
+        for t in range(tiles):
+            cols = [slice((t + j * tiles) * LANES, (t + j * tiles + 1) * LANES) for j in range(3)]
+            q, k, v = [slope[r, col] for col in cols]
+            logs = [totals[g, t * per_tile + h : t * per_tile + h + 1, :] for h in range(per_tile)]
+            found = attend_tile_back(q, k, v, mixed[r, cols[0]], bias, logs, head_size)
+            for j in range(3):
+                act[r, cols[j]] = found[j].astype(BF16)
+
+    some(0, groups // 2, attend_back)
+    reducer.step(1)
+    some(groups // 2, groups, attend_back)
+    reducer.step(4)
+    reducer.step(3)
+    weight_sum(g_qkv, act.at[:, :wide], h_one, stage, sem)
+    reducer.begin(5)
+    reducer.step(4)
+    reducer.step(3)
+    loads[10].wait()
+
+    def finish(i):
+        r = rows_of(i, chunk)
+        d_h = nn(act[r, :wide], up_v[:wide, :])
+        hat, scale = unit(patches[r, :].astype(F32))
+        g_norms[0:1, :] += column_sum(d_h * hat)
+        g_norms[1:2, :] += column_sum(d_h)
+        d_patches[r, :] += unit_back(d_h * gain[0], hat, scale)
+
+    some(0, 2, finish)
+    reducer.step(5)
+    some(2, 4, finish)
+    gather_norms(g_norms[0:4, :], 0, sizes[0], sizes[1], small)
+    line = lax.broadcasted_iota(jnp.int32, g_dec.shape, 0)
+    gather_norms(jnp.where(line == 7, g_shift[0:1, :], g_dec[...]), NORM_ROWS // 2, sizes[2], sizes[3], small)
+    reducer.begin(6)
+    reducer.step(4)
+    reducer.step(6)
+    reducer.step(5)
+    reducer.step(6)
+    reducer.step(3)
+    reducer.step(6)
+    for i in range(n_in):
+        reducer.finish(i)
+    reducer.drain()
+
+
+def rear(rows_in, norms, g_dec, g_dec_qkv, weights, embed, d_table, stored, sizes):
+    x, keys, own = rows_in
+    rows, width = x.shape
+    groups, _, n = own.shape
+    head_size = width // HEADS_E
+    ff = weights[2].shape[0]
+    first = (8 * g_dec_qkv.shape[2], g_dec_qkv.shape[3])
+    shapes = [first, weights[3].shape, embed.shape, weights[2].shape, weights[1].shape, weights[0].shape]
+    entries = [entry_of(s[0] // 8, s[1]) for s in shapes] + [entry_of(NORM_ROWS, 512)]
+    vm, hbm = pl.BlockSpec(memory_space=pltpu.VMEM), pl.BlockSpec(memory_space=pl.ANY)
+    sem = pltpu.SemaphoreType.DMA
+    n_in = len(entries)
+    totals = stored[1]
+    found = pl.pallas_call(
+        functools.partial(rear_kernel, entries, head_size, groups, rows // 4, sizes),
+        out_shape=[jax.ShapeDtypeStruct((rows, width), F32)]
+        + [jax.ShapeDtypeStruct(s, BF16) for s in (shapes[2], shapes[1], *shapes[3:])]
+        + [jax.ShapeDtypeStruct((e.part, e.q), F32) for e in entries],
+        in_specs=[vm] * 5 + [hbm] * 14,
+        out_specs=[vm] + [hbm] * 5 + [vm] * n_in,
+        scratch_shapes=[
+            pltpu.VMEM(weights[2].shape, BF16),
+            pltpu.VMEM(weights[3].shape, BF16),
+            pltpu.VMEM(embed.shape, BF16),
+            pltpu.VMEM((rows, ff), BF16),
+            pltpu.VMEM((rows, ff), BF16),
+            pltpu.VMEM((rows, width), BF16),
+            pltpu.VMEM((rows, width), BF16),
+            pltpu.VMEM((rows, width), BF16),
+            pltpu.VMEM((rows, width), BF16),
+            pltpu.VMEM(d_table.shape, BF16),
+            pltpu.VMEM(totals.shape, F32),
+            pltpu.VMEM(entries[-1].whole, BF16),
+            pltpu.VMEM((2, 256, width), BF16),
+            pltpu.VMEM((2, LANES, ff), BF16),
+            sem((2,)),
+            pltpu.VMEM((8, width), F32),
+            pltpu.VMEM((8, embed.shape[0]), F32),
+        ]
+        + [pltpu.VMEM(shape, BF16) for e in entries for shape in reduce_buffers(e)]
+        + [sem((n_in, 9)), sem((n_in, 9)), sem((n_in,)), sem((13,))],
+        compiler_params=pltpu.CompilerParams(
+            collective_id=2, has_side_effects=True, vmem_limit_bytes=63 << 20
+        ),
+        name="rear",
+    )(x, keys, own, norms, g_dec, g_dec_qkv, *weights, embed, d_table, *stored)
+    return found[0], found[6:]
+
+
 def per_device(
     staged,
     patches,
@@ -1323,16 +1635,47 @@
         table = swap(embedded)
     place_of = source_index // slot_rows * padded + source_index % slot_rows
     index = jnp.where(source_index >= 0, place_of, -1)
-    decoded, d_table, g_dec_norms, *dec_grads = decoder(
-        table, index, dec_segment, cotangent, norms_d, dec_weights, HEADS_D
-    )
-    d_patches, g_enc_norms, g_shift, *enc_grads = encoder_back(
-        enc_inputs, norms_e, enc_weights, embed, swap(d_table), stored, HEADS_E
-    )
-    g_dec_norms = jnp.concatenate([g_dec_norms[:7], g_shift[:1]], axis=0)
-    s_enc_norms, s_dec_norms, sums = reduce_masters(
-        staged, g_enc_norms[:4], g_dec_norms, [*enc_grads, *dec_grads]
-    )
+    if staged:
+        decoded, d_table, g_dec_norms, g_qkv, _, _, _, s_down, s_up, s_out = decoder(
+            True, table, index, dec_segment, cotangent, norms_d, dec_weights, HEADS_D
+        )
+        e = entry_of(g_qkv.shape[0] // 8, g_qkv.shape[1])
+        d_patches, sums = rear(
+            enc_inputs,
+            norms_e,
+            g_dec_norms,
+            g_qkv.reshape(e.whole),
+            enc_weights,
+            embed,
+            d_table.reshape(table.shape),
+            stored,
+            sizes,
+        )
+        s_qkv, e_down, s_embed, e_up, e_out, e_qkv, small = sums
+        half = NORM_ROWS // 2
+        s_enc_norms = small[: sizes[0], : sizes[1]]
+        s_dec_norms = small[half : half + sizes[2], : sizes[3]]
+        sums = own_blocks(
+            [e_qkv, e_out, e_up, e_down, s_embed, s_qkv, s_out, s_up, s_down],
+            [enc_qkv, enc_out, enc_up, enc_down, dec_embed, dec_qkv, dec_out, dec_up, dec_down],
+        )
+    else:
+        decoded, d_table, g_dec_norms, *dec_grads = decoder(
+            False, table, index, dec_segment, cotangent, norms_d, dec_weights, HEADS_D
+        )
+        d_patches, g_enc_norms, g_shift, *enc_grads = encoder_back(
+            enc_inputs,
+            norms_e,
+            enc_weights,
+            embed,
+            swap(d_table.reshape(table.shape)),
+            stored,
+            HEADS_E,
+        )
+        g_dec_norms = jnp.concatenate([g_dec_norms[:7], g_shift[:1]], axis=0)
+        s_enc_norms, s_dec_norms, sums = reduce_masters(
+            g_enc_norms[:4], g_dec_norms, [*enc_grads, *dec_grads]
+        )
     d_patches = d_patches.reshape(peers, padded, width)[:, :slot_rows]
     return (
         decoded,

time: 537 us -> 462 us (0.86)
  Pallas kernels: 446 us -> 411 us
  waiting for transfers between devices: 22.5 us -> 0.01 us
  starting transfers between devices: 14.2 us -> 0.52 us
    pallas_call x3 -> x2, Pallas kernels: 309 us -> 274 us  [the longest x1 139 us: decoder(): pl.pallas_call(functools.partial(middle_kernel, entries, head_size, chunk...]
    all_to_all x1 -> x0, waiting for transfers between devices: 22.5 us -> none  [swap(): lax.all_to_all(slots, 'dp', split_axis=0, concat_axis=0, tiled=True)]
    all_to_all x1 -> x0, starting transfers between devices: 13.7 us -> none  [swap(): lax.all_to_all(slots, 'dp', split_axis=0, concat_axis=0, tiled=True)]
    unnamed x58 -> x54, local copies, waits for them, and re-layouts: 16.5 us -> 16.9 us
  transfers between devices with their start and end apart: 3 -> 2, of which waited for: 1 -> 0; matrix products, arithmetic and copies ran while one was open for 4% -> 5% of each run, Pallas kernels for 0% -> 0%
where the time goes in v4:
time: 462 us; the launch traced here: 455 us
  Pallas kernels  411 us (89%)
  local copies, waits for them, and re-layouts  31.6 us (7%)
  other arithmetic  10.4 us (2%)
    pallas_call x1, Pallas kernels, decoder(): pl.pallas_call(functools.partial(middle_kernel, entries, head_size, chunk...  139 us
    pallas_call x1, Pallas kernels, front(): pl.pallas_call(functools.partial(front_kernel, entries, head_size, groups...  137 us
    pallas_call x1, Pallas kernels, rear(): pl.pallas_call(functools.partial(rear_kernel, entries, head_size, groups,...  136 us
    unnamed x54, local copies, waits for them, and re-layouts  16.9 us
  transfers between devices with their start and end apart: 2, of which 0 were waited for; matrix products, arithmetic and copies ran while one was open for 5% of the time, Pallas kernels for 0%

profile of v4, /device:TPU:0, one launch (start us, length us, event | category | flops | bytes accessed | tf_op | source)
XLA Modules:
  0.0 455.5 jit_solution(1918377688870154176)
XLA Ops:
  0.7 0.9 convert_element_type.42
  1.6 1.0 convert_bitcast_fusion.1
  2.8 1.1 copy.41
  3.9 1.1 copy.40
  5.1 0.5 collective-permute-start
  5.7 1.2 broadcast_in_dim_reshape.9.refs_1_
  6.9 0.7 broadcast_in_dim_reshape.8.refs_2_
  7.5 1.2 reshape.244.refs_3_
  8.8 0.6 broadcast_in_dim.25.refs_4_
  9.4 0.7 convert_bitcast_fusion.refs_5_
  10.1 0.6 convert_bitcast_fusion.4.refs_6_
  10.7 0.7 copy.43
  11.5 0.6 convert_bitcast_fusion.2.refs_9_
  12.1 0.4 reshape.225
  12.5 1.2 pad.25
  13.7 1.0 select_n.81.refs_11_.refs_1_
  14.7 2.0 copy.45
  16.8 1.6 pad.28.refs_5_
  18.4 0.2 scatter.9.refs_0_
  18.6 0.6 convert_bitcast_fusion.5.refs_7_
  19.2 0.7 fusion.1.refs_1_
  20.0 0.7 fusion.2.refs_2_
  20.7 0.8 fusion.refs_3_
  21.4 0.7 pad_maximum_fusion.1.refs_4_
  22.1 0.6 reshape.227.refs_12_
  22.7 137.2 %front.1 = (bf16[4,2,32,512]{3,2,1,0:T(8,128)(2,1)}, bf16[4,2,2,144,768]{4,3,2,1,0:T(8,128)(2,1)}, bf16[4,2,2,48,768]{4,3,2,1,0:T(8,128)(2,1)}, bf16[4,2,2,192,7...) custom-call(bf16[32,128]{1,0:T(8,128)(2,1)} %copy-done.11, ...), custom_call_target="tpu_custom_call" | custom-call | tf_op jit(solution)/shard_map/front/pallas_call | solution.py:1273
  159.9 138.6 %middle.1 = (f32[2,529,512]{2,1,0:T(8,128)}, bf16[8,112,512]{2,1,0:T(8,128)(2,1)}, f32[8,512]{1,0:T(8,128)}, bf16[1536,512]{1,0:T(8,128)(2,1)}, bf16[512,512]{1,...) custom-call(bf16[896,512]{1,0:T(8,128)(2,1)} %bitcast.68, ...), custom_call_target="tpu_custom_call" | custom-call | tf_op jit(solution)/shard_map/middle/pallas_call | solution.py:767
  298.6 0.6 reshape.234.refs_2_
  299.2 135.6 %rear.1 = (f32[896,768]{1,0:T(8,128)}, bf16[512,768]{1,0:T(8,128)(2,1)}, bf16[768,3072]{1,0:T(8,128)(2,1)}, bf16[3072,768]{1,0:T(8,128)(2,1)}, bf16[768,768]{1,0...) custom-call(bf16[896,768]{1,0:T(8,128)(2,1)} %bitcast.58, ...), custom_call_target="tpu_custom_call" | custom-call | tf_op jit(solution)/shard_map/rear/pallas_call | solution.py:1554
  434.8 1.1 constant_dynamic-update-slice_fusion.3
  435.9 0.9 constant_dynamic-update-slice_fusion.2
  436.8 1.0 constant_dynamic-update-slice_fusion.1
  437.8 0.8 constant_dynamic-update-slice_fusion
  438.6 0.9 slice_select_fusion
  439.5 1.3 slice.75
  440.9 1.2 slice.78
  442.1 3.0 copy.49
  445.3 1.7 reshape.243
  447.1 0.8 copy.53
  447.8 1.2 broadcast_select_fusion.1
  449.2 0.9 copy.50
  450.1 0.7 copy.51
  450.9 0.9 copy.52
  451.7 0.6 maximum_bitcast_fusion.3
  452.4 0.7 copy.63
  453.1 0.6 copy.64
  453.7 0.6 copy.65
  454.4 0.7 copy.66
  (66 shorter events, 0.8 us)
Async XLA Ops:
  0.6 5.0 %copy-start.14 = (s32[2,529]{1,0:T(2,128)S(1)}, s32[2,529]{1,0:T(2,128)}, u32[]{:S(2)}) copy-start(s32[2,529]{1,0:T(2,128)} %param.23) | copy-start | bytes 12700
  0.7 6.9 %copy-start.15 = (s32[2,529]{1,0:T(2,128)S(1)}, s32[2,529]{1,0:T(2,128)}, u32[]{:S(2)}) copy-start(s32[2,529]{1,0:T(2,128)} %param.22) | copy-start | bytes 12700
  0.7 8.7 %copy-start.17 = (f32[1,96]{1,0:T(1,128)S(1)}, f32[1,96]{1,0:T(1,128)}, u32[]{:S(2)}) copy-start(f32[1,96]{1,0:T(1,128)} %param.25) | copy-start | bytes 1156
  0.7 8.7 %copy-start.16 = (f32[2,64]{1,0:T(2,128)S(1)}, f32[2,64]{1,0:T(2,128)}, u32[]{:S(2)}) copy-start(f32[2,64]{1,0:T(2,128)} %param.30) | copy-start | bytes 1540
  0.7 8.7 %copy-start.3 = (f32[768,96]{0,1:T(8,128)S(1)}, f32[768,96]{0,1:T(8,128)}, u32[]{:S(2)}) copy-start(f32[768,96]{0,1:T(8,128)} %param.29) | copy-start | bytes 884740
  0.7 9.4 %copy-start.9 = (f32[128,192]{0,1:T(8,128)S(1)}, f32[128,192]{0,1:T(8,128)}, u32[]{:S(2)}) copy-start(f32[128,192]{0,1:T(8,128)} %param.32) | copy-start | bytes 294916
  1.6 9.1 %copy-start.5 = (f32[128,256]{1,0:T(8,128)S(1)}, f32[128,256]{1,0:T(8,128)}, u32[]{:S(2)}) copy-start(f32[128,256]{1,0:T(8,128)} %param.34) | copy-start | bytes 393220
  2.6 8.8 %copy-start.6 = (f32[512,64]{0,1:T(8,128)S(1)}, f32[512,64]{0,1:T(8,128)}, u32[]{:S(2)}) copy-start(f32[512,64]{0,1:T(8,128)} %param.35) | copy-start | bytes 393220
  2.6 9.5 %copy-start.2 = (bf16[792,768]{1,0:T(8,128)(2,1)S(1)}, bf16[792,768]{1,0:T(8,128)(2,1)}, u32[]{:S(2)}) copy-start(bf16[792,768]{1,0:T(8,128)(2,1)} %param.20) | copy-start | bytes 3649540
  5.1 14.1 %collective-permute-start = (bf16[416,192]{1,0:T(8,128)(2,1)S(1)}, bf16[416,192]{1,0:T(8,128)(2,1)S(1)}, u32[]{:S(2)}, u32[]{:S(2)}) collective-permute-start(bf16[416,192]{1,0:T(8,128)(2,1)S(1)} %dynamic-slice_bitcast_fusion), channel_id=1, source_target_pairs={{0,1},{1,0},{2,3},{3,2},{4,5},{5,4},{6,7},{7,6},{8,9},{9,8},{10,11... | collective-permute-start | bytes 479240 | tf_op jit(solution)/shard_map/ppermute | solution.py:255
  12.1 1.6 copy-start.18
  16.8 1.8 copy-start.12
  18.6 4.1 copy-start.11
  434.8 7.3 %copy-start.1 = (f32[2,529,512]{2,1,0:T(8,128)S(1)}, f32[2,529,512]{2,1,0:T(8,128)}, u32[]{:S(2)}) copy-start(f32[2,529,512]{2,1,0:T(8,128)} %get-tuple-element.118) | copy-start | bytes 6500356
  439.5 5.6 %copy-start = (f32[896,768]{1,0:T(8,128)S(1)}, f32[896,768]{1,0:T(8,128)}, u32[]{:S(2)}) copy-start(f32[896,768]{1,0:T(8,128)} %get-tuple-element.94) | copy-start | bytes 8257540
  439.5 8.3 %collective-permute-start.1 = (f32[416,192]{1,0:T(8,128)}, f32[416,192]{1,0:T(8,128)}, u32[]{:S(2)}, u32[]{:S(2)}) collective-permute-start(f32[416,192]{1,0:T(8,128)} %slice_select_fusion), channel_id=1, source_target_pairs={{0,1},{1,0},{2,3},{3,2},{4,5},{5,4},{6,7},{7,6},{8,9},{9,8},{10,11... | collective-permute-start | bytes 958472 | tf_op jit(solution)/shard_map/ppermute | solution.py:266
  445.3 1.7 copy-start.8
  449.1 3.3 copy-start.4
  449.1 4.0 copy-start.10
  449.1 4.6 %copy-start.13 = (f32[64,128]{1,0:T(8,128)S(1)}, f32[64,128]{1,0:T(8,128)}, u32[]{:S(2)}) copy-start(f32[64,128]{1,0:T(8,128)} %get-tuple-element.102) | copy-start | bytes 98308
  449.1 5.2 %copy-start.7 = (f32[64,512]{1,0:T(8,128)S(1)}, f32[64,512]{1,0:T(8,128)}, u32[]{:S(2)}) copy-start(f32[64,512]{1,0:T(8,128)} %get-tuple-element.104) | copy-start | bytes 393220

commit v5 on v4

--- a/solution.py
+++ b/solution.py
@@ -37,14 +37,19 @@
     rows: int
     width: int
     by_core: bool
+    share: int = 1
 
     @property
     def q(self):
         return self.width // 2 if self.by_core else self.width // 4
 
     @property
+    def block(self):
+        return self.rows // 2 if self.by_core else self.rows
+
+    @property
     def part(self):
-        return self.rows // 2 if self.by_core else self.rows
+        return self.block // self.share
 
     @property
     def whole(self):
@@ -133,7 +138,7 @@
     return local, [first, second, third, fourth]
 
 
-def reduce_stages(e, i, grad, out, buf, sems, local_sem):
+def reduce_stages(e, i, grad, out, buf, sems, local_sem, row=0):
     z, x, y, c = place()
     acc, r4, r3a, r3b, r2a, r2b, r1 = buf
     q, cut, part = e.q, e.cut, e.part
@@ -145,16 +150,17 @@
     def share(core, ref):
         if len(grad.shape) > 2:
             into = [ref] if e.by_core else [ref.at[:, :, :, pl.ds(k * q, q)] for k in range(2)]
-            return list(zip(region_pair(e, grad, ALL, ALL, ALL, core), into))
+            return list(zip(region_pair(e, grad, ALL, ALL, slice(row, row + part), core), into))
         found = []
         for b in range(8):
             to = ref.at[b // 2, b % 2]
             if e.by_core:
-                found.append((grad.at[pl.ds(pl.multiple_of((2 * b + core) * part, 16), part), :], to))
+                first = pl.multiple_of((2 * b + core) * e.block + row, 16)
+                found.append((grad.at[pl.ds(first, part), :], to))
                 continue
             for k in range(2):
                 cols = pl.ds(pl.multiple_of((2 * k + core) * q, 128), q)
-                found.append((grad.at[pl.ds(b * part, part), cols], to.at[:, pl.ds(k * q, q)]))
+                found.append((grad.at[pl.ds(b * e.block + row, part), cols], to.at[:, pl.ds(k * q, q)]))
         return found
 
     def local():
@@ -226,7 +232,7 @@
         total = acc[z, x, :, lanes(y)].astype(F32)
         for k in range(3):
             total = total + r1[k].astype(F32)
-        out[...] = total
+        out[row : row + part, :] = total
 
     return local, [(first, add_first), (second, add_second), (third, add_third), (fourth, add_fourth)]
 
@@ -645,9 +651,9 @@
         self.swap = (swap_send, swap_recv, swap_local)
 
     def summed(self, k):
+        if k == 1:
+            self.reducer.step(0)
         self.reducer.begin(k)
-        for i in range(k):
-            self.reducer.step(i)
 
     def pause(self, k):
         for i in range(3):
@@ -1037,7 +1043,7 @@
     def tick(self, count=1):
         for _ in range(count):
             for stage in (3, 2, 1, 0):
-                i = self.t - stage
+                i = self.t - 2 * stage
                 if 0 <= i < len(self.plans):
                     self.advance(i, stage)
             self.t += 1
@@ -1122,7 +1128,7 @@
         copy.start()
         keeping.append(copy)
 
-    ticker.tick(5)
+    ticker.tick(8)
     copies = [load(0), load(1)]
     for copy in copies:
         copy.wait()
@@ -1151,10 +1157,9 @@
             for h in range(per_tile):
                 totals[g, t * per_tile + h : t * per_tile + h + 1, :] = logs[h]
 
-    some(0, groups // 2, attend)
+    some(0, groups, attend)
+    keep(1)
     ticker.tick()
-    some(groups // 2, groups, attend)
-    keep(1)
     copies = [load(2), load(3)]
     ticker.tick()
     for copy in copies:
@@ -1173,13 +1178,10 @@
             act[r, t * step : (t + 1) * step] = a.astype(BF16)
             slope[r, t * step : (t + 1) * step] = s.astype(BF16)
 
-    some(0, 1, lift)
+    some(0, 4, lift)
     copies = [load(4)]
-    some(1, 2, lift)
     ticker.tick()
-    some(2, 3, lift)
     copies.append(load(5))
-    some(3, 4, lift)
     for k in (2, 3, 4):
         keep(k)
     for copy in copies:
@@ -1207,9 +1209,10 @@
             def _(s=s):
                 pltpu.make_async_copy(embedded.at[s], table.at[s], swap_local.at[0]).start()
 
-        ticker.tick()
+        if i == 1:
+            ticker.tick()
     keep(5)
-    while ticker.t < n_in + 3:
+    while ticker.t < n_in + 6:
         ticker.tick()
     for i in range(6, n_in):
         ticker.arrived(i)
@@ -1372,18 +1375,17 @@
             ]
 
 
-def rear_kernel(entries, head_size, groups, chunk, sizes, *refs):
+def rear_kernel(parts, names, head_size, groups, chunk, sizes, *refs):
     patches, key_col, own_row, norms, g_dec, g_dec_qkv, *refs = refs
     weights, refs = refs[:5], refs[5:]
     d_table, *refs = refs
     stored, refs = refs[:7], refs[7:]
     d_patches, *refs = refs
     g_embed, g_down, g_up, g_out, g_qkv, *refs = refs
-    n_in = len(entries)
-    outs, refs = refs[:n_in], refs[n_in:]
+    outs, refs = refs[: len(names)], refs[len(names) :]
     up_v, down_v, embed_v, act, slope, mixed, sent, e_two, e_one, d_emb, totals, small, *refs = refs
     stage, stage_wide, sem, g_norms, g_shift, *refs = refs
-    bufs, refs = refs[: 7 * n_in], refs[7 * n_in :]
+    bufs, refs = refs[: 7 * len(parts)], refs[7 * len(parts) :]
     send_sem, recv_sem, local_sem, load_sem = refs
     w_qkv, w_out, w_up, w_down, w_embed = weights
     s_qkv, s_totals, s_mixed, s_one, s_act, s_slope, s_sent = stored
@@ -1413,37 +1415,39 @@
     g_norms[...] = jnp.zeros_like(g_norms)
     g_shift[...] = jnp.zeros_like(g_shift)
     meet(z, x, y, c)
-    grads = [g_dec_qkv, g_down, g_embed, g_up, g_out, g_qkv, small]
-    reducer = Reducer(
-        [
-            reduce_stages(e, i, grads[i], outs[i], bufs[7 * i : 7 * i + 7], (send_sem, recv_sem), local_sem)
-            for i, e in enumerate(entries)
-        ]
-    )
-    reducer.begin(0)
+    sources = {"dq": g_dec_qkv, "do": g_down, "em": g_embed, "up": g_up, "ou": g_out, "qk": g_qkv, "sm": small}
+    plans = {}
+    for i, (name, e, row) in enumerate(parts):
+        out = outs[names.index(name[:2])]
+        plans[name] = reduce_stages(
+            e, i, sources[name[:2]], out, bufs[7 * i : 7 * i + 7], (send_sem, recv_sem), local_sem, row
+        )
+    reducer = Reducer(plans)
     gain = [norms[k : k + 1, :] for k in range(4)]
-
-    def enter(i):
+    h_two, h_one = sent, e_two
+    step = 512
+
+    def enter():
+        loads[0].wait()
+        loads[1].wait()
+        some(0, rows // chunk, enter_rows)
+        loads[2].wait()
+
+    def enter_rows(i):
         r = rows_of(i, chunk)
         g_shift[0:1, :] += column_sum(d_emb[r, :].astype(F32))
         e_two[r, :] = nn(d_emb[r, :], embed_v[...]).astype(BF16)
 
-    loads[0].wait()
-    loads[1].wait()
-    outer_loop(rows // chunk, enter)
-    loads[2].wait()
-    weight_sum(g_down, e_two, act, stage_wide, sem)
-    reducer.begin(1)
-    reducer.step(0)
-    loads[3].wait()
-    weight_sum(g_embed, d_emb, sent, stage, sem)
-    reducer.begin(2)
-    reducer.step(1)
-    reducer.step(0)
-    h_two = sent
-    step = 512
-
-    def middle(i):
+    def sum_down():
+        weight_sum(g_down, e_two, act, stage_wide, sem)
+
+    def sum_embed():
+        loads[3].wait()
+        weight_sum(g_embed, d_emb, sent, stage, sem)
+        for k in range(4, 8):
+            loads[k].wait()
+
+    def middle_rows(i):
         r = rows_of(i, chunk)
         e = e_two[r, :]
         for t in range(slope.shape[1] // step):
@@ -1459,36 +1463,30 @@
         d_patches[r, :] = d_one
         e_one[r, :] = d_one.astype(BF16)
 
-    for k in range(4, 8):
-        loads[k].wait()
-    for i, then in enumerate(((2, 0), (0, 2), (1, 2), (2,))):
-        some(i, i + 1, middle)
-        for k in then:
-            reducer.step(k)
-    load(10, w_qkv, up_v.at[:wide, :])
-    load(11, w_out, up_v.at[wide:, :])
-    weight_sum(g_up, slope, h_two, stage, sem)
-    reducer.begin(3)
-    reducer.step(1)
-    qkv = slope.at[:, :wide]
-    load(12, s_qkv, qkv)
-    loads[8].wait()
-    loads[9].wait()
-    weight_sum(g_out, e_one, mixed, stage, sem)
-    reducer.begin(4)
-
-    def mix_back(i):
+    def middle(i):
+        some(i, i + 1, middle_rows)
+
+    def sum_up():
+        load(10, w_qkv, up_v.at[:wide, :])
+        load(11, w_out, up_v.at[wide:, :])
+        weight_sum(g_up, slope, h_two, stage, sem)
+        load(12, s_qkv, slope.at[:, :wide])
+
+    def sum_out():
+        loads[8].wait()
+        loads[9].wait()
+        weight_sum(g_out, e_one, mixed, stage, sem)
+
+    def mix_rows(i):
         r = rows_of(i, chunk)
         mixed[r, :] = nn(e_one[r, :], up_v[wide:, :]).astype(BF16)
         hat, _ = unit(patches[r, :].astype(F32))
-        e_two[r, :] = (hat * gain[0] + gain[1]).astype(BF16)
-
-    loads[11].wait()
-    outer_loop(rows // chunk, mix_back)
-    h_one = e_two
-    reducer.step(3)
-    reducer.step(4)
-    loads[12].wait()
+        h_one[r, :] = (hat * gain[0] + gain[1]).astype(BF16)
+
+    def mix():
+        loads[11].wait()
+        some(0, rows // chunk, mix_rows)
+        loads[12].wait()
 
     def attend_back(g):
         r = rows_of(g, n)
@@ -1501,18 +1499,14 @@
             for j in range(3):
                 act[r, cols[j]] = found[j].astype(BF16)
 
-    some(0, groups // 2, attend_back)
-    reducer.step(1)
-    some(groups // 2, groups, attend_back)
-    reducer.step(4)
-    reducer.step(3)
-    weight_sum(g_qkv, act.at[:, :wide], h_one, stage, sem)
-    reducer.begin(5)
-    reducer.step(4)
-    reducer.step(3)
-    loads[10].wait()
-
-    def finish(i):
+    def attend(i):
+        some(i * groups // 4, (i + 1) * groups // 4, attend_back)
+
+    def sum_qkv():
+        weight_sum(g_qkv, act.at[:, :wide], h_one, stage, sem)
+        loads[10].wait()
+
+    def finish_rows(i):
         r = rows_of(i, chunk)
         d_h = nn(act[r, :wide], up_v[:wide, :])
         hat, scale = unit(patches[r, :].astype(F32))
@@ -1520,22 +1514,70 @@
         g_norms[1:2, :] += column_sum(d_h)
         d_patches[r, :] += unit_back(d_h * gain[0], hat, scale)
 
-    some(0, 2, finish)
-    reducer.step(5)
-    some(2, 4, finish)
-    gather_norms(g_norms[0:4, :], 0, sizes[0], sizes[1], small)
-    line = lax.broadcasted_iota(jnp.int32, g_dec.shape, 0)
-    gather_norms(jnp.where(line == 7, g_shift[0:1, :], g_dec[...]), NORM_ROWS // 2, sizes[2], sizes[3], small)
-    reducer.begin(6)
-    reducer.step(4)
-    reducer.step(6)
-    reducer.step(5)
-    reducer.step(6)
-    reducer.step(3)
-    reducer.step(6)
-    for i in range(n_in):
-        reducer.finish(i)
+    def finish(i):
+        some(i, i + 1, finish_rows)
+
+    def norms_of_all():
+        gather_norms(g_norms[0:4, :], 0, sizes[0], sizes[1], small)
+
+    def norms_of_decoder():
+        line = lax.broadcasted_iota(jnp.int32, g_dec.shape, 0)
+        joined = jnp.where(line == 7, g_shift[0:1, :], g_dec[...])
+        gather_norms(joined, NORM_ROWS // 2, sizes[2], sizes[3], small)
+
+    blocks = {
+        "enter": enter,
+        "down": sum_down,
+        "embed": sum_embed,
+        "up": sum_up,
+        "out": sum_out,
+        "mix": mix,
+        "qkv": sum_qkv,
+        "norms": norms_of_all,
+        "dnorms": norms_of_decoder,
+    }
+    for i in range(4):
+        blocks["mid" + str(i)] = functools.partial(middle, i)
+        blocks["att" + str(i)] = functools.partial(attend, i)
+        blocks["fin" + str(i)] = functools.partial(finish, i)
+    for name, actions in REAR_PLAN:
+        if name:
+            blocks[name]()
+        for action in actions:
+            if action[0] == "+":
+                reducer.begin(action[1:])
+            else:
+                reducer.step(action)
+    for name, _, _ in parts:
+        reducer.finish(name)
     reducer.drain()
+
+
+REAR_SPLIT = {"qk": 3}
+REAR_PLAN = (
+    ("", ("+dq",)),
+    ("enter", ()),
+    ("down", ("+do", "dq")),
+    ("dnorms", ()),
+    ("embed", ("+em",)),
+    ("mid0", ()),
+    ("mid1", ("dq", "em", "do")),
+    ("mid2", ()),
+    ("mid3", ("dq",)),
+    ("up", ("+up", "em", "dq")),
+    ("out", ("+ou",)),
+    ("mix", ()),
+    ("att0", ("ou", "do", "up", "em")),
+    ("att1", ()),
+    ("att2", ("em", "ou")),
+    ("att3", ("do",)),
+    ("qkv", ("+qk0", "+qk1", "+qk2", "up")),
+    ("fin0", ()),
+    ("fin1", ("ou",)),
+    ("fin2", ("qk0",)),
+    ("fin3", ("qk1", "qk2")),
+    ("norms", ("+sm", "up", "do", "sm", "qk0", "sm", "qk1", "qk0", "qk2", "sm", "qk1", "qk2", "ou", "up")),
+)
 
 
 def rear(rows_in, norms, g_dec, g_dec_qkv, weights, embed, d_table, stored, sizes):
@@ -1545,19 +1587,26 @@
     head_size = width // HEADS_E
     ff = weights[2].shape[0]
     first = (8 * g_dec_qkv.shape[2], g_dec_qkv.shape[3])
+    names = ("dq", "do", "em", "up", "ou", "qk", "sm")
     shapes = [first, weights[3].shape, embed.shape, weights[2].shape, weights[1].shape, weights[0].shape]
     entries = [entry_of(s[0] // 8, s[1]) for s in shapes] + [entry_of(NORM_ROWS, 512)]
+    parts = []
+    for name, e in zip(names, entries):
+        count = REAR_SPLIT.get(name, 1)
+        for k in range(count):
+            cut = dataclasses.replace(e, share=count)
+            parts.append((name + (str(k) if count > 1 else ""), cut, k * cut.part))
     vm, hbm = pl.BlockSpec(memory_space=pltpu.VMEM), pl.BlockSpec(memory_space=pl.ANY)
     sem = pltpu.SemaphoreType.DMA
-    n_in = len(entries)
+    n_in = len(parts)
     totals = stored[1]
     found = pl.pallas_call(
-        functools.partial(rear_kernel, entries, head_size, groups, rows // 4, sizes),
+        functools.partial(rear_kernel, parts, names, head_size, groups, rows // 4, sizes),
         out_shape=[jax.ShapeDtypeStruct((rows, width), F32)]
         + [jax.ShapeDtypeStruct(s, BF16) for s in (shapes[2], shapes[1], *shapes[3:])]
         + [jax.ShapeDtypeStruct((e.part, e.q), F32) for e in entries],
         in_specs=[vm] * 5 + [hbm] * 14,
-        out_specs=[vm] + [hbm] * 5 + [vm] * n_in,
+        out_specs=[vm] + [hbm] * 5 + [vm] * len(names),
         scratch_shapes=[
             pltpu.VMEM(weights[2].shape, BF16),
             pltpu.VMEM(weights[3].shape, BF16),
@@ -1577,7 +1626,7 @@
             pltpu.VMEM((8, width), F32),
             pltpu.VMEM((8, embed.shape[0]), F32),
         ]
-        + [pltpu.VMEM(shape, BF16) for e in entries for shape in reduce_buffers(e)]
+        + [pltpu.VMEM(shape, BF16) for _, e, _ in parts for shape in reduce_buffers(e)]
         + [sem((n_in, 9)), sem((n_in, 9)), sem((n_in,)), sem((13,))],
         compiler_params=pltpu.CompilerParams(
             collective_id=2, has_side_effects=True, vmem_limit_bytes=63 << 20

time: 462 us -> 431 us (0.933)
  Pallas kernels: 411 us -> 379 us
    pallas_call x1, Pallas kernels: 136 us -> 115 us  [rear(): pl.pallas_call(functools.partial(rear_kernel, parts, names, head_size, gr...]
    pallas_call x1, Pallas kernels: 137 us -> 129 us  [front(): pl.pallas_call(functools.partial(front_kernel, entries, head_size, groups...]
where the time goes in v5:
time: 431 us; the launch traced here: 423 us
  Pallas kernels  379 us (88%)
  local copies, waits for them, and re-layouts  31.6 us (7%)
  other arithmetic  10.4 us (2%)
    pallas_call x1, Pallas kernels, decoder(): pl.pallas_call(functools.partial(middle_kernel, entries, head_size, chunk...  136 us
    pallas_call x1, Pallas kernels, front(): pl.pallas_call(functools.partial(front_kernel, entries, head_size, groups...  129 us
    pallas_call x1, Pallas kernels, rear(): pl.pallas_call(functools.partial(rear_kernel, parts, names, head_size, gr...  115 us
    unnamed x54, local copies, waits for them, and re-layouts  16.9 us
  transfers between devices with their start and end apart: 2, of which 0 were waited for; matrix products, arithmetic and copies ran while one was open for 5% of the time, Pallas kernels for 0%

profile of v5, /device:TPU:0, one launch (start us, length us, event | category | flops | bytes accessed | tf_op | source)
XLA Modules:
  0.0 422.8 jit_solution(18360796450364258108)
XLA Ops:
  0.7 0.9 convert_element_type.42
  1.6 1.0 convert_bitcast_fusion.1
  2.8 1.1 copy.41
  3.9 1.1 copy.40
  5.1 0.5 collective-permute-start
  5.7 1.2 broadcast_in_dim_reshape.9.refs_1_
  6.9 0.7 broadcast_in_dim_reshape.8.refs_2_
  7.5 1.2 reshape.244.refs_3_
  8.8 0.6 broadcast_in_dim.25.refs_4_
  9.4 0.7 convert_bitcast_fusion.refs_5_
  10.1 0.6 convert_bitcast_fusion.4.refs_6_
  10.7 0.7 copy.43
  11.5 0.6 convert_bitcast_fusion.2.refs_9_
  12.1 0.4 reshape.225
  12.5 1.2 pad.25
  13.7 1.0 select_n.81.refs_11_.refs_1_
  14.7 2.0 copy.45
  16.8 1.6 pad.28.refs_5_
  18.4 0.2 scatter.9.refs_0_
  18.6 0.6 convert_bitcast_fusion.5.refs_7_
  19.2 0.7 fusion.1.refs_1_
  20.0 0.7 fusion.2.refs_2_
  20.7 0.8 fusion.refs_3_
  21.4 0.7 pad_maximum_fusion.1.refs_4_
  22.1 0.6 reshape.227.refs_12_
  22.7 128.7 %front.1 = (bf16[4,2,32,512]{3,2,1,0:T(8,128)(2,1)}, bf16[4,2,2,144,768]{4,3,2,1,0:T(8,128)(2,1)}, bf16[4,2,2,48,768]{4,3,2,1,0:T(8,128)(2,1)}, bf16[4,2,2,192,7...) custom-call(bf16[32,128]{1,0:T(8,128)(2,1)} %copy-done.11, ...), custom_call_target="tpu_custom_call" | custom-call | tf_op jit(solution)/shard_map/front/pallas_call | solution.py:1276
  151.4 135.7 %middle.1 = (f32[2,529,512]{2,1,0:T(8,128)}, bf16[8,112,512]{2,1,0:T(8,128)(2,1)}, f32[8,512]{1,0:T(8,128)}, bf16[1536,512]{1,0:T(8,128)(2,1)}, bf16[512,512]{1,...) custom-call(bf16[896,512]{1,0:T(8,128)(2,1)} %bitcast.68, ...), custom_call_target="tpu_custom_call" | custom-call | tf_op jit(solution)/shard_map/middle/pallas_call | solution.py:773
  287.1 0.6 reshape.234.refs_2_
  287.7 114.7 %rear.1 = (f32[896,768]{1,0:T(8,128)}, bf16[512,768]{1,0:T(8,128)(2,1)}, bf16[768,3072]{1,0:T(8,128)(2,1)}, bf16[3072,768]{1,0:T(8,128)(2,1)}, bf16[768,768]{1,0...) custom-call(bf16[896,768]{1,0:T(8,128)(2,1)} %bitcast.58, ...), custom_call_target="tpu_custom_call" | custom-call | tf_op jit(solution)/shard_map/rear/pallas_call | solution.py:1603
  402.4 1.1 constant_dynamic-update-slice_fusion.3
  403.5 0.9 constant_dynamic-update-slice_fusion.2
  404.4 1.0 constant_dynamic-update-slice_fusion.1
  405.4 0.8 constant_dynamic-update-slice_fusion
  406.2 0.9 slice_select_fusion
  407.1 1.3 slice.75
  408.5 1.2 slice.78
  409.7 3.0 copy.49
  412.9 1.7 reshape.243
  414.7 0.8 copy.53
  415.4 1.2 broadcast_select_fusion.1
  416.8 0.9 copy.50
  417.7 0.7 copy.51
  418.5 0.9 copy.52
  419.3 0.6 maximum_bitcast_fusion.3
  420.0 0.7 copy.63
  420.7 0.6 copy.64
  421.3 0.6 copy.65
  422.0 0.7 copy.66
  (66 shorter events, 0.8 us)
Async XLA Ops:
  0.6 5.0 %copy-start.14 = (s32[2,529]{1,0:T(2,128)S(1)}, s32[2,529]{1,0:T(2,128)}, u32[]{:S(2)}) copy-start(s32[2,529]{1,0:T(2,128)} %param.23) | copy-start | bytes 12700
  0.7 6.9 %copy-start.15 = (s32[2,529]{1,0:T(2,128)S(1)}, s32[2,529]{1,0:T(2,128)}, u32[]{:S(2)}) copy-start(s32[2,529]{1,0:T(2,128)} %param.22) | copy-start | bytes 12700
  0.7 8.7 %copy-start.17 = (f32[1,96]{1,0:T(1,128)S(1)}, f32[1,96]{1,0:T(1,128)}, u32[]{:S(2)}) copy-start(f32[1,96]{1,0:T(1,128)} %param.25) | copy-start | bytes 1156
  0.7 8.7 %copy-start.16 = (f32[2,64]{1,0:T(2,128)S(1)}, f32[2,64]{1,0:T(2,128)}, u32[]{:S(2)}) copy-start(f32[2,64]{1,0:T(2,128)} %param.30) | copy-start | bytes 1540
  0.7 8.7 %copy-start.3 = (f32[768,96]{0,1:T(8,128)S(1)}, f32[768,96]{0,1:T(8,128)}, u32[]{:S(2)}) copy-start(f32[768,96]{0,1:T(8,128)} %param.29) | copy-start | bytes 884740
  0.7 9.4 %copy-start.9 = (f32[128,192]{0,1:T(8,128)S(1)}, f32[128,192]{0,1:T(8,128)}, u32[]{:S(2)}) copy-start(f32[128,192]{0,1:T(8,128)} %param.32) | copy-start | bytes 294916
  1.6 9.1 %copy-start.5 = (f32[128,256]{1,0:T(8,128)S(1)}, f32[128,256]{1,0:T(8,128)}, u32[]{:S(2)}) copy-start(f32[128,256]{1,0:T(8,128)} %param.34) | copy-start | bytes 393220
  2.6 8.8 %copy-start.6 = (f32[512,64]{0,1:T(8,128)S(1)}, f32[512,64]{0,1:T(8,128)}, u32[]{:S(2)}) copy-start(f32[512,64]{0,1:T(8,128)} %param.35) | copy-start | bytes 393220
  2.6 9.5 %copy-start.2 = (bf16[792,768]{1,0:T(8,128)(2,1)S(1)}, bf16[792,768]{1,0:T(8,128)(2,1)}, u32[]{:S(2)}) copy-start(bf16[792,768]{1,0:T(8,128)(2,1)} %param.20) | copy-start | bytes 3649540
  5.1 14.1 %collective-permute-start = (bf16[416,192]{1,0:T(8,128)(2,1)S(1)}, bf16[416,192]{1,0:T(8,128)(2,1)S(1)}, u32[]{:S(2)}, u32[]{:S(2)}) collective-permute-start(bf16[416,192]{1,0:T(8,128)(2,1)S(1)} %dynamic-slice_bitcast_fusion), channel_id=1, source_target_pairs={{0,1},{1,0},{2,3},{3,2},{4,5},{5,4},{6,7},{7,6},{8,9},{9,8},{10,11... | collective-permute-start | bytes 479240 | tf_op jit(solution)/shard_map/ppermute | solution.py:261
  12.1 1.6 copy-start.18
  16.8 1.8 copy-start.12
  18.6 4.1 copy-start.11
  402.4 7.3 %copy-start.1 = (f32[2,529,512]{2,1,0:T(8,128)S(1)}, f32[2,529,512]{2,1,0:T(8,128)}, u32[]{:S(2)}) copy-start(f32[2,529,512]{2,1,0:T(8,128)} %get-tuple-element.118) | copy-start | bytes 6500356
  407.1 5.6 %copy-start = (f32[896,768]{1,0:T(8,128)S(1)}, f32[896,768]{1,0:T(8,128)}, u32[]{:S(2)}) copy-start(f32[896,768]{1,0:T(8,128)} %get-tuple-element.94) | copy-start | bytes 8257540
  407.1 8.3 %collective-permute-start.1 = (f32[416,192]{1,0:T(8,128)}, f32[416,192]{1,0:T(8,128)}, u32[]{:S(2)}, u32[]{:S(2)}) collective-permute-start(f32[416,192]{1,0:T(8,128)} %slice_select_fusion), channel_id=1, source_target_pairs={{0,1},{1,0},{2,3},{3,2},{4,5},{5,4},{6,7},{7,6},{8,9},{9,8},{10,11... | collective-permute-start | bytes 958472 | tf_op jit(solution)/shard_map/ppermute | solution.py:272
  412.9 1.7 copy-start.8
  416.7 3.3 copy-start.4
  416.7 4.0 copy-start.10
  416.7 4.6 %copy-start.13 = (f32[64,128]{1,0:T(8,128)S(1)}, f32[64,128]{1,0:T(8,128)}, u32[]{:S(2)}) copy-start(f32[64,128]{1,0:T(8,128)} %get-tuple-element.102) | copy-start | bytes 98308
  416.7 5.2 %copy-start.7 = (f32[64,512]{1,0:T(8,128)S(1)}, f32[64,512]{1,0:T(8,128)}, u32[]{:S(2)}) copy-start(f32[64,512]{1,0:T(8,128)} %get-tuple-element.104) | copy-start | bytes 393220

commit v6 on v5

--- a/solution.py
+++ b/solution.py
@@ -138,7 +138,7 @@
     return local, [first, second, third, fourth]
 
 
-def reduce_stages(e, i, grad, out, buf, sems, local_sem, row=0):
+def reduce_stages(e, i, grad, out, buf, sems, local_sem, row=0, place_row=0):
     z, x, y, c = place()
     acc, r4, r3a, r3b, r2a, r2b, r1 = buf
     q, cut, part = e.q, e.cut, e.part
@@ -232,7 +232,7 @@
         total = acc[z, x, :, lanes(y)].astype(F32)
         for k in range(3):
             total = total + r1[k].astype(F32)
-        out[row : row + part, :] = total
+        out[place_row + row : place_row + row + part, :] = total
 
     return local, [(first, add_first), (second, add_second), (third, add_third), (fourth, add_fourth)]
 
@@ -263,20 +263,13 @@
     return jnp.concatenate([left, right], axis=1)
 
 
-def pieces_to_halves(pieces):
+def pieces_to_halves(whole):
     c = lax.rem(lax.axis_index("fsdp"), 2)
-    whole = jnp.concatenate(pieces, axis=0)
     q = whole.shape[1] // 2
     left, right = whole[:, :q], whole[:, q:]
     mine, other = jnp.where(c == 0, left, right), jnp.where(c == 0, right, left)
     came = lax.ppermute(other, "fsdp", CORE_SWAP)
-    first, second = jnp.where(c == 0, mine, came), jnp.where(c == 0, came, mine)
-    sizes = [p.shape[0] for p in pieces]
-    ends = [sum(sizes[:k]) for k in range(1, len(sizes))]
-    return [
-        jnp.concatenate([a, b], axis=0)
-        for a, b in zip(jnp.split(first, ends, axis=0), jnp.split(second, ends, axis=0))
-    ]
+    return jnp.where(c == 0, mine, came), jnp.where(c == 0, came, mine)
 
 
 def gather_masters(enc_norms, dec_norms, weights):
@@ -323,12 +316,9 @@
     )
 
 
-def own_blocks(sums, like):
-    blocks = list(sums)
-    cores = [k for k, b in enumerate(blocks) if b.shape[0] != like[k].shape[1]]
-    for k, b in zip(cores, pieces_to_halves([blocks[k] for k in cores])):
-        blocks[k] = b
-    return [b.T for b in blocks]
+def own_block(halves, first, master):
+    rows = master.shape[1] // 2
+    return jnp.concatenate([h[first : first + rows] for h in halves], axis=0).T
 
 
 def nn(a, b):
@@ -371,17 +361,20 @@
     return jnp.where(head_lanes(values.shape, head_size, h), values, jnp.zeros_like(values))
 
 
+LOG2_E = 1.4426950408889634
+
+
 def attend_tile(q, k, v, bias, head_size):
     v_t = v.astype(F32).T.astype(BF16)
     mixed, totals = [], []
     for h in range(LANES // head_size):
-        scores = nt(pick(k, head_size, h), q) * head_size**-0.5 + bias
+        scores = nt(pick(k, head_size, h), q) * (head_size**-0.5 * LOG2_E) + bias
         top = jnp.max(scores, axis=0, keepdims=True)
-        weight = jnp.exp(scores - top)
+        weight = jnp.exp2(scores - top)
         total = jnp.sum(weight, axis=0, keepdims=True)
         part = nn(v_t[h * head_size : (h + 1) * head_size], weight.astype(BF16))
         mixed.append(part * (1.0 / total))
-        totals.append(top + jnp.log(total))
+        totals.append(top + jnp.log(total) * LOG2_E)
     return jnp.concatenate(mixed, axis=0).T, totals
 
 
@@ -389,8 +382,8 @@
     k_t = k.astype(F32).T.astype(BF16)
     d_q, d_k, d_v = [], 0.0, 0.0
     for h in range(LANES // head_size):
-        scores = nt(pick(k, head_size, h), q) * head_size**-0.5 + bias
-        prob = jnp.exp(scores - totals[h])
+        scores = nt(pick(k, head_size, h), q) * (head_size**-0.5 * LOG2_E) + bias
+        prob = jnp.exp2(scores - totals[h])
         d_prob = nt(pick(v, head_size, h), d_mixed)
         centre = jnp.sum(d_prob * prob, axis=0, keepdims=True)
         d_score = (prob * (d_prob - centre)).astype(BF16)
@@ -449,10 +442,8 @@
     head_size,
     chunk,
     table,
-    index_col,
-    index_row,
-    seg_col,
-    seg_row,
+    marks_col,
+    marks_row,
     cot,
     norms,
     w_qkv,
@@ -495,7 +486,7 @@
     def start(i):
         r = rows_of(i, chunk)
         slots = lax.broadcasted_iota(jnp.int32, (chunk, table.shape[0]), 1)
-        named = index_col[r, :]
+        named = marks_col[r, 0:1]
         chosen = jnp.where(slots == named, 1.0, 0.0).astype(BF16)
         picked = nn(chosen, table[...])
         begin = jnp.where(named >= 0, picked, gain[6])
@@ -508,7 +499,7 @@
     outer_loop(rows // chunk, start)
 
     def attend(g):
-        bias[...] = mask_bias(seg_row[g], seg_col[rows_of(g, n), :])
+        bias[...] = mask_bias(marks_row[g, 1:2, :], marks_col[rows_of(g, n), 1:2])
         r = rows_of(g, n)
 
         def one(t):
@@ -582,7 +573,7 @@
     d_qkv = act
 
     for g in range(groups):
-        bias[...] = mask_bias(seg_row[g], seg_col[rows_of(g, n), :])
+        bias[...] = mask_bias(marks_row[g, 1:2, :], marks_col[rows_of(g, n), 1:2])
         r = rows_of(g, n)
 
         def one(t, g=g, r=r):
@@ -604,7 +595,7 @@
         g_norms[0:1, :] += column_sum(d_h * hat)
         g_norms[1:2, :] += column_sum(d_h)
         d_start = d_x[g, cr, :] + unit_back(d_h * gain[0], hat, scale)
-        seen = index_col[r, :] >= 0
+        seen = marks_col[r, 0:1] >= 0
         g_norms[6:7, :] += column_sum(jnp.where(seen, 0.0, d_start))
         e_two[r, :] = jnp.where(seen, d_start, 0.0).astype(BF16)
 
@@ -613,9 +604,12 @@
     slots, slot_rows, _ = d_table.shape
 
     def back(s):
-        line = lax.broadcasted_iota(jnp.int32, (slot_rows, rows), 0) + s * slot_rows
-        chosen = jnp.where(line == index_row[...], 1.0, 0.0).astype(BF16)
-        d_table[s] = nn(chosen, e_two[...]).astype(BF16)
+        line = lax.broadcasted_iota(jnp.int32, (slot_rows, n), 0) + s * slot_rows
+        total = 0.0
+        for g in range(groups):
+            chosen = jnp.where(line == marks_row[g, 0:1, :], 1.0, 0.0).astype(BF16)
+            total = total + nn(chosen, e_two[g * n : (g + 1) * n, :])
+        d_table[s] = total.astype(BF16)
 
     hooks.slots(back, slots)
     weight_sum(g_qkv, d_qkv.at[:, : 3 * width], h_one, stage, sem)
@@ -689,7 +683,7 @@
 
 
 def middle_kernel(entries, head_size, chunk, *refs):
-    ins, refs = refs[:11], refs[11:]
+    ins, refs = refs[:9], refs[9:]
     decoded, returned, g_norms, *refs = refs
     grads, refs = refs[:4], refs[4:]
     outs, refs = refs[:3], refs[3:]
@@ -717,8 +711,8 @@
     rows = groups * n
     head_size = width // heads
     pad = n - real
-    index = jnp.pad(index, ((0, 0), (0, pad)), constant_values=-1).reshape(rows)
-    segment = jnp.pad(segment, ((0, 0), (0, pad)), constant_values=-1)
+    marks = jnp.stack([index, segment], axis=1)
+    marks = jnp.pad(marks, ((0, 0), (0, 0), (0, pad)), constant_values=-1)
     cot = jnp.pad(cotangent, ((0, 0), (0, pad), (0, 0)))
     tiles = width // LANES
     ff = weights[2].shape[0]
@@ -744,10 +738,8 @@
     ]
     args = (
         table,
-        index[:, None],
-        index[None, :],
-        segment.reshape(rows, 1),
-        segment[:, None, :],
+        marks.transpose(0, 2, 1).reshape(rows, 2),
+        marks,
         cot,
         norms,
         *weights,
@@ -762,7 +754,7 @@
         return pl.pallas_call(
             functools.partial(decoder_kernel, head_size, chunk),
             out_shape=shapes,
-            in_specs=[vm] * 11,
+            in_specs=[vm] * 9,
             out_specs=[vm] * 3 + [hbm] * 4,
             scratch_shapes=scratch,
             compiler_params=pltpu.CompilerParams(vmem_limit_bytes=60 << 20),
@@ -773,7 +765,7 @@
     return pl.pallas_call(
         functools.partial(middle_kernel, entries, head_size, chunk),
         out_shape=shapes + [jax.ShapeDtypeStruct((e.part, e.q), F32) for e in entries],
-        in_specs=[vm] * 11,
+        in_specs=[vm] * 9,
         out_specs=[vm, hbm, vm] + [hbm] * 4 + [vm] * 3,
         scratch_shapes=scratch
         + [pltpu.VMEM(slots, BF16)]
@@ -1375,14 +1367,14 @@
             ]
 
 
-def rear_kernel(parts, names, head_size, groups, chunk, sizes, *refs):
+def rear_kernel(parts, places, n_out, head_size, groups, chunk, sizes, *refs):
     patches, key_col, own_row, norms, g_dec, g_dec_qkv, *refs = refs
     weights, refs = refs[:5], refs[5:]
     d_table, *refs = refs
     stored, refs = refs[:7], refs[7:]
     d_patches, *refs = refs
     g_embed, g_down, g_up, g_out, g_qkv, *refs = refs
-    outs, refs = refs[: len(names)], refs[len(names) :]
+    outs, refs = refs[:n_out], refs[n_out:]
     up_v, down_v, embed_v, act, slope, mixed, sent, e_two, e_one, d_emb, totals, small, *refs = refs
     stage, stage_wide, sem, g_norms, g_shift, *refs = refs
     bufs, refs = refs[: 7 * len(parts)], refs[7 * len(parts) :]
@@ -1418,9 +1410,9 @@
     sources = {"dq": g_dec_qkv, "do": g_down, "em": g_embed, "up": g_up, "ou": g_out, "qk": g_qkv, "sm": small}
     plans = {}
     for i, (name, e, row) in enumerate(parts):
-        out = outs[names.index(name[:2])]
+        out, first = outs[places[name[:2]][0]], places[name[:2]][1]
         plans[name] = reduce_stages(
-            e, i, sources[name[:2]], out, bufs[7 * i : 7 * i + 7], (send_sem, recv_sem), local_sem, row
+            e, i, sources[name[:2]], out, bufs[7 * i : 7 * i + 7], (send_sem, recv_sem), local_sem, row, first
         )
     reducer = Reducer(plans)
     gain = [norms[k : k + 1, :] for k in range(4)]
@@ -1590,6 +1582,16 @@
     names = ("dq", "do", "em", "up", "ou", "qk", "sm")
     shapes = [first, weights[3].shape, embed.shape, weights[2].shape, weights[1].shape, weights[0].shape]
     entries = [entry_of(s[0] // 8, s[1]) for s in shapes] + [entry_of(NORM_ROWS, 512)]
+    places, sums, high = {}, [], 0
+    for name, e in zip(names, entries):
+        if e.by_core:
+            places[name] = (0, high)
+            high += e.part
+    sums.append((high, entries[5].q))
+    for name, e in zip(names, entries):
+        if not e.by_core:
+            places[name] = (len(sums), 0)
+            sums.append((e.part, e.q))
     parts = []
     for name, e in zip(names, entries):
         count = REAR_SPLIT.get(name, 1)
@@ -1601,12 +1603,12 @@
     n_in = len(parts)
     totals = stored[1]
     found = pl.pallas_call(
-        functools.partial(rear_kernel, parts, names, head_size, groups, rows // 4, sizes),
+        functools.partial(rear_kernel, parts, places, len(sums), head_size, groups, rows // 4, sizes),
         out_shape=[jax.ShapeDtypeStruct((rows, width), F32)]
         + [jax.ShapeDtypeStruct(s, BF16) for s in (shapes[2], shapes[1], *shapes[3:])]
-        + [jax.ShapeDtypeStruct((e.part, e.q), F32) for e in entries],
+        + [jax.ShapeDtypeStruct(s, F32) for s in sums],
         in_specs=[vm] * 5 + [hbm] * 14,
-        out_specs=[vm] + [hbm] * 5 + [vm] * len(names),
+        out_specs=[vm] + [hbm] * 5 + [vm] * len(sums),
         scratch_shapes=[
             pltpu.VMEM(weights[2].shape, BF16),
             pltpu.VMEM(weights[3].shape, BF16),
@@ -1633,7 +1635,7 @@
         ),
         name="rear",
     )(x, keys, own, norms, g_dec, g_dec_qkv, *weights, embed, d_table, *stored)
-    return found[0], found[6:]
+    return found[0], found[6:], places
 
 
 def per_device(
@@ -1689,7 +1691,7 @@
             True, table, index, dec_segment, cotangent, norms_d, dec_weights, HEADS_D
         )
         e = entry_of(g_qkv.shape[0] // 8, g_qkv.shape[1])
-        d_patches, sums = rear(
+        d_patches, sums, places = rear(
             enc_inputs,
             norms_e,
             g_dec_norms,
@@ -1700,14 +1702,17 @@
             stored,
             sizes,
         )
-        s_qkv, e_down, s_embed, e_up, e_out, e_qkv, small = sums
+        small = sums[places["sm"][0]]
         half = NORM_ROWS // 2
         s_enc_norms = small[: sizes[0], : sizes[1]]
         s_dec_norms = small[half : half + sizes[2], : sizes[3]]
-        sums = own_blocks(
-            [e_qkv, e_out, e_up, e_down, s_embed, s_qkv, s_out, s_up, s_down],
-            [enc_qkv, enc_out, enc_up, enc_down, dec_embed, dec_qkv, dec_out, dec_up, dec_down],
-        )
+        halves = pieces_to_halves(sums[0])
+        e_qkv, e_out, e_up, s_embed = [
+            own_block(halves, places[name][1], master)
+            for name, master in (("qk", enc_qkv), ("ou", enc_out), ("up", enc_up), ("em", dec_embed))
+        ]
+        e_down, s_qkv = sums[places["do"][0]].T, sums[places["dq"][0]].T
+        sums = [e_qkv, e_out, e_up, e_down, s_embed, s_qkv, s_out.T, s_up.T, s_down.T]
     else:
         decoded, d_table, g_dec_norms, *dec_grads = decoder(
             False, table, index, dec_segment, cotangent, norms_d, dec_weights, HEADS_D

time: 431 us -> 424 us (0.984)
    unnamed x54 -> x51, local copies, waits for them, and re-layouts: 16.9 us -> 15.4 us
where the time goes in v6:
time: 424 us; the launch traced here: 417 us
  Pallas kernels  376 us (89%)
  local copies, waits for them, and re-layouts  27.3 us (6%)
  other arithmetic  11.6 us (3%)
    pallas_call x1, Pallas kernels, decoder(): pl.pallas_call(functools.partial(middle_kernel, entries, head_size, chunk...  133 us
    pallas_call x1, Pallas kernels, front(): pl.pallas_call(functools.partial(front_kernel, entries, head_size, groups...  129 us
    pallas_call x1, Pallas kernels, rear(): pl.pallas_call(functools.partial(rear_kernel, parts, places, len(sums), h...  115 us
    unnamed x51, local copies, waits for them, and re-layouts  15.4 us
  transfers between devices with their start and end apart: 2, of which 0 were waited for; matrix products, arithmetic and copies ran while one was open for 5% of the time, Pallas kernels for 0%

profile of v6, /device:TPU:0, one launch (start us, length us, event | category | flops | bytes accessed | tf_op | source)
XLA Modules:
  0.0 416.8 jit_solution(16358813845594852707)
XLA Ops:
  0.7 1.0 convert_element_type.42
  1.7 1.0 convert_bitcast_fusion.1
  2.7 0.1 copy.53
  2.8 1.0 copy.40
  3.8 1.1 copy.39
  4.9 0.1 pad_maximum_fusion
  5.0 0.5 collective-permute-start
  5.6 0.7 convert_bitcast_fusion.refs_5_
  6.3 0.6 convert_bitcast_fusion.4.refs_6_
  6.9 0.7 copy.42
  7.6 0.6 convert_bitcast_fusion.2.refs_9_
  8.3 0.4 reshape.225
  8.6 0.0 copy-start.15
  8.7 1.2 pad.22
  9.8 0.1 iota_select_fusion
  9.9 1.0 select_n.81.refs_11_.refs_1_
  11.0 0.6 fusion.5
  11.6 1.0 copy.54
  12.6 2.0 copy.45
  14.7 0.0 copy-start.12
  14.7 1.6 pad.24.refs_3_
  16.3 0.2 scatter.9.refs_0_
  16.5 0.6 convert_bitcast_fusion.5.refs_7_
  17.1 0.7 fusion.1.refs_1_
  17.9 0.7 fusion.2.refs_2_
  18.6 0.8 fusion.refs_3_
  19.3 0.7 pad_maximum_fusion.1.refs_4_
  20.0 0.6 reshape.227.refs_12_
  20.6 128.6 %front.1 = (bf16[4,2,32,512]{3,2,1,0:T(8,128)(2,1)}, bf16[4,2,2,144,768]{4,3,2,1,0:T(8,128)(2,1)}, bf16[4,2,2,48,768]{4,3,2,1,0:T(8,128)(2,1)}, bf16[4,2,2,192,7...) custom-call(bf16[32,128]{1,0:T(8,128)(2,1)} %copy-done.11, ...), custom_call_target="tpu_custom_call" | custom-call | tf_op jit(solution)/shard_map/front/pallas_call | solution.py:1268
  149.2 132.7 %middle.1 = (f32[2,529,512]{2,1,0:T(8,128)}, bf16[8,112,512]{2,1,0:T(8,128)(2,1)}, f32[8,512]{1,0:T(8,128)}, bf16[1536,512]{1,0:T(8,128)(2,1)}, bf16[512,512]{1,...) custom-call(bf16[896,512]{1,0:T(8,128)(2,1)} %bitcast.72, ...), custom_call_target="tpu_custom_call" | custom-call | tf_op jit(solution)/shard_map/middle/pallas_call | solution.py:765
  281.9 0.6 reshape.234.refs_2_
  282.5 114.8 %rear.1 = (f32[896,768]{1,0:T(8,128)}, bf16[512,768]{1,0:T(8,128)(2,1)}, bf16[768,3072]{1,0:T(8,128)(2,1)}, bf16[3072,768]{1,0:T(8,128)(2,1)}, bf16[768,768]{1,0...) custom-call(bf16[896,768]{1,0:T(8,128)(2,1)} %bitcast.61, ...), custom_call_target="tpu_custom_call" | custom-call | tf_op jit(solution)/shard_map/rear/pallas_call | solution.py:1605
  397.3 2.1 slice_select_fusion
  399.5 1.3 slice.99
  400.8 1.2 slice.108
  402.0 4.6 %copy.48 = f32[2,529,512]{2,0,1:T(2,128)} copy(f32[2,529,512]{2,1,0:T(8,128)} %get-tuple-element.112) | data formatting | bytes 4333568
  406.7 0.2 slice.117
  406.9 1.7 reshape.243
  408.6 0.8 copy.52
  409.4 1.2 broadcast_select_fusion.1
  410.8 0.9 copy.49
  411.7 0.7 copy.50
  412.4 0.9 copy.51
  413.3 0.6 maximum_bitcast_fusion.3
  413.9 0.7 copy.61
  414.7 0.6 copy.62
  415.3 0.6 copy.63
  415.9 0.7 copy.64
  (61 shorter events, 0.3 us)
Async XLA Ops:
  0.6 4.9 %copy-start.17 = (f32[1,96]{1,0:T(1,128)S(1)}, f32[1,96]{1,0:T(1,128)}, u32[]{:S(2)}) copy-start(f32[1,96]{1,0:T(1,128)} %param.25) | copy-start | bytes 1156
  0.7 4.9 %copy-start.16 = (f32[2,64]{1,0:T(2,128)S(1)}, f32[2,64]{1,0:T(2,128)}, u32[]{:S(2)}) copy-start(f32[2,64]{1,0:T(2,128)} %param.30) | copy-start | bytes 1540
  0.7 4.9 %copy-start.3 = (f32[768,96]{0,1:T(8,128)S(1)}, f32[768,96]{0,1:T(8,128)}, u32[]{:S(2)}) copy-start(f32[768,96]{0,1:T(8,128)} %param.29) | copy-start | bytes 884740
  0.7 5.6 %copy-start.9 = (f32[128,192]{0,1:T(8,128)S(1)}, f32[128,192]{0,1:T(8,128)}, u32[]{:S(2)}) copy-start(f32[128,192]{0,1:T(8,128)} %param.32) | copy-start | bytes 294916
  0.7 6.2 %copy-start.5 = (f32[128,256]{1,0:T(8,128)S(1)}, f32[128,256]{1,0:T(8,128)}, u32[]{:S(2)}) copy-start(f32[128,256]{1,0:T(8,128)} %param.34) | copy-start | bytes 393220
  0.7 6.9 %copy-start.6 = (f32[512,64]{0,1:T(8,128)S(1)}, f32[512,64]{0,1:T(8,128)}, u32[]{:S(2)}) copy-start(f32[512,64]{0,1:T(8,128)} %param.35) | copy-start | bytes 393220
  0.7 7.6 %copy-start.2 = (bf16[792,768]{1,0:T(8,128)(2,1)S(1)}, bf16[792,768]{1,0:T(8,128)(2,1)}, u32[]{:S(2)}) copy-start(bf16[792,768]{1,0:T(8,128)(2,1)} %param.20) | copy-start | bytes 3649540
  5.0 12.1 %collective-permute-start = (bf16[416,192]{1,0:T(8,128)(2,1)S(1)}, bf16[416,192]{1,0:T(8,128)(2,1)S(1)}, u32[]{:S(2)}, u32[]{:S(2)}) collective-permute-start(bf16[416,192]{1,0:T(8,128)(2,1)S(1)} %dynamic-slice_bitcast_fusion), channel_id=1, source_target_pairs={{0,1},{1,0},{2,3},{3,2},{4,5},{5,4},{6,7},{7,6},{8,9},{9,8},{10,11... | collective-permute-start | bytes 479240 | tf_op jit(solution)/shard_map/ppermute | solution.py:261
  8.3 1.6 copy-start.18
  8.3 2.6 copy-start.14
  8.6 2.3 copy-start.15
  14.7 1.8 copy-start.12
  16.5 4.1 copy-start.11
  399.5 7.2 %copy-start.1 = (f32[896,768]{1,0:T(8,128)S(1)}, f32[896,768]{1,0:T(8,128)}, u32[]{:S(2)}) copy-start(f32[896,768]{1,0:T(8,128)} %get-tuple-element.91) | copy-start | bytes 8257540
  399.5 9.9 %collective-permute-start.1 = (f32[416,192]{1,0:T(8,128)}, f32[416,192]{1,0:T(8,128)}, u32[]{:S(2)}, u32[]{:S(2)}) collective-permute-start(f32[416,192]{1,0:T(8,128)} %slice_select_fusion), channel_id=1, source_target_pairs={{0,1},{1,0},{2,3},{3,2},{4,5},{5,4},{6,7},{7,6},{8,9},{9,8},{10,11... | collective-permute-start | bytes 958472 | tf_op jit(solution)/shard_map/ppermute | solution.py:271
  406.9 1.8 copy-start.8
  406.9 2.5 copy-start
  410.6 3.3 copy-start.4
  410.7 4.0 copy-start.10
  410.7 4.6 %copy-start.13 = (f32[64,128]{1,0:T(8,128)S(1)}, f32[64,128]{1,0:T(8,128)}, u32[]{:S(2)}) copy-start(f32[64,128]{1,0:T(8,128)} %get-tuple-element.96) | copy-start | bytes 98308
  410.7 5.2 %copy-start.7 = (f32[64,512]{1,0:T(8,128)S(1)}, f32[64,512]{1,0:T(8,128)}, u32[]{:S(2)}) copy-start(f32[64,512]{1,0:T(8,128)} %get-tuple-element.98) | copy-start | bytes 393220

commit v7 on v6

--- a/solution.py
+++ b/solution.py
@@ -101,7 +101,7 @@
 ALL = slice(None)
 
 
-def gather_stages(e, i, piece, out, sems, local_sem):
+def gather_stages(e, i, piece, out, sems, local_sem, z_second):
     z, x, y, c = place()
     top, bottom = slice(0, e.cut), slice(e.cut, e.part)
 
@@ -122,19 +122,36 @@
             send(b, b, sems, i, 4, at(z, x, 1 - y, c)),
         ]
 
+    def first_xy():
+        a, b = piece.at[top], piece.at[bottom]
+        return [
+            send(a, region(e, out, z, x, top, y, c), sems, i, 0, at(z, 1 - x, y, c)),
+            send(b, region(e, out, z, x, bottom, y, c), sems, i, 1, at(z, x, 1 - y, c)),
+        ]
+
+    def second_z():
+        blocks = [region(e, out, z, ALL, top, y, c)] + region_pair(e, out, z, x, bottom, c)
+        found = []
+        for k in (1, 2, 3):
+            for j, b in enumerate(blocks):
+                found.append(send(b, b, sems, i, 4 + 3 * k + j, at(lax.rem(z + k, 4), x, y, c)))
+        return found
+
     def third():
         a = region(e, out, ALL, ALL, top, y, c)
-        found = [send(a, a, sems, i, 5, at(z, x, 1 - y, c))]
+        found = [send(a, a, sems, i, 4 if z_second else 5, at(z, x, 1 - y, c))]
         for k, b in enumerate(region_pair(e, out, ALL, x, bottom, c)):
-            found.append(send(b, b, sems, i, 6 + k, at(z, 1 - x, y, c)))
+            found.append(send(b, b, sems, i, (2 if z_second else 6) + k, at(z, 1 - x, y, c)))
         return found
 
     def fourth():
         return [
-            send(b, b, sems, i, 8 + k, at(z, x, y, 1 - c))
+            send(b, b, sems, i, (5 if z_second else 8) + k, at(z, x, y, 1 - c))
             for k, b in enumerate(region_pair(e, out, ALL, ALL, ALL, c))
         ]
 
+    if z_second:
+        return local, [first_xy, second_z, third, fourth]
     return local, [first, second, third, fourth]
 
 
@@ -474,8 +491,8 @@
     stage_wide,
     sem,
 ):
-    groups, n, width = cot.shape
-    real = decoded.shape[1]
+    groups, real, width = cot.shape
+    n = d_x.shape[1]
     rows = groups * n
     per_group = n // chunk
     tiles = width // LANES
@@ -512,6 +529,8 @@
         outer_loop(tiles, one)
 
     outer_loop(groups, attend)
+
+    hooks.ready()
 
     def middle(i):
         g, j = i // per_group, lax.rem(i, per_group)
@@ -537,9 +556,12 @@
                 @pl.when(i == b * per_group + c)
                 def _(b=b, lo=lo, hi=hi):
                     decoded[b, lo:hi, :] = result[: hi - lo]
+                    d_x[b, lo:hi, :] = cot[b, lo:hi, :]
+                    if hi < lo + chunk:
+                        d_x[b, hi : lo + chunk, :] = jnp.zeros((lo + chunk - hi, width), F32)
 
         cr = rows_of(j, chunk)
-        d = cot[g, cr, :]
+        d = d_x[g, cr, :]
         g_norms[4:5, :] += column_sum(d * hat)
         g_norms[5:6, :] += column_sum(d)
         d_two = unit_back(d * gain[4], hat, scale)
@@ -625,6 +647,9 @@
 
 
 class NoHooks:
+    def ready(self):
+        pass
+
     def summed(self, k):
         pass
 
@@ -639,10 +664,14 @@
 
 
 class MiddleHooks:
-    def __init__(self, reducer, d_table, returned, swap_send, swap_recv, swap_local):
-        self.reducer = reducer
+    def __init__(self, loads, reducer, d_table, returned, swap_send, swap_recv, swap_local):
+        self.loads, self.reducer = loads, reducer
         self.d_table, self.returned = d_table, returned
         self.swap = (swap_send, swap_recv, swap_local)
+
+    def ready(self):
+        for copy in self.loads:
+            copy.wait()
 
     def summed(self, k):
         if k == 1:
@@ -683,14 +712,18 @@
 
 
 def middle_kernel(entries, head_size, chunk, *refs):
-    ins, refs = refs[:9], refs[9:]
+    ins, late, refs = refs[:6], refs[6:9], refs[9:]
     decoded, returned, g_norms, *refs = refs
     grads, refs = refs[:4], refs[4:]
     outs, refs = refs[:3], refs[3:]
     scratch, refs = refs[:16], refs[16:]
+    loaded, refs = refs[:3], refs[3:]
     d_table, *refs = refs
     bufs, refs = refs[:21], refs[21:]
-    send_sem, recv_sem, local_sem, swap_send, swap_recv, swap_local = refs
+    send_sem, recv_sem, local_sem, swap_send, swap_recv, swap_local, load_sem = refs
+    loads = [pltpu.make_async_copy(late[k], loaded[k], load_sem.at[k]) for k in range(3)]
+    for copy in loads:
+        copy.start()
     z, x, y, c = place()
     meet(z, x, y, c)
     by_entry = [grads[3], grads[2], grads[1]]
@@ -700,8 +733,8 @@
             for i, e in enumerate(entries)
         ]
     )
-    hooks = MiddleHooks(reducer, d_table, returned, swap_send, swap_recv, swap_local)
-    decoder_body(hooks, head_size, chunk, *ins, decoded, d_table, g_norms, *grads, *scratch)
+    hooks = MiddleHooks(loads, reducer, d_table, returned, swap_send, swap_recv, swap_local)
+    decoder_body(hooks, head_size, chunk, *ins, *loaded, decoded, d_table, g_norms, *grads, *scratch)
 
 
 def decoder(staged, table, index, segment, cotangent, norms, weights, heads):
@@ -713,7 +746,6 @@
     pad = n - real
     marks = jnp.stack([index, segment], axis=1)
     marks = jnp.pad(marks, ((0, 0), (0, 0), (0, pad)), constant_values=-1)
-    cot = jnp.pad(cotangent, ((0, 0), (0, pad), (0, 0)))
     tiles = width // LANES
     ff = weights[2].shape[0]
     vm = pl.BlockSpec(memory_space=pltpu.VMEM)
@@ -731,7 +763,7 @@
         pltpu.VMEM((rows, width), BF16),
         pltpu.VMEM((rows, width), BF16),
         pltpu.VMEM((n, n), F32),
-        pltpu.VMEM(cot.shape, F32),
+        pltpu.VMEM((groups, n, width), F32),
         pltpu.VMEM((2, 256, width), BF16),
         pltpu.VMEM((2, LANES, ff), BF16),
         pltpu.SemaphoreType.DMA((2,)),
@@ -740,7 +772,7 @@
         table,
         marks.transpose(0, 2, 1).reshape(rows, 2),
         marks,
-        cot,
+        cotangent,
         norms,
         *weights,
     )
@@ -765,12 +797,13 @@
     return pl.pallas_call(
         functools.partial(middle_kernel, entries, head_size, chunk),
         out_shape=shapes + [jax.ShapeDtypeStruct((e.part, e.q), F32) for e in entries],
-        in_specs=[vm] * 9,
+        in_specs=[vm] * 6 + [hbm] * 3,
         out_specs=[vm, hbm, vm] + [hbm] * 4 + [vm] * 3,
         scratch_shapes=scratch
+        + [pltpu.VMEM(w.shape, BF16) for w in weights[1:]]
         + [pltpu.VMEM(slots, BF16)]
         + [pltpu.VMEM(shape, BF16) for e in entries for shape in reduce_buffers(e)]
-        + [sem((3, 9)), sem((3, 9)), sem((3,)), sem((8,)), sem((8,)), sem((1,))],
+        + [sem((3, 9)), sem((3, 9)), sem((3,)), sem((8,)), sem((8,)), sem((1,)), sem((3,))],
         compiler_params=pltpu.CompilerParams(
             collective_id=1, has_side_effects=True, vmem_limit_bytes=62 << 20
         ),
@@ -1034,11 +1067,18 @@
 
     def tick(self, count=1):
         for _ in range(count):
-            for stage in (3, 2, 1, 0):
-                i = self.t - 2 * stage
-                if 0 <= i < len(self.plans):
-                    self.advance(i, stage)
+            self.part((3, 2, 1, 0))
             self.t += 1
+
+    def part(self, stages):
+        for stage in stages:
+            i = self.t - 2 * stage
+            if 0 <= i < len(self.plans):
+                self.advance(i, stage)
+
+    def rest(self):
+        self.part((2, 1, 0))
+        self.t += 1
 
     def advance(self, i, stage):
         if stage > 0:
@@ -1099,7 +1139,9 @@
 
     plans, locals_ = [], []
     for i, e in enumerate(entries):
-        local, stages = gather_stages(e, i, pieces[i], whole[i], (send_sem, recv_sem), local_sem)
+        local, stages = gather_stages(
+            e, i, pieces[i], whole[i], (send_sem, recv_sem), local_sem, i >= 6
+        )
         plans.append(stages)
         locals_.append(local())
     for copy in locals_:
@@ -1120,7 +1162,8 @@
         copy.start()
         keeping.append(copy)
 
-    ticker.tick(8)
+    ticker.tick(7)
+    ticker.part((3,))
     copies = [load(0), load(1)]
     for copy in copies:
         copy.wait()
@@ -1135,8 +1178,9 @@
         qkv[r, :] = nt((hat * gain[0] + gain[1]).astype(BF16), flat(w_qkv)).astype(BF16)
 
     some(0, 2, start)
+    ticker.rest()
+    some(2, 4, start)
     ticker.tick()
-    some(2, 4, start)
     keep(0)
 
     def attend(g):
@@ -1149,9 +1193,10 @@
             for h in range(per_tile):
                 totals[g, t * per_tile + h : t * per_tile + h + 1, :] = logs[h]
 
-    some(0, groups, attend)
+    some(0, 3 * groups // 4, attend)
+    ticker.tick()
+    some(3 * groups // 4, groups, attend)
     keep(1)
-    ticker.tick()
     copies = [load(2), load(3)]
     ticker.tick()
     for copy in copies:
@@ -1170,10 +1215,10 @@
             act[r, t * step : (t + 1) * step] = a.astype(BF16)
             slope[r, t * step : (t + 1) * step] = s.astype(BF16)
 
-    some(0, 4, lift)
-    copies = [load(4)]
+    some(0, 3, lift)
     ticker.tick()
-    copies.append(load(5))
+    some(3, 4, lift)
+    copies = [load(4), load(5)]
     for k in (2, 3, 4):
         keep(k)
     for copy in copies:
@@ -1281,8 +1326,8 @@
         + [pltpu.VMEM(by[k].whole, BF16) for k in range(6)]
         + [
             pltpu.VMEM((peers, padded, embed), BF16),
-            sem((n_in, 10)),
-            sem((n_in, 10)),
+            sem((n_in, 16)),
+            sem((n_in, 16)),
             sem((n_in,)),
             sem((6,)),
             sem((6,)),

time: 424 us -> 419 us (0.988)
  Pallas kernels: 376 us -> 370 us
    unnamed x51 -> x57, local copies, waits for them, and re-layouts: 15.4 us -> 15.9 us
where the time goes in v7:
time: 419 us; the launch traced here: 411 us
  Pallas kernels  370 us (88%)
  local copies, waits for them, and re-layouts  26.9 us (6%)
  other arithmetic  12.6 us (3%)
    pallas_call x1, Pallas kernels, decoder(): pl.pallas_call(functools.partial(middle_kernel, entries, head_size, chunk...  129 us
    pallas_call x1, Pallas kernels, front(): pl.pallas_call(functools.partial(front_kernel, entries, head_size, groups...  126 us
    pallas_call x1, Pallas kernels, rear(): pl.pallas_call(functools.partial(rear_kernel, parts, places, len(sums), h...  115 us
    unnamed x57, local copies, waits for them, and re-layouts  15.9 us
  transfers between devices with their start and end apart: 2, of which 0 were waited for; matrix products, arithmetic and copies ran while one was open for 5% of the time, Pallas kernels for 0%

profile of v7, /device:TPU:0, one launch (start us, length us, event | category | flops | bytes accessed | tf_op | source)
XLA Modules:
  0.0 411.0 jit_solution(2312797500020581762)
XLA Ops:
  0.7 1.0 convert_element_type.40
  1.7 1.0 convert_bitcast_fusion.1
  2.7 0.1 copy.53
  2.8 1.0 copy.40
  3.8 1.1 copy.39
  4.9 0.1 pad_maximum_fusion
  5.0 0.8 copy-done.3
  5.7 0.7 dynamic-slice_bitcast_fusion
  6.4 0.5 collective-permute-start
  6.9 0.7 convert_bitcast_fusion.refs_5_
  7.6 0.6 convert_bitcast_fusion.4.refs_6_
  8.2 0.7 copy.42
  9.0 0.6 convert_bitcast_fusion.2.refs_9_
  9.6 0.4 reshape.225
  10.0 1.2 pad.18
  11.2 0.1 iota_select_fusion
  11.3 1.0 select_n.81.refs_11_.refs_1_
  12.4 0.6 fusion.5
  13.0 1.1 copy.54
  14.0 1.7 copy.46.refs_3_
  15.8 0.2 scatter.9.refs_0_
  16.0 0.6 convert_bitcast_fusion.5.refs_7_
  16.6 1.0 bitcast_select_fusion
  17.6 0.7 fusion.1.refs_1_
  18.3 0.7 fusion.2.refs_2_
  19.0 0.8 fusion.refs_3_
  19.8 0.7 pad_maximum_fusion.1.refs_4_
  20.5 0.6 reshape.227.refs_12_
  21.1 125.6 %front.1 = (bf16[4,2,32,512]{3,2,1,0:T(8,128)(2,1)}, bf16[4,2,2,144,768]{4,3,2,1,0:T(8,128)(2,1)}, bf16[4,2,2,48,768]{4,3,2,1,0:T(8,128)(2,1)}, bf16[4,2,2,192,7...) custom-call(bf16[32,128]{1,0:T(8,128)(2,1)} %copy-done.14, ...), custom_call_target="tpu_custom_call" | custom-call | tf_op jit(solution)/shard_map/front/pallas_call | solution.py:1313
  146.6 128.7 %middle.1 = (f32[2,529,512]{2,1,0:T(8,128)}, bf16[8,112,512]{2,1,0:T(8,128)(2,1)}, f32[8,512]{1,0:T(8,128)}, bf16[1536,512]{1,0:T(8,128)(2,1)}, bf16[512,512]{1,...) custom-call(bf16[896,512]{1,0:T(8,128)(2,1)} %bitcast.72, ...), custom_call_target="tpu_custom_call" | custom-call | tf_op jit(solution)/shard_map/middle/pallas_call | solution.py:797
  275.3 0.6 reshape.234.refs_2_
  275.9 115.4 %rear.1 = (f32[896,768]{1,0:T(8,128)}, bf16[512,768]{1,0:T(8,128)(2,1)}, bf16[768,3072]{1,0:T(8,128)(2,1)}, bf16[3072,768]{1,0:T(8,128)(2,1)}, bf16[768,768]{1,0...) custom-call(bf16[896,768]{1,0:T(8,128)(2,1)} %bitcast.61, ...), custom_call_target="tpu_custom_call" | custom-call | tf_op jit(solution)/shard_map/rear/pallas_call | solution.py:1650
  391.3 2.1 slice_select_fusion
  393.4 1.3 slice.99
  394.8 1.2 slice.108
  396.0 4.6 %copy.48 = f32[2,529,512]{2,0,1:T(2,128)} copy(f32[2,529,512]{2,1,0:T(8,128)} %get-tuple-element.112) | data formatting | bytes 4333568
  400.7 0.2 slice.117
  400.9 1.7 reshape.243
  402.6 0.8 copy.52
  403.4 1.2 broadcast_select_fusion.1
  404.8 0.9 copy.49
  405.7 0.7 copy.50
  406.4 0.9 copy.51
  407.3 0.6 maximum_bitcast_fusion.3
  407.9 0.7 copy.61
  408.7 0.6 copy.62
  409.3 0.6 copy.63
  409.9 0.7 copy.64
  (66 shorter events, 0.3 us)
Async XLA Ops:
  0.6 6.3 %copy-start.20 = (f32[1,96]{1,0:T(1,128)S(1)}, f32[1,96]{1,0:T(1,128)}, u32[]{:S(2)}) copy-start(f32[1,96]{1,0:T(1,128)} %param.25) | copy-start | bytes 1156
  0.7 6.3 %copy-start.19 = (f32[2,64]{1,0:T(2,128)S(1)}, f32[2,64]{1,0:T(2,128)}, u32[]{:S(2)}) copy-start(f32[2,64]{1,0:T(2,128)} %param.30) | copy-start | bytes 1540
  0.7 6.3 %copy-start.6 = (f32[768,96]{0,1:T(8,128)S(1)}, f32[768,96]{0,1:T(8,128)}, u32[]{:S(2)}) copy-start(f32[768,96]{0,1:T(8,128)} %param.29) | copy-start | bytes 884740
  0.7 6.9 %copy-start.12 = (f32[128,192]{0,1:T(8,128)S(1)}, f32[128,192]{0,1:T(8,128)}, u32[]{:S(2)}) copy-start(f32[128,192]{0,1:T(8,128)} %param.32) | copy-start | bytes 294916
  0.7 7.6 %copy-start.8 = (f32[128,256]{1,0:T(8,128)S(1)}, f32[128,256]{1,0:T(8,128)}, u32[]{:S(2)}) copy-start(f32[128,256]{1,0:T(8,128)} %param.34) | copy-start | bytes 393220
  0.7 8.3 %copy-start.9 = (f32[512,64]{0,1:T(8,128)S(1)}, f32[512,64]{0,1:T(8,128)}, u32[]{:S(2)}) copy-start(f32[512,64]{0,1:T(8,128)} %param.35) | copy-start | bytes 393220
  0.7 8.9 %copy-start.5 = (bf16[792,768]{1,0:T(8,128)(2,1)S(1)}, bf16[792,768]{1,0:T(8,128)(2,1)}, u32[]{:S(2)}) copy-start(bf16[792,768]{1,0:T(8,128)(2,1)} %param.20) | copy-start | bytes 3649540
  5.0 0.8 copy-start.3
  6.4 10.2 %collective-permute-start = (bf16[416,192]{1,0:T(8,128)(2,1)}, bf16[416,192]{1,0:T(8,128)(2,1)}, u32[]{:S(2)}, u32[]{:S(2)}) collective-permute-start(bf16[416,192]{1,0:T(8,128)(2,1)} %dynamic-slice_bitcast_fusion), channel_id=1, source_target_pairs={{0,1},{1,0},{2,3},{3,2},{4,5},{5,4},{6,7},{7,6},{8,9},{9,8},{10,11... | collective-permute-start | bytes 479240 | tf_op jit(solution)/shard_map/ppermute | solution.py:278
  9.6 1.6 copy-start.21
  9.6 2.6 copy-start.17
  10.0 2.3 copy-start.18
  10.0 4.0 copy-start.2
  14.0 2.0 copy-start.15
  14.0 2.6 copy-start.4
  16.0 5.1 %copy-start.14 = (bf16[32,128]{1,0:T(8,128)(2,1)}, bf16[32,128]{1,0:T(8,128)(2,1)S(1)}, u32[]{:S(2)}) copy-start(bf16[32,128]{1,0:T(8,128)(2,1)S(1)} %scatter.9.refs_0_) | copy-start | bytes 24580
  393.4 7.2 %copy-start.1 = (f32[896,768]{1,0:T(8,128)S(1)}, f32[896,768]{1,0:T(8,128)}, u32[]{:S(2)}) copy-start(f32[896,768]{1,0:T(8,128)} %get-tuple-element.91) | copy-start | bytes 8257540
  393.4 9.9 %collective-permute-start.1 = (f32[416,192]{1,0:T(8,128)}, f32[416,192]{1,0:T(8,128)}, u32[]{:S(2)}, u32[]{:S(2)}) collective-permute-start(f32[416,192]{1,0:T(8,128)} %slice_select_fusion), channel_id=1, source_target_pairs={{0,1},{1,0},{2,3},{3,2},{4,5},{5,4},{6,7},{7,6},{8,9},{9,8},{10,11... | collective-permute-start | bytes 958472 | tf_op jit(solution)/shard_map/ppermute | solution.py:288
  400.9 1.8 copy-start.11
  400.9 2.5 copy-start
  404.6 3.3 copy-start.7
  404.7 4.0 copy-start.13
  404.7 4.6 %copy-start.16 = (f32[64,128]{1,0:T(8,128)S(1)}, f32[64,128]{1,0:T(8,128)}, u32[]{:S(2)}) copy-start(f32[64,128]{1,0:T(8,128)} %get-tuple-element.96) | copy-start | bytes 98308
  404.7 5.2 %copy-start.10 = (f32[64,512]{1,0:T(8,128)S(1)}, f32[64,512]{1,0:T(8,128)}, u32[]{:S(2)}) copy-start(f32[64,512]{1,0:T(8,128)} %get-tuple-element.98) | copy-start | bytes 393220
